TPU v7x, 32 devices: a whole 2x2x4 slice. The times are simulated.
32 devices in a mesh: tok: 4 (over y, x), blk: 8 (over z, core).
Axes of the slice: x: 2, y: 2, z: 4, core: 2. Of those that a mesh axis runs over, the one named last changes fastest.
Arguments:
- tokens: bfloat16 [512, 8192], P('tok', 'blk'), may hold values from -6 to 6
- w_blocks: bfloat16 [3072, 128, 128], P('blk'), may hold values from -0.15625 to 0.15625
- blk_row: int32 [3072], P('blk'), may hold values from 0 to 63, as said below
- blk_col: int32 [3072], P('blk'), may hold values from 0 to 319, as said below
- blk_count: int32 [8], P('blk'), may hold values from 96 to 384, as said below
- col_owner: int32 [320], replicated, may hold values from 0 to 7, as said below
- cotangent: bfloat16 [512, 40960], P('tok', 'blk'), may hold values from -6 to 6
Outputs:
- activated: bfloat16 [512, 40960], P('tok', 'blk')
- input_grad: bfloat16 [512, 8192], P('tok', 'blk')
- block_grad: bfloat16 [3072, 128, 128], P('blk', 'tok')
Inputs may be any that keep to these rules, and one draw needn't show every extreme that they name: Slots from blk_count[o] on are unused; some owner has exactly 384 live slots. `blk_row`: the live slots of one owner name distinct blocks. `blk_col`: every slot names a block column that col_owner gives to the slot's owner. `col_owner`: each owner owns exactly 40 block columns.
All inputs are finite; a program needn't handle non-finite values.
Results may differ from a plain program's by a relative error of at most 0.018.
Values may be sent and summed in bfloat16 or wider, within the bound.
No kernel may reach another device: no remote copies, remote signals or barrier semaphores. Data moves between devices by JAX's collectives and lax.ppermute only.
A program may use at most 128 MiB of HBM per device.

v0:
```python
import functools

import jax
import jax.numpy as jnp
from jax import lax
from jax.experimental import pallas as pl
from jax.experimental.pallas import tpu as pltpu
from jax.sharding import PartitionSpec as P


GROUP = 4
LIMIT = 16 * 1024 * 1024
VMEM = pl.BlockSpec(memory_space=pltpu.VMEM)
SMEM = pl.BlockSpec(memory_space=pltpu.SMEM)
ANY = pl.BlockSpec(memory_space=pl.ANY)
HBM = pl.BlockSpec(memory_space=pltpu.HBM)


def group_ranks(key, live, n_keys):
    ids = jnp.arange(key.shape[0], dtype=jnp.int32)
    keys = jnp.arange(n_keys, dtype=jnp.int32)
    same = (key[:, None] == key[None, :]) & (ids[None, :] < ids[:, None]) & live[None, :]
    rank = jnp.sum(same.astype(jnp.int32), axis=1)
    hit = (key[:, None] == keys[None, :]) & live[:, None]
    return rank, (jnp.sum(hit.astype(jnp.int32), axis=0) + GROUP - 1) // GROUP


def group_table(key, other, live, rank, groups, pad_other):
    slots, n_keys = key.shape[0], groups.shape[0]
    ids = jnp.arange(slots, dtype=jnp.int32)
    keys = jnp.arange(n_keys, dtype=jnp.int32)
    start = jnp.sum(jnp.where(keys[None, :] < key[:, None], groups[None, :], 0), axis=1)
    total = (slots + n_keys * (GROUP - 1) + GROUP - 1) // GROUP * GROUP
    place = jnp.where(live, start * GROUP + rank, total)
    pad = slots | (pad_other << 9)
    entry = ids | (other << 9) | (key << 16)
    at = jnp.arange(total, dtype=jnp.int32)
    return pad + jnp.sum(
        jnp.where(place[None, :] == at[:, None], (entry - pad)[None, :], 0), axis=1
    )


def each(lo, hi, body, unroll):
    n = hi - lo
    main = n // unroll

    def many(i, carry):
        for u in range(unroll):
            body(lo + i * unroll + u)
        return carry

    def one(i, carry):
        body(i)
        return carry

    lax.fori_loop(0, main, many, 0)
    lax.fori_loop(lo + main * unroll, hi, one, 0)


def unpack(tab, g):
    entries = [tab[g * GROUP + i] for i in range(GROUP)]
    return (
        [e & 511 for e in entries],
        [lax.shift_right_logical(e, 9) & 127 for e in entries],
        lax.shift_right_logical(entries[0], 16),
    )


def lanes(ref, at, i, block):
    return ref[at, :, pl.ds(pl.multiple_of(i * block, block), block)]


def forward_kernel(shards, cuts, tab, meta, *refs):
    x_in = refs[:shards]
    w_ref, cot_ref, act_ref = refs[shards : shards + 3]
    h_refs = refs[shards + 3 : -3]
    x_ref, acc, sem = refs[-3:]
    slots, block, _ = w_ref.shape
    per = x_ref.shape[2] // block
    cols = acc.shape[0]
    copies = []
    for i, ref in enumerate(x_in):
        n = ref.shape[0]
        copies.append(pltpu.make_async_copy(ref, x_ref.at[pl.ds(meta[4 + i], n)], sem.at[i]))
    for copy in copies:
        copy.start()
    acc[...] = jnp.zeros_like(acc)
    x_ref[x_ref.shape[0] - 1, :, 0:block] = jnp.zeros((x_ref.shape[1], block), x_ref.dtype)
    for copy in copies:
        copy.wait()

    def group(g):
        ids, rows, col = unpack(tab, g)
        x = jnp.concatenate([lanes(x_ref, r // per, r % per, block) for r in rows], axis=1)
        w = jnp.concatenate([w_ref[jnp.minimum(s, slots - 1)] for s in ids], axis=0)
        acc[col] += jnp.dot(x, w, preferred_element_type=jnp.float32)

    each(0, meta[0], group, 4)
    for c in range(cols):
        at = slice(c * block, (c + 1) * block)
        hidden = acc[c]
        gate = jax.nn.sigmoid(hidden)
        act_ref[:, at] = (hidden * gate).astype(act_ref.dtype)
        slope = gate * (1.0 + hidden * (1.0 - gate))
        grad = (cot_ref[:, at].astype(jnp.float32) * slope).astype(act_ref.dtype)
        k = max(i for i in range(len(cuts)) if cuts[i] <= c)
        h_refs[k][:, (c - cuts[k]) * block : (c - cuts[k] + 1) * block] = grad


def term_kernel(chunks, ordered, tab, meta, *refs):
    h_in = refs[:chunks]
    w_ref = refs[chunks]
    outs = refs[chunks + 1 : -2]
    h_ref, acc = refs[-2:]
    slots, block, _ = w_ref.shape
    acc[...] = jnp.zeros_like(acc)
    at = 0
    for ref in h_in:
        h_ref[:, at : at + ref.shape[1]] = ref[...]
        at += ref.shape[1]
    h_ref[:, at : at + block] = jnp.zeros((h_ref.shape[0], block), h_ref.dtype)

    def group(g):
        ids, cols, row = unpack(tab, g)
        h = jnp.concatenate(
            [h_ref[:, pl.ds(pl.multiple_of(c * block, block), block)] for c in cols], axis=1
        )
        w = jnp.concatenate([w_ref[jnp.minimum(s, slots - 1)] for s in ids], axis=1)
        acc[row] += lax.dot_general(
            h, w, (((1,), (1,)), ((), ())), preferred_element_type=jnp.float32
        )

    each(0, meta[1], group, 4)
    role = 0
    for ref in outs:
        for i in range(ref.shape[0]):
            panel = meta[4 + role] if ordered else role
            per = ref.shape[2] // block
            for j in range(per):
                ref[i, :, j * block : (j + 1) * block] = acc[panel * per + j].astype(ref.dtype)
            role += 1


def grad_kernel(second, shards, base_col, per, tab, meta, *refs):
    x_in = refs[:shards]
    h_in = refs[shards : -3]
    out_ref, x_ref, sem = refs[-3:]
    if second:
        h_in, old_ref = h_in[:-1], h_in[-1]
    block = out_ref.shape[2]
    part = out_ref.shape[1]
    copies = []
    for i, ref in enumerate(x_in):
        n = ref.shape[0]
        copies.append(pltpu.make_async_copy(ref, x_ref.at[pl.ds(meta[4 + i] * per, n)], sem.at[i]))
    for copy in copies:
        copy.start()
    if second:
        out_ref[...] = old_ref[...]
    else:
        out_ref[...] = jnp.zeros_like(out_ref)
    for copy in copies:
        copy.wait()

    def group(g):
        ids, rows, col = unpack(tab, g)
        first = ids[0]
        live = [s < out_ref.shape[0] for s in ids]
        ids = [jnp.where(l, s, first) for l, s in zip(live, ids)]
        rows = [jnp.where(l, r, rows[0]) for l, r in zip(live, rows)]
        x = jnp.concatenate([x_ref[r] for r in rows], axis=0)
        h = []
        for ref in h_in:
            at = pl.ds(pl.multiple_of((col - base_col) * block, block), block)
            if len(ref.shape) == 2:
                h.append(ref[:, at])
            else:
                h += [ref[i, :, at] for i in range(ref.shape[0])]
        h = jnp.concatenate(h, axis=0)
        out = jnp.dot(x, h, preferred_element_type=jnp.float32).astype(out_ref.dtype)
        for i, s in enumerate(ids):
            out_ref[s] = out[i * part : (i + 1) * part]

    lo, hi = (meta[2], meta[0]) if second else (0, meta[2])
    each(lo, hi, group, 4)


def quarter_kernel(me, tok_ref, *refs):
    outs, scratch = refs[:-1], refs[-1]
    block = scratch.shape[1]
    part = outs[0].shape[1]
    for r in range(scratch.shape[0]):
        scratch[r] = tok_ref[:, r * block : (r + 1) * block].T
    for j, ref in enumerate(outs):
        at = pl.multiple_of((me[0] ^ j) * part, part)
        ref[...] = scratch[:, pl.ds(at, part), :]


def along_z(pairs):
    return [(a * 2 + c, b * 2 + c) for a, b in pairs for c in range(2)]


EVEN = along_z([(0, 1), (1, 0), (2, 3), (3, 2)])
ODD = along_z([(1, 2), (2, 1)])
OUTWARD = along_z([(1, 0), (2, 3)])
INWARD = along_z([(0, 1), (3, 2)])
CORES = [(b, b ^ 1) for b in range(8)]
TOK_X = [(t, t ^ 1) for t in range(4)]
TOK_Y = [(t, t ^ 2) for t in range(4)]
TOK_XY = [(t, t ^ 3) for t in range(4)]


def blk(x, pairs):
    return lax.ppermute(x, "blk", pairs)


def tok(x, pairs):
    return lax.ppermute(x, "tok", pairs)


def gather_line(x, middle):
    e1, o1 = blk(x, EVEN), blk(x, ODD)
    p0 = blk(x, CORES)
    o2, e2 = blk(e1, ODD), blk(o1, OUTWARD)
    p1 = blk(e1, CORES)
    e3 = blk(o2, OUTWARD)
    n2 = jnp.where(middle, o1, e2)
    p2 = blk(n2, CORES)
    n3 = jnp.where(middle, o2, e3)
    p3 = blk(n3, CORES)
    return [x, e1, n2, n3, p0, p1, p2, p3]


def on_device(n_tok, n_blk, tokens, w_blocks, blk_row, blk_col, blk_count, col_owner, cotangent):
    fast = (n_tok, n_blk) == (4, 8)
    rows_tok, width = tokens.shape
    slots, block, _ = w_blocks.shape
    cols = cotangent.shape[1] // block
    per = width // block
    n_rows = per * n_blk
    part = block // n_tok
    me_blk = lax.axis_index("blk")
    me_tok = lax.axis_index("tok")
    z, core = me_blk // 2, me_blk % 2
    middle = (z == 1) | (z == 2)
    bf16 = tokens.dtype
    params = pltpu.CompilerParams(vmem_limit_bytes=LIMIT)

    if fast:
        far = [z, z ^ 1, jnp.where(z < 2, 2, 1), jnp.where(z < 2, 3, 0)]
        panels = [f * 2 + core for f in far] + [f * 2 + 1 - core for f in far]
        shards = gather_line(tokens, middle)
        shards = [s[None] for s in shards]
    else:
        panels = [jnp.int32(0)]
        shards = [lax.all_gather(tokens, "blk", axis=0)]

    mine = (col_owner == me_blk)[None, :]
    all_cols = jnp.arange(col_owner.shape[0], dtype=jnp.int32)[None, :]
    local = jnp.sum((mine & (all_cols < blk_col[:, None])).astype(jnp.int32), axis=1)
    live = jnp.arange(slots, dtype=jnp.int32) < blk_count[0]
    col_rank, col_groups = group_ranks(local, live, cols)
    row_rank, row_groups = group_ranks(blk_row, live, n_rows)
    cuts = (0, cols // 2)
    sizes = (cols // 2, cols - cols // 2)
    col_tab = group_table(local, blk_row, live, col_rank, col_groups, n_rows)
    row_tab = group_table(blk_row, local, live, row_rank, row_groups, cols)
    values = [jnp.sum(col_groups), jnp.sum(row_groups), jnp.sum(col_groups[: cuts[1]]), me_tok]
    meta = jnp.stack([jnp.asarray(v, jnp.int32) for v in values + panels])

    xq = pl.pallas_call(
        quarter_kernel,
        out_shape=[jax.ShapeDtypeStruct((per, part, rows_tok), bf16)] * n_tok,
        in_specs=[SMEM, VMEM],
        out_specs=[VMEM] * n_tok,
        scratch_shapes=[pltpu.VMEM((per, block, rows_tok), bf16)],
        compiler_params=params,
        name="quarter",
    )(me_tok.astype(jnp.int32)[None], tokens)
    if fast:
        xq = [xq[0], tok(xq[1], TOK_X), tok(xq[2], TOK_Y), tok(xq[3], TOK_XY)]
        xq = jnp.concatenate(xq, axis=2)
        xq_shards = gather_line(xq, middle)
    else:
        order = me_tok ^ jnp.arange(n_tok)
        xq = jnp.take(jnp.stack(xq), order, axis=0)
        xq = lax.all_to_all(xq, "tok", split_axis=0, concat_axis=0, tiled=True)
        xq = xq.transpose(1, 2, 0, 3).reshape(per, part, n_tok * rows_tok)
        xq_shards = [lax.all_gather(xq, "blk", axis=0, tiled=True)]

    act, *hs = pl.pallas_call(
        functools.partial(forward_kernel, len(shards), cuts),
        out_shape=[jax.ShapeDtypeStruct(cotangent.shape, bf16)]
        + [jax.ShapeDtypeStruct((rows_tok, n * block), bf16) for n in sizes],
        in_specs=[SMEM, SMEM] + [ANY] * len(shards) + [VMEM, VMEM],
        out_specs=[VMEM] * (1 + len(sizes)),
        scratch_shapes=[
            pltpu.VMEM((n_blk + 1, rows_tok, width), bf16),
            pltpu.VMEM((cols, rows_tok, block), jnp.float32),
            pltpu.SemaphoreType.DMA((len(shards),)),
        ],
        compiler_params=params,
        name="forward",
    )(col_tab, meta, *shards, w_blocks, cotangent)

    if fast:
        (a, b) = hs
        ax, ay = tok(a, TOK_X), tok(a, TOK_Y)
        bx, by = tok(b, TOK_X), tok(b, TOK_Y)
        ad, bd = tok(ax, TOK_Y), tok(by, TOK_X)
        gathered = [[a, ax, ay, ad], [b, bx, by, bd]]
    else:
        gathered = [[lax.all_gather(h, "tok", axis=0)] for h in hs]

    if fast:
        outs = [4, 4]
    else:
        outs = [n_blk]
    terms = pl.pallas_call(
        functools.partial(term_kernel, len(hs), fast),
        out_shape=[jax.ShapeDtypeStruct((n, rows_tok, width), bf16) for n in outs],
        in_specs=[SMEM, SMEM] + [VMEM] * (len(hs) + 1),
        out_specs=[VMEM] * len(outs),
        scratch_shapes=[
            pltpu.VMEM((rows_tok, (cols + 1) * block), bf16),
            pltpu.VMEM((n_rows, rows_tok, block), jnp.float32),
        ],
        compiler_params=params,
        name="term",
    )(row_tab, meta, *hs, w_blocks)

    def add(*xs):
        return sum(x.astype(jnp.float32) for x in xs).astype(bf16)

    if fast:
        keep, send = terms
        q = add(keep, blk(send, CORES))
        own, near, mid, last = (q[i] for i in range(4))
        a1 = blk(last, INWARD)
        b1 = blk(mid, INWARD)
        a2 = blk(add(last, a1), ODD)
        e3 = blk(add(near, a2), EVEN)
        o3 = blk(add(mid, b1), ODD)
        input_grad = add(own, e3, o3)
    else:
        input_grad = lax.psum_scatter(terms[0], "blk", scatter_dimension=0, tiled=True)[0]

    grad = None
    for k, hk in enumerate(gathered):
        extra = [] if grad is None else [grad]
        grad = pl.pallas_call(
            functools.partial(grad_kernel, k > 0, len(xq_shards), cuts[k], per),
            out_shape=jax.ShapeDtypeStruct((slots, part, block), bf16),
            in_specs=[SMEM, SMEM] + [ANY] * len(xq_shards) + [VMEM] * (len(hk) + len(extra)),
            out_specs=VMEM,
            scratch_shapes=[
                pltpu.VMEM((n_rows, part, n_tok * rows_tok), bf16),
                pltpu.SemaphoreType.DMA((len(xq_shards),)),
            ],
            compiler_params=params,
            name="weight_grad",
        )(col_tab, meta, *xq_shards, *hk, *extra)
    return act, input_grad, grad


def solution(mesh):
    n_tok, n_blk = mesh.shape["tok"], mesh.shape["blk"]

    def body(*args):
        return on_device(n_tok, n_blk, *args)

    return jax.shard_map(
        body,
        mesh=mesh,
        in_specs=(
            P("tok", "blk"),
            P("blk", None, None),
            P("blk"),
            P("blk"),
            P("blk"),
            P(),
            P("tok", "blk"),
        ),
        out_specs=(P("tok", "blk"), P("tok", "blk"), P("blk", "tok", None)),
        check_vma=False,
    )
```

profile of v0, /device:TPU:0, one launch (start us, length us, event | category | flops | bytes accessed | tf_op | source)
XLA Modules:
  0.0 139.3 jit_solution(17911324028164099237)
XLA Ops:
  0.6 3.1 %collective-permute-start = (bf16[128,1024]{1,0:T(8,128)(2,1)}, bf16[128,1024]{1,0:T(8,128)(2,1)S(1)}, u32[]{:S(2)}, u32[]{:S(2)}) collective-permute-start(bf16[128,1024]{1,0:T(8,128)(2,1)} %tok_ref.1), channel_id=1, source_target_pairs={{0,2},{1,3},{2,0},{3,1},{4,6},{5,7},{6,4},{7,5},{8,10},{9,11},{10,... | collective-permute-start | bytes 786440 | tf_op jit(solution)/shard_map/ppermute | solution.py:214
  3.8 0.7 collective-permute-start.1
  5.2 0.7 broadcast_compare_fusion
  5.9 0.8 convert_reduce_fusion.2
  6.7 0.8 convert_reduce_fusion.3
  7.5 1.1 convert_reduce_fusion
  8.6 0.1 convert_reduce_fusion.4
  8.7 0.6 fusion.10
  9.3 0.8 select_reduce_fusion.2
  10.1 0.6 fusion.11
  10.7 0.1 select_reduce_fusion.3
  10.8 0.7 or_add_fusion
  11.5 0.7 collective-permute-start.3
  12.2 0.2 select_reduce_fusion.1
  12.4 1.3 collective-permute-start.2
  13.7 1.3 collective-permute-start.4
  15.0 0.2 select_reduce_fusion
  15.2 0.6 collective-permute-start.6
  15.8 10.5 %collective-permute-done.2 = bf16[128,1024]{1,0:T(8,128)(2,1)S(1)} collective-permute-done((bf16[128,1024]{1,0:T(8,128)(2,1)S(1)}, bf16[128,1024]{1,0:T(8,128)(2,1)S(1)}, u32[]{:S(2)}, u32[]{:S(2)}) %collective-permute-start.2) | collective-permute-done | bytes 262176 | tf_op jit(solution)/shard_map/ppermute | solution.py:214
  26.4 7.5 %collective-permute-done.4 = bf16[128,1024]{1,0:T(8,128)(2,1)S(1)} collective-permute-done((bf16[128,1024]{1,0:T(8,128)(2,1)S(1)}, bf16[128,1024]{1,0:T(8,128)(2,1)S(1)}, u32[]{:S(2)}, u32[]{:S(2)}) %collective-permute-start.4) | collective-permute-done | bytes 262176 | tf_op jit(solution)/shard_map/ppermute | solution.py:214
  34.0 0.6 slice_reduce_fusion
  34.6 2.0 %stack.51.meta = s32[12]{0:T(128)S(1)} concatenate(s32[1]{0:T(128)} %bitcast.1, s32[1]{0:T(128)} %bitcast.2, s32[1]{0:T(128)} %bitcast.3, s32[1]{0:T(128)} %bitcast.4.me, s32[1]{0:T(128)} %bitcast.5, s32[1]{0:T(128)} %bitcast.6, s32[1]{0:T(128)} %bitcast.7, s32[1]{0:T(128)} %bitcast.8, s32[1]{0:T(128)} %bitcast.9, s32[1]{0:T(128)} %bitcast.10, s32[1]{0:T(128)} %bitcast.11, s32[1]{0:T(128)} %bitcast.12), dimensions={0} | concatenate | bytes 96 | tf_op jit(solution)/shard_map/stack | solution.py:269
  36.7 4.6 %copy-done = bf16[384,128,128]{2,1,0:T(8,128)(2,1)S(1)} copy-done((bf16[384,128,128]{2,1,0:T(8,128)(2,1)S(1)}, bf16[384,128,128]{2,1,0:T(8,128)(2,1)}, u32[]{:S(2)}) %copy-start) | copy-done | bytes 12582936
  41.3 0.9 copy-done.3
  42.3 7.6 %forward.1 = (bf16[128,5120]{1,0:T(8,128)(2,1)}, bf16[128,2560]{1,0:T(8,128)(2,1)S(1)}, bf16[128,2560]{1,0:T(8,128)(2,1)S(1)}) custom-call(s32[504]{0:T(512)S(1)} %broadcast_add_fusion.1.tab, s32[12]{0:T(128)S(1)} %stack.51.meta, bf16[1,128,1024]{2,1,0:T(8,128)(2,1)S(1)} %bitcast.41, bf16[1,128,1024]{2,1,0:T(8,128)(2,1)S(1)} %bitcast.44, ...), custom_call_target="tpu_custom_call" | custom-call | tf_op jit(solution)/shard_map/forward/pallas_call | solution.py:291
  49.9 7.0 %term.1 = (bf16[4,128,1024]{2,1,0:T(8,128)(2,1)S(1)}, bf16[4,128,1024]{2,1,0:T(8,128)(2,1)S(1)}) custom-call(s32[576]{0:T(1024)S(1)} %broadcast_add_fusion.tab, s32[12]{0:T(128)S(1)} %stack.51.meta, bf16[128,2560]{1,0:T(8,128)(2,1)S(1)} %get-tuple-element.13.refs_0_.refs_8_, bf16[128,2560]{1,0:T(8,128)(2,1)S(1)} %get-tuple-element.14.refs_1_.refs_8_, ...), custom_call_target="tpu_custom_call" | custom-call | tf_op jit(solution)/shard_map/term/pallas_call | solution.py:319
  56.9 8.2 %collective-permute-start.9 = (bf16[4,128,1024]{2,1,0:T(8,128)(2,1)S(1)}, bf16[4,128,1024]{2,1,0:T(8,128)(2,1)S(1)}, u32[]{:S(2)}, u32[]{:S(2)}) collective-permute-start(bf16[4,128,1024]{2,1,0:T(8,128)(2,1)S(1)} %get-tuple-element.16), channel_id=1, source_target_pairs={{0,1},{1,0},{2,3},{3,2},{4,5},{5,4},{6,7},{7,6},{8,9},{9,8},{10,11... | collective-permute-start | bytes 3145736 | tf_op jit(solution)/shard_map/ppermute | solution.py:214
  65.1 0.1 quarter.1
  65.2 1.5 %collective-permute-start.15 = (bf16[8,32,128]{2,1,0:T(8,128)(2,1)S(1)}, bf16[8,32,128]{2,1,0:T(8,128)(2,1)S(1)}, u32[]{:S(2)}, u32[]{:S(2)}) collective-permute-start(bf16[8,32,128]{2,1,0:T(8,128)(2,1)S(1)} %get-tuple-element.18), channel_id=1, source_target_pairs={{0,8},{8,0},{16,24},{24,16},{1,9},{9,1},{17,25},{25,17},{2,10},{10... | collective-permute-start | bytes 196616 | tf_op jit(solution)/shard_map/ppermute | solution.py:218
  66.8 1.5 %collective-permute-start.16 = (bf16[8,32,128]{2,1,0:T(8,128)(2,1)S(1)}, bf16[8,32,128]{2,1,0:T(8,128)(2,1)S(1)}, u32[]{:S(2)}, u32[]{:S(2)}) collective-permute-start(bf16[8,32,128]{2,1,0:T(8,128)(2,1)S(1)} %get-tuple-element.19), channel_id=1, source_target_pairs={{0,16},{8,24},{16,0},{24,8},{1,17},{9,25},{17,1},{25,9},{2,18},{10... | collective-permute-start | bytes 196616 | tf_op jit(solution)/shard_map/ppermute | solution.py:218
  68.3 0.5 collective-permute-start.17
  68.8 0.8 collective-permute-done.15
  69.6 1.5 %collective-permute-done.16 = bf16[8,32,128]{2,1,0:T(8,128)(2,1)S(1)} collective-permute-done((bf16[8,32,128]{2,1,0:T(8,128)(2,1)S(1)}, bf16[8,32,128]{2,1,0:T(8,128)(2,1)S(1)}, u32[]{:S(2)}, u32[]{:S(2)}) %collective-permute-start.16) | collective-permute-done | bytes 65568 | tf_op jit(solution)/shard_map/ppermute | solution.py:218
  71.1 2.4 %collective-permute-done.17 = bf16[8,32,128]{2,1,0:T(8,128)(2,1)S(1)} collective-permute-done((bf16[8,32,128]{2,1,0:T(8,128)(2,1)S(1)}, bf16[8,32,128]{2,1,0:T(8,128)(2,1)S(1)}, u32[]{:S(2)}, u32[]{:S(2)}) %collective-permute-start.17) | collective-permute-done | bytes 65568 | tf_op jit(solution)/shard_map/ppermute | solution.py:218
  73.5 0.4 collective-permute-start.18
  73.8 0.7 collective-permute-start.19
  74.6 5.5 %collective-permute-done.18.refs_1_ = bf16[8,32,512]{2,1,0:T(8,128)(2,1)S(1)} collective-permute-done((bf16[8,32,512]{2,1,0:T(8,128)(2,1)S(1)}, bf16[8,32,512]{2,1,0:T(8,128)(2,1)S(1)}, u32[]{:S(2)}, u32[]{:S(2)}) %collective-permute-start.18) | collective-permute-done | bytes 262176 | tf_op jit(solution)/shard_map/ppermute | solution.py:214
  80.1 0.7 collective-permute-start.21
  80.8 1.3 collective-permute-start.20
  82.1 0.6 collective-permute-start.28
  82.8 0.4 add_convert_fusion
  83.2 0.9 collective-permute-start.30
  84.1 1.3 collective-permute-start.22
  85.4 6.8 %collective-permute-done.20 = bf16[8,32,512]{2,1,0:T(8,128)(2,1)S(1)} collective-permute-done((bf16[8,32,512]{2,1,0:T(8,128)(2,1)S(1)}, bf16[8,32,512]{2,1,0:T(8,128)(2,1)S(1)}, u32[]{:S(2)}, u32[]{:S(2)}) %collective-permute-start.20) | collective-permute-done | bytes 262176 | tf_op jit(solution)/shard_map/ppermute | solution.py:214
  92.3 1.5 %collective-permute-start.10 = (bf16[128,1024]{1,0:T(8,128)(2,1)S(1)}, bf16[128,1024]{1,0:T(8,128)(2,1)S(1)}, u32[]{:S(2)}, u32[]{:S(2)}) collective-permute-start(bf16[128,1024]{1,0:T(8,128)(2,1)S(1)} %get-tuple-element.29), channel_id=1, source_target_pairs={{0,2},{1,3},{6,4},{7,5},{8,10},{9,11},{14,12},{15,13},{16,18},{17,... | collective-permute-start | bytes 786440 | tf_op jit(solution)/shard_map/ppermute | solution.py:214
  93.8 3.7 %collective-permute-done.22 = bf16[8,32,512]{2,1,0:T(8,128)(2,1)S(1)} collective-permute-done((bf16[8,32,512]{2,1,0:T(8,128)(2,1)S(1)}, bf16[8,32,512]{2,1,0:T(8,128)(2,1)S(1)}, u32[]{:S(2)}, u32[]{:S(2)}) %collective-permute-start.22) | collective-permute-done | bytes 262176 | tf_op jit(solution)/shard_map/ppermute | solution.py:214
  97.5 0.6 collective-permute-start.31
  98.1 0.9 collective-permute-done.10
  99.0 4.4 %collective-permute-start.13 = (bf16[128,1024]{1,0:T(8,128)(2,1)S(1)}, bf16[128,1024]{1,0:T(8,128)(2,1)S(1)}, u32[]{:S(2)}, u32[]{:S(2)}) collective-permute-start(bf16[128,1024]{1,0:T(8,128)(2,1)S(1)} %get-tuple-element.30), channel_id=1, source_target_pairs={{0,2},{1,3},{6,4},{7,5},{8,10},{9,11},{14,12},{15,13},{16,18},{17,... | collective-permute-start | bytes 786440 | tf_op jit(solution)/shard_map/ppermute | solution.py:214
  103.4 0.7 collective-permute-start.11
  104.1 0.9 collective-permute-start.27
  105.0 1.2 collective-permute-start.29
  106.2 1.5 %collective-permute-done.13 = bf16[128,1024]{1,0:T(8,128)(2,1)S(1)} collective-permute-done((bf16[128,1024]{1,0:T(8,128)(2,1)S(1)}, bf16[128,1024]{1,0:T(8,128)(2,1)S(1)}, u32[]{:S(2)}, u32[]{:S(2)}) %collective-permute-start.13) | collective-permute-done | bytes 262176 | tf_op jit(solution)/shard_map/ppermute | solution.py:214
  107.7 0.7 collective-permute-start.32
  108.6 0.2 fusion.4
  108.8 1.3 collective-permute-done.26.refs_7_
  110.1 0.7 collective-permute-start.14
  110.8 4.3 %collective-permute-done.31.refs_10_ = bf16[128,2560]{1,0:T(8,128)(2,1)S(1)} collective-permute-done((bf16[128,2560]{1,0:T(8,128)(2,1)S(1)}, bf16[128,2560]{1,0:T(8,128)(2,1)S(1)}, u32[]{:S(2)}, u32[]{:S(2)}) %collective-permute-start.31) | collective-permute-done | bytes 655392 | tf_op jit(solution)/shard_map/ppermute | solution.py:218
  115.1 1.7 %collective-permute-start.12 = (bf16[128,1024]{1,0:T(8,128)(2,1)S(1)}, bf16[128,1024]{1,0:T(8,128)(2,1)S(1)}, u32[]{:S(2)}, u32[]{:S(2)}) collective-permute-start(bf16[128,1024]{1,0:T(8,128)(2,1)S(1)} %get-tuple-element.27), channel_id=1, source_target_pairs={{0,2},{1,3},{2,0},{3,1},{4,6},{5,7},{6,4},{7,5},{8,10},{9,11},{10,... | collective-permute-start | bytes 786440 | tf_op jit(solution)/shard_map/ppermute | solution.py:214
  116.9 11.1 %collective-permute-done.32.refs_11_ = bf16[128,2560]{1,0:T(8,128)(2,1)S(1)} collective-permute-done((bf16[128,2560]{1,0:T(8,128)(2,1)S(1)}, bf16[128,2560]{1,0:T(8,128)(2,1)S(1)}, u32[]{:S(2)}, u32[]{:S(2)}) %collective-permute-start.32) | collective-permute-done | bytes 655392 | tf_op jit(solution)/shard_map/ppermute | solution.py:218
  127.9 3.4 %weight_grad.2.refs_12_ = bf16[384,32,128]{2,1,0:T(8,128)(2,1)S(1)} custom-call(s32[504]{0:T(512)S(1)} %broadcast_add_fusion.1.tab, s32[12]{0:T(128)S(1)} %stack.51.meta, bf16[8,32,512]{2,1,0:T(8,128)(2,1)S(1)} %constant_dynamic-update-slice_fusion.refs_0_, bf16[8,32,512]{2,1,0:T(8,128)(2,1)S(1)} %collective-permute-done.18.refs_1_, ...), custom_call_target="tpu_custom_call" | custom-call | tf_op jit(solution)/shard_map/weight_grad/pallas_call | solution.py:351
  131.4 1.9 %collective-permute-done.29.refs_11_ = bf16[128,2560]{1,0:T(8,128)(2,1)S(1)} collective-permute-done((bf16[128,2560]{1,0:T(8,128)(2,1)S(1)}, bf16[128,2560]{1,0:T(8,128)(2,1)S(1)}, u32[]{:S(2)}, u32[]{:S(2)}) %collective-permute-start.29) | collective-permute-done | bytes 655392 | tf_op jit(solution)/shard_map/ppermute | solution.py:218
  133.3 5.1 %weight_grad.3 = bf16[384,32,128]{2,1,0:T(8,128)(2,1)} custom-call(s32[504]{0:T(512)S(1)} %broadcast_add_fusion.1.tab, s32[12]{0:T(128)S(1)} %stack.51.meta, bf16[8,32,512]{2,1,0:T(8,128)(2,1)S(1)} %constant_dynamic-update-slice_fusion.refs_0_, bf16[8,32,512]{2,1,0:T(8,128)(2,1)S(1)} %collective-permute-done.18.refs_1_, ...), custom_call_target="tpu_custom_call" | custom-call | tf_op jit(solution)/shard_map/weight_grad/pallas_call | solution.py:351
  138.4 0.8 fusion.6
  (48 shorter events, 0.9 us)
Async XLA Ops:
  0.6 36.1 %copy-start.2 = (bf16[128,5120]{1,0:T(8,128)(2,1)S(1)}, bf16[128,5120]{1,0:T(8,128)(2,1)}, u32[]{:S(2)}) copy-start(bf16[128,5120]{1,0:T(8,128)(2,1)} %refs_9_.1) | copy-start | bytes 3932164
  0.6 10.9 %collective-permute-start = (bf16[128,1024]{1,0:T(8,128)(2,1)}, bf16[128,1024]{1,0:T(8,128)(2,1)S(1)}, u32[]{:S(2)}, u32[]{:S(2)}) collective-permute-start(bf16[128,1024]{1,0:T(8,128)(2,1)} %tok_ref.1), channel_id=1, source_target_pairs={{0,2},{1,3},{2,0},{3,1},{4,6},{5,7},{6,4},{7,5},{8,10},{9,11},{10,... | collective-permute-start | bytes 786440 | tf_op jit(solution)/shard_map/ppermute | solution.py:214
  3.8 8.6 %collective-permute-start.1 = (bf16[128,1024]{1,0:T(8,128)(2,1)}, bf16[128,1024]{1,0:T(8,128)(2,1)S(1)}, u32[]{:S(2)}, u32[]{:S(2)}) collective-permute-start(bf16[128,1024]{1,0:T(8,128)(2,1)} %tok_ref.1), channel_id=1, source_target_pairs={{2,4},{3,5},{4,2},{5,3},{10,12},{11,13},{12,10},{13,11},{18,20},{1... | collective-permute-start | bytes 786440 | tf_op jit(solution)/shard_map/ppermute | solution.py:214
  4.4 32.2 %collective-permute-start.5 = (bf16[128,1024]{1,0:T(8,128)(2,1)}, bf16[128,1024]{1,0:T(8,128)(2,1)S(1)}, u32[]{:S(2)}, u32[]{:S(2)}) collective-permute-start(bf16[128,1024]{1,0:T(8,128)(2,1)} %tok_ref.1), channel_id=1, source_target_pairs={{0,1},{1,0},{2,3},{3,2},{4,5},{5,4},{6,7},{7,6},{8,9},{9,8},{10,11... | collective-permute-start | bytes 786440 | tf_op jit(solution)/shard_map/ppermute | solution.py:214
  11.5 2.2 %collective-permute-start.3 = (bf16[128,1024]{1,0:T(8,128)(2,1)S(1)}, bf16[128,1024]{1,0:T(8,128)(2,1)S(1)}, u32[]{:S(2)}, u32[]{:S(2)}) collective-permute-start(bf16[128,1024]{1,0:T(8,128)(2,1)S(1)} %collective-permute-done), channel_id=1, source_target_pairs={{2,4},{3,5},{4,2},{5,3},{10,12},{11,13},{12,10},{13,11},{18,20},{1... | collective-permute-start | bytes 786440 | tf_op jit(solution)/shard_map/ppermute | solution.py:214
  12.4 13.9 %collective-permute-start.2 = (bf16[128,1024]{1,0:T(8,128)(2,1)S(1)}, bf16[128,1024]{1,0:T(8,128)(2,1)S(1)}, u32[]{:S(2)}, u32[]{:S(2)}) collective-permute-start(bf16[128,1024]{1,0:T(8,128)(2,1)S(1)} %collective-permute-done.1), channel_id=1, source_target_pairs={{2,0},{3,1},{4,6},{5,7},{10,8},{11,9},{12,14},{13,15},{18,16},{19,... | collective-permute-start | bytes 786440 | tf_op jit(solution)/shard_map/ppermute | solution.py:214
  13.7 20.2 %collective-permute-start.4 = (bf16[128,1024]{1,0:T(8,128)(2,1)S(1)}, bf16[128,1024]{1,0:T(8,128)(2,1)S(1)}, u32[]{:S(2)}, u32[]{:S(2)}) collective-permute-start(bf16[128,1024]{1,0:T(8,128)(2,1)S(1)} %collective-permute-done.3), channel_id=1, source_target_pairs={{2,0},{3,1},{4,6},{5,7},{10,8},{11,9},{12,14},{13,15},{18,16},{19,... | collective-permute-start | bytes 786440 | tf_op jit(solution)/shard_map/ppermute | solution.py:214
  15.2 21.5 %collective-permute-start.6 = (bf16[128,1024]{1,0:T(8,128)(2,1)S(1)}, bf16[128,1024]{1,0:T(8,128)(2,1)S(1)}, u32[]{:S(2)}, u32[]{:S(2)}) collective-permute-start(bf16[128,1024]{1,0:T(8,128)(2,1)S(1)} %collective-permute-done), channel_id=1, source_target_pairs={{0,1},{1,0},{2,3},{3,2},{4,5},{5,4},{6,7},{7,6},{8,9},{9,8},{10,11... | collective-permute-start | bytes 786440 | tf_op jit(solution)/shard_map/ppermute | solution.py:214
  26.3 10.4 %collective-permute-start.7 = (bf16[128,1024]{1,0:T(8,128)(2,1)S(1)}, bf16[128,1024]{1,0:T(8,128)(2,1)S(1)}, u32[]{:S(2)}, u32[]{:S(2)}) collective-permute-start(bf16[128,1024]{1,0:T(8,128)(2,1)S(1)} %broadcast_select_fusion.3), channel_id=1, source_target_pairs={{0,1},{1,0},{2,3},{3,2},{4,5},{5,4},{6,7},{7,6},{8,9},{9,8},{10,11... | collective-permute-start | bytes 786440 | tf_op jit(solution)/shard_map/ppermute | solution.py:214
  33.9 2.8 %collective-permute-start.8 = (bf16[128,1024]{1,0:T(8,128)(2,1)S(1)}, bf16[128,1024]{1,0:T(8,128)(2,1)S(1)}, u32[]{:S(2)}, u32[]{:S(2)}) collective-permute-start(bf16[128,1024]{1,0:T(8,128)(2,1)S(1)} %broadcast_select_fusion.2), channel_id=1, source_target_pairs={{0,1},{1,0},{2,3},{3,2},{4,5},{5,4},{6,7},{7,6},{8,9},{9,8},{10,11... | collective-permute-start | bytes 786440 | tf_op jit(solution)/shard_map/ppermute | solution.py:214
  36.7 4.6 %copy-start = (bf16[384,128,128]{2,1,0:T(8,128)(2,1)S(1)}, bf16[384,128,128]{2,1,0:T(8,128)(2,1)}, u32[]{:S(2)}) copy-start(bf16[384,128,128]{2,1,0:T(8,128)(2,1)} %refs_2_.1) | copy-start | bytes 37748740
  41.3 0.9 copy-start.3
  42.3 7.6 %copy-start.1 = (bf16[384,128,128]{2,1,0:T(8,128)(2,1)S(1)}, bf16[384,128,128]{2,1,0:T(8,128)(2,1)}, u32[]{:S(2)}) copy-start(bf16[384,128,128]{2,1,0:T(8,128)(2,1)} %refs_2_.1) | copy-start | bytes 37748740
  49.9 15.2 %copy-start.4 = (bf16[128,1024]{1,0:T(8,128)(2,1)S(1)}, bf16[128,1024]{1,0:T(8,128)(2,1)}, u32[]{:S(2)}) copy-start(bf16[128,1024]{1,0:T(8,128)(2,1)} %tok_ref.1) | copy-start | bytes 786436
  56.9 25.2 %collective-permute-start.9 = (bf16[4,128,1024]{2,1,0:T(8,128)(2,1)S(1)}, bf16[4,128,1024]{2,1,0:T(8,128)(2,1)S(1)}, u32[]{:S(2)}, u32[]{:S(2)}) collective-permute-start(bf16[4,128,1024]{2,1,0:T(8,128)(2,1)S(1)} %get-tuple-element.16), channel_id=1, source_target_pairs={{0,1},{1,0},{2,3},{3,2},{4,5},{5,4},{6,7},{7,6},{8,9},{9,8},{10,11... | collective-permute-start | bytes 3145736 | tf_op jit(solution)/shard_map/ppermute | solution.py:214
  65.2 4.3 %collective-permute-start.15 = (bf16[8,32,128]{2,1,0:T(8,128)(2,1)S(1)}, bf16[8,32,128]{2,1,0:T(8,128)(2,1)S(1)}, u32[]{:S(2)}, u32[]{:S(2)}) collective-permute-start(bf16[8,32,128]{2,1,0:T(8,128)(2,1)S(1)} %get-tuple-element.18), channel_id=1, source_target_pairs={{0,8},{8,0},{16,24},{24,16},{1,9},{9,1},{17,25},{25,17},{2,10},{10... | collective-permute-start | bytes 196616 | tf_op jit(solution)/shard_map/ppermute | solution.py:218
  66.8 4.3 %collective-permute-start.16 = (bf16[8,32,128]{2,1,0:T(8,128)(2,1)S(1)}, bf16[8,32,128]{2,1,0:T(8,128)(2,1)S(1)}, u32[]{:S(2)}, u32[]{:S(2)}) collective-permute-start(bf16[8,32,128]{2,1,0:T(8,128)(2,1)S(1)} %get-tuple-element.19), channel_id=1, source_target_pairs={{0,16},{8,24},{16,0},{24,8},{1,17},{9,25},{17,1},{25,9},{2,18},{10... | collective-permute-start | bytes 196616 | tf_op jit(solution)/shard_map/ppermute | solution.py:218
  68.3 5.2 %collective-permute-start.17 = (bf16[8,32,128]{2,1,0:T(8,128)(2,1)S(1)}, bf16[8,32,128]{2,1,0:T(8,128)(2,1)S(1)}, u32[]{:S(2)}, u32[]{:S(2)}) collective-permute-start(bf16[8,32,128]{2,1,0:T(8,128)(2,1)S(1)} %get-tuple-element.20), channel_id=1, source_target_pairs={{0,24},{8,16},{16,8},{24,0},{1,25},{9,17},{17,9},{25,1},{2,26},{10... | collective-permute-start | bytes 196616 | tf_op jit(solution)/shard_map/ppermute | solution.py:218
  73.5 6.6 %collective-permute-start.18 = (bf16[8,32,512]{2,1,0:T(8,128)(2,1)S(1)}, bf16[8,32,512]{2,1,0:T(8,128)(2,1)S(1)}, u32[]{:S(2)}, u32[]{:S(2)}) collective-permute-start(bf16[8,32,512]{2,1,0:T(8,128)(2,1)S(1)} %constant_dynamic-update-slice_fusion.refs_0_), channel_id=1, source_target_pairs={{0,2},{1,3},{2,0},{3,1},{4,6},{5,7},{6,4},{7,5},{8,10},{9,11},{10,... | collective-permute-start | bytes 786440 | tf_op jit(solution)/shard_map/ppermute | solution.py:214
  73.8 7.0 %collective-permute-start.19 = (bf16[8,32,512]{2,1,0:T(8,128)(2,1)S(1)}, bf16[8,32,512]{2,1,0:T(8,128)(2,1)S(1)}, u32[]{:S(2)}, u32[]{:S(2)}) collective-permute-start(bf16[8,32,512]{2,1,0:T(8,128)(2,1)S(1)} %constant_dynamic-update-slice_fusion.refs_0_), channel_id=1, source_target_pairs={{2,4},{3,5},{4,2},{5,3},{10,12},{11,13},{12,10},{13,11},{18,20},{1... | collective-permute-start | bytes 786440 | tf_op jit(solution)/shard_map/ppermute | solution.py:214
  74.5 8.7 %collective-permute-start.23 = (bf16[8,32,512]{2,1,0:T(8,128)(2,1)S(1)}, bf16[8,32,512]{2,1,0:T(8,128)(2,1)S(1)}, u32[]{:S(2)}, u32[]{:S(2)}) collective-permute-start(bf16[8,32,512]{2,1,0:T(8,128)(2,1)S(1)} %constant_dynamic-update-slice_fusion.refs_0_), channel_id=1, source_target_pairs={{0,1},{1,0},{2,3},{3,2},{4,5},{5,4},{6,7},{7,6},{8,9},{9,8},{10,11... | collective-permute-start | bytes 786440 | tf_op jit(solution)/shard_map/ppermute | solution.py:214
  80.1 4.0 %collective-permute-start.21 = (bf16[8,32,512]{2,1,0:T(8,128)(2,1)S(1)}, bf16[8,32,512]{2,1,0:T(8,128)(2,1)S(1)}, u32[]{:S(2)}, u32[]{:S(2)}) collective-permute-start(bf16[8,32,512]{2,1,0:T(8,128)(2,1)S(1)} %collective-permute-done.18.refs_1_), channel_id=1, source_target_pairs={{2,4},{3,5},{4,2},{5,3},{10,12},{11,13},{12,10},{13,11},{18,20},{1... | collective-permute-start | bytes 786440 | tf_op jit(solution)/shard_map/ppermute | solution.py:214
  80.7 13.0 %collective-permute-start.24 = (bf16[8,32,512]{2,1,0:T(8,128)(2,1)S(1)}, bf16[8,32,512]{2,1,0:T(8,128)(2,1)S(1)}, u32[]{:S(2)}, u32[]{:S(2)}) collective-permute-start(bf16[8,32,512]{2,1,0:T(8,128)(2,1)S(1)} %collective-permute-done.18.refs_1_), channel_id=1, source_target_pairs={{0,1},{1,0},{2,3},{3,2},{4,5},{5,4},{6,7},{7,6},{8,9},{9,8},{10,11... | collective-permute-start | bytes 786440 | tf_op jit(solution)/shard_map/ppermute | solution.py:214
  80.8 11.4 %collective-permute-start.20 = (bf16[8,32,512]{2,1,0:T(8,128)(2,1)S(1)}, bf16[8,32,512]{2,1,0:T(8,128)(2,1)S(1)}, u32[]{:S(2)}, u32[]{:S(2)}) collective-permute-start(bf16[8,32,512]{2,1,0:T(8,128)(2,1)S(1)} %collective-permute-done.19), channel_id=1, source_target_pairs={{2,0},{3,1},{4,6},{5,7},{10,8},{11,9},{12,14},{13,15},{18,16},{19,... | collective-permute-start | bytes 786440 | tf_op jit(solution)/shard_map/ppermute | solution.py:214
  82.1 22.0 %collective-permute-start.28 = (bf16[128,2560]{1,0:T(8,128)(2,1)S(1)}, bf16[128,2560]{1,0:T(8,128)(2,1)S(1)}, u32[]{:S(2)}, u32[]{:S(2)}) collective-permute-start(bf16[128,2560]{1,0:T(8,128)(2,1)S(1)} %get-tuple-element.14.refs_1_.refs_8_), channel_id=1, source_target_pairs={{0,16},{8,24},{16,0},{24,8},{1,17},{9,25},{17,1},{25,9},{2,18},{10... | collective-permute-start | bytes 1966088 | tf_op jit(solution)/shard_map/ppermute | solution.py:218
  83.2 21.8 %collective-permute-start.30 = (bf16[128,2560]{1,0:T(8,128)(2,1)S(1)}, bf16[128,2560]{1,0:T(8,128)(2,1)S(1)}, u32[]{:S(2)}, u32[]{:S(2)}) collective-permute-start(bf16[128,2560]{1,0:T(8,128)(2,1)S(1)} %get-tuple-element.13.refs_0_.refs_8_), channel_id=1, source_target_pairs={{0,8},{8,0},{16,24},{24,16},{1,9},{9,1},{17,25},{25,17},{2,10},{10... | collective-permute-start | bytes 1966088 | tf_op jit(solution)/shard_map/ppermute | solution.py:218
  84.1 13.4 %collective-permute-start.22 = (bf16[8,32,512]{2,1,0:T(8,128)(2,1)S(1)}, bf16[8,32,512]{2,1,0:T(8,128)(2,1)S(1)}, u32[]{:S(2)}, u32[]{:S(2)}) collective-permute-start(bf16[8,32,512]{2,1,0:T(8,128)(2,1)S(1)} %collective-permute-done.21), channel_id=1, source_target_pairs={{2,0},{3,1},{4,6},{5,7},{10,8},{11,9},{12,14},{13,15},{18,16},{19,... | collective-permute-start | bytes 786440 | tf_op jit(solution)/shard_map/ppermute | solution.py:214
  92.3 6.7 %collective-permute-start.10 = (bf16[128,1024]{1,0:T(8,128)(2,1)S(1)}, bf16[128,1024]{1,0:T(8,128)(2,1)S(1)}, u32[]{:S(2)}, u32[]{:S(2)}) collective-permute-start(bf16[128,1024]{1,0:T(8,128)(2,1)S(1)} %get-tuple-element.29), channel_id=1, source_target_pairs={{0,2},{1,3},{6,4},{7,5},{8,10},{9,11},{14,12},{15,13},{16,18},{17,... | collective-permute-start | bytes 786440 | tf_op jit(solution)/shard_map/ppermute | solution.py:214
  93.8 9.7 %collective-permute-start.25 = (bf16[8,32,512]{2,1,0:T(8,128)(2,1)S(1)}, bf16[8,32,512]{2,1,0:T(8,128)(2,1)S(1)}, u32[]{:S(2)}, u32[]{:S(2)}) collective-permute-start(bf16[8,32,512]{2,1,0:T(8,128)(2,1)S(1)} %broadcast_select_fusion.1.refs_2_), channel_id=1, source_target_pairs={{0,1},{1,0},{2,3},{3,2},{4,5},{5,4},{6,7},{7,6},{8,9},{9,8},{10,11... | collective-permute-start | bytes 786440 | tf_op jit(solution)/shard_map/ppermute | solution.py:214
  97.5 17.6 %collective-permute-start.31 = (bf16[128,2560]{1,0:T(8,128)(2,1)S(1)}, bf16[128,2560]{1,0:T(8,128)(2,1)S(1)}, u32[]{:S(2)}, u32[]{:S(2)}) collective-permute-start(bf16[128,2560]{1,0:T(8,128)(2,1)S(1)} %get-tuple-element.13.refs_0_.refs_8_), channel_id=1, source_target_pairs={{0,16},{8,24},{16,0},{24,8},{1,17},{9,25},{17,1},{25,9},{2,18},{10... | collective-permute-start | bytes 1966088 | tf_op jit(solution)/shard_map/ppermute | solution.py:218
  99.0 8.8 %collective-permute-start.13 = (bf16[128,1024]{1,0:T(8,128)(2,1)S(1)}, bf16[128,1024]{1,0:T(8,128)(2,1)S(1)}, u32[]{:S(2)}, u32[]{:S(2)}) collective-permute-start(bf16[128,1024]{1,0:T(8,128)(2,1)S(1)} %get-tuple-element.30), channel_id=1, source_target_pairs={{0,2},{1,3},{6,4},{7,5},{8,10},{9,11},{14,12},{15,13},{16,18},{17,... | collective-permute-start | bytes 786440 | tf_op jit(solution)/shard_map/ppermute | solution.py:214
  103.4 5.1 %collective-permute-start.11 = (bf16[128,1024]{1,0:T(8,128)(2,1)S(1)}, bf16[128,1024]{1,0:T(8,128)(2,1)S(1)}, u32[]{:S(2)}, u32[]{:S(2)}) collective-permute-start(bf16[128,1024]{1,0:T(8,128)(2,1)S(1)} %add_convert_fusion.2), channel_id=1, source_target_pairs={{2,4},{3,5},{4,2},{5,3},{10,12},{11,13},{12,10},{13,11},{18,20},{1... | collective-permute-start | bytes 786440 | tf_op jit(solution)/shard_map/ppermute | solution.py:214
  104.1 27.2 %collective-permute-start.27 = (bf16[128,2560]{1,0:T(8,128)(2,1)S(1)}, bf16[128,2560]{1,0:T(8,128)(2,1)S(1)}, u32[]{:S(2)}, u32[]{:S(2)}) collective-permute-start(bf16[128,2560]{1,0:T(8,128)(2,1)S(1)} %get-tuple-element.14.refs_1_.refs_8_), channel_id=1, source_target_pairs={{0,8},{8,0},{16,24},{24,16},{1,9},{9,1},{17,25},{25,17},{2,10},{10... | collective-permute-start | bytes 1966088 | tf_op jit(solution)/shard_map/ppermute | solution.py:218
  105.0 28.3 %collective-permute-start.29 = (bf16[128,2560]{1,0:T(8,128)(2,1)S(1)}, bf16[128,2560]{1,0:T(8,128)(2,1)S(1)}, u32[]{:S(2)}, u32[]{:S(2)}) collective-permute-start(bf16[128,2560]{1,0:T(8,128)(2,1)S(1)} %collective-permute-done.28.refs_10_), channel_id=1, source_target_pairs={{0,8},{8,0},{16,24},{24,16},{1,9},{9,1},{17,25},{25,17},{2,10},{10... | collective-permute-start | bytes 1966088 | tf_op jit(solution)/shard_map/ppermute | solution.py:218
  107.7 20.2 %collective-permute-start.32 = (bf16[128,2560]{1,0:T(8,128)(2,1)S(1)}, bf16[128,2560]{1,0:T(8,128)(2,1)S(1)}, u32[]{:S(2)}, u32[]{:S(2)}) collective-permute-start(bf16[128,2560]{1,0:T(8,128)(2,1)S(1)} %collective-permute-done.30.refs_9_), channel_id=1, source_target_pairs={{0,16},{8,24},{16,0},{24,8},{1,17},{9,25},{17,1},{25,9},{2,18},{10... | collective-permute-start | bytes 1966088 | tf_op jit(solution)/shard_map/ppermute | solution.py:218
  108.5 1.6 %collective-permute-start.26 = (bf16[8,32,512]{2,1,0:T(8,128)(2,1)S(1)}, bf16[8,32,512]{2,1,0:T(8,128)(2,1)S(1)}, u32[]{:S(2)}, u32[]{:S(2)}) collective-permute-start(bf16[8,32,512]{2,1,0:T(8,128)(2,1)S(1)} %broadcast_select_fusion.refs_3_), channel_id=1, source_target_pairs={{0,1},{1,0},{2,3},{3,2},{4,5},{5,4},{6,7},{7,6},{8,9},{9,8},{10,11... | collective-permute-start | bytes 786440 | tf_op jit(solution)/shard_map/ppermute | solution.py:214
  110.1 28.3 %collective-permute-start.14 = (bf16[128,1024]{1,0:T(8,128)(2,1)S(1)}, bf16[128,1024]{1,0:T(8,128)(2,1)S(1)}, u32[]{:S(2)}, u32[]{:S(2)}) collective-permute-start(bf16[128,1024]{1,0:T(8,128)(2,1)S(1)} %get-tuple-element.28), channel_id=1, source_target_pairs={{2,4},{3,5},{4,2},{5,3},{10,12},{11,13},{12,10},{13,11},{18,20},{1... | collective-permute-start | bytes 786440 | tf_op jit(solution)/shard_map/ppermute | solution.py:214
  115.1 23.3 %collective-permute-start.12 = (bf16[128,1024]{1,0:T(8,128)(2,1)S(1)}, bf16[128,1024]{1,0:T(8,128)(2,1)S(1)}, u32[]{:S(2)}, u32[]{:S(2)}) collective-permute-start(bf16[128,1024]{1,0:T(8,128)(2,1)S(1)} %get-tuple-element.27), channel_id=1, source_target_pairs={{0,2},{1,3},{2,0},{3,1},{4,6},{5,7},{6,4},{7,5},{8,10},{9,11},{10,... | collective-permute-start | bytes 786440 | tf_op jit(solution)/shard_map/ppermute | solution.py:214
where the time goes:
time: 141 us; the launch traced here: 139 us
  waiting for transfers between devices  59.7 us (42%)
  starting transfers between devices  37.9 us (27%)
  Pallas kernels  23.3 us (17%)
  other arithmetic  8.96 us (6%)
  local copies, waits for them, and re-layouts  7.66 us (5%)
  between operations  1.77 us (1%)
    ppermute x24, waiting for transfers between devices, blk(): return lax.ppermute(x, 'blk', pairs)  37.8 us
    ppermute x24, starting transfers between devices, blk(): return lax.ppermute(x, 'blk', pairs)  29.5 us
    ppermute x9, waiting for transfers between devices, tok(): return lax.ppermute(x, 'tok', pairs)  22 us
    pallas_call x2, Pallas kernels, on_device(): pl.pallas_call(functools.partial(grad_kernel, k > 0, len(xq_shards), cuts...  8.52 us
    ppermute x9, starting transfers between devices, tok(): return lax.ppermute(x, 'tok', pairs)  8.42 us
    pallas_call x1, Pallas kernels, on_device(): pl.pallas_call(functools.partial(forward_kernel, len(shards), cuts), out_...  7.63 us
    pallas_call x1, Pallas kernels, on_device(): pl.pallas_call(functools.partial(term_kernel, len(hs), fast), out_shape=[...  6.98 us
    unnamed x13, local copies, waits for them, and re-layouts  5.58 us
  transfers between devices with their start and end apart: 33, of which 14 were waited for; matrix products, arithmetic and copies ran while one was open for 7% of the time, Pallas kernels for 6%

commit v1 on v0

v1 whole, which is shorter than its diff:
```python
import functools

import jax
import jax.numpy as jnp
from jax import lax
from jax.experimental import pallas as pl
from jax.experimental.pallas import tpu as pltpu
from jax.sharding import PartitionSpec as P


GROUP = 4
LIMIT = 16 * 1024 * 1024
VMEM = pl.BlockSpec(memory_space=pltpu.VMEM)
SMEM = pl.BlockSpec(memory_space=pltpu.SMEM)
ANY = pl.BlockSpec(memory_space=pl.ANY)
HBM = pl.BlockSpec(memory_space=pltpu.HBM)


def group_ranks(key, live, n_keys):
    ids = jnp.arange(key.shape[0], dtype=jnp.int32)
    keys = jnp.arange(n_keys, dtype=jnp.int32)
    same = (key[:, None] == key[None, :]) & (ids[None, :] < ids[:, None]) & live[None, :]
    rank = jnp.sum(same.astype(jnp.int32), axis=1)
    hit = (key[:, None] == keys[None, :]) & live[:, None]
    return rank, (jnp.sum(hit.astype(jnp.int32), axis=0) + GROUP - 1) // GROUP


def group_table(key, other, live, rank, groups, pad_other):
    slots, n_keys = key.shape[0], groups.shape[0]
    ids = jnp.arange(slots, dtype=jnp.int32)
    keys = jnp.arange(n_keys, dtype=jnp.int32)
    start = jnp.sum(jnp.where(keys[None, :] < key[:, None], groups[None, :], 0), axis=1)
    total = (slots + n_keys * (GROUP - 1) + GROUP - 1) // GROUP * GROUP
    place = jnp.where(live, start * GROUP + rank, total)
    pad = slots | (pad_other << 9)
    entry = ids | (other << 9) | (key << 16)
    at = jnp.arange(total, dtype=jnp.int32)
    return pad + jnp.sum(
        jnp.where(place[None, :] == at[:, None], (entry - pad)[None, :], 0), axis=1
    )


def each(lo, hi, body, unroll):
    n = hi - lo
    main = n // unroll

    def many(i, carry):
        for u in range(unroll):
            body(lo + i * unroll + u)
        return carry

    def one(i, carry):
        body(i)
        return carry

    lax.fori_loop(0, main, many, 0)
    lax.fori_loop(lo + main * unroll, hi, one, 0)


def unpack(tab, g):
    entries = [tab[g * GROUP + i] for i in range(GROUP)]
    return (
        [e & 511 for e in entries],
        [lax.shift_right_logical(e, 9) & 127 for e in entries],
        lax.shift_right_logical(entries[0], 16),
    )


def lanes(ref, i, block):
    return ref[:, pl.ds(pl.multiple_of(i * block, block), block)]


def panels_of(me, n):
    if n == 1:
        return [0]
    z, core = lax.shift_right_logical(me, 1), me & 1
    far = [z, z ^ 1, jnp.where(z < 2, 2, 1), jnp.where(z < 2, 3, 0)]
    return [f * 2 + core for f in far] + [f * 2 + 1 - core for f in far]


def total(groups, lo, hi):
    n = jnp.int32(0)
    for i in range(lo, hi):
        n += groups[i]
    return n


def copy_shards(shards, dst, me, per, sem):
    copies = []
    for i, (ref, panel) in enumerate(zip(shards, panels_of(me, len(shards)))):
        at = dst.at[pl.ds(panel * per, ref.shape[0])]
        copies.append(pltpu.make_async_copy(ref, at, sem.at[i]))
    for copy in copies:
        copy.start()
    return copies


def forward_kernel(shards, start, stop, tab, groups, me, *refs):
    if shards:
        x_in, refs = refs[:shards], refs[shards:]
        w_ref, cot_ref, act_out, h_ref, x_ref, acc, act_ref, sems = refs
        copies = copy_shards(x_in, x_ref, me[0], 1, sems)
    else:
        x_ref, w_ref, cot_ref, _, act_out, h_ref, acc, act_ref, sems = refs
        copies = []
    slots, block, _ = w_ref.shape
    per = x_ref.shape[2] // block
    acc[...] = jnp.zeros_like(acc)
    if shards:
        x_ref[x_ref.shape[0] - 1, :, 0:block] = jnp.zeros((x_ref.shape[1], block), x_ref.dtype)
    lo = total(groups, 0, start)
    hi = lo + total(groups, start, stop)
    for copy in copies:
        copy.wait()

    def group(g):
        ids, rows, col = unpack(tab, g)
        x = jnp.concatenate([lanes(x_ref.at[r // per], r % per, block) for r in rows], axis=1)
        w = jnp.concatenate([w_ref[jnp.minimum(s, slots - 1)] for s in ids], axis=0)
        acc[col - start] += jnp.dot(x, w, preferred_element_type=jnp.float32)

    each(lo, hi, group, 4)
    for c in range(stop - start):
        at = slice(c * block, (c + 1) * block)
        hidden = acc[c]
        gate = jax.nn.sigmoid(hidden)
        act_ref[:, at] = (hidden * gate).astype(act_ref.dtype)
        slope = gate * (1.0 + hidden * (1.0 - gate))
        cot = cot_ref[:, (start + c) * block : (start + c + 1) * block]
        h_ref[:, at] = (cot.astype(jnp.float32) * slope).astype(h_ref.dtype)
    copy = pltpu.make_async_copy(
        act_ref, act_out.at[:, start * block : stop * block], sems.at[sems.shape[0] - 1]
    )
    copy.start()
    copy.wait()


def term_kernel(chunks, fast, tab, groups, me, *refs):
    h_in = refs[:chunks]
    w_ref = refs[chunks]
    outs = refs[chunks + 1 : -2]
    h_ref, acc = refs[-2:]
    slots, block, _ = w_ref.shape
    acc[...] = jnp.zeros_like(acc)
    at = 0
    for ref in h_in:
        h_ref[:, at : at + ref.shape[1]] = ref[...]
        at += ref.shape[1]
    h_ref[:, at : at + block] = jnp.zeros((h_ref.shape[0], block), h_ref.dtype)

    def group(g):
        ids, cols, row = unpack(tab, g)
        h = jnp.concatenate([lanes(h_ref, c, block) for c in cols], axis=1)
        w = jnp.concatenate([w_ref[jnp.minimum(s, slots - 1)] for s in ids], axis=1)
        acc[row] += lax.dot_general(
            h, w, (((1,), (1,)), ((), ())), preferred_element_type=jnp.float32
        )

    each(0, total(groups, 0, groups.shape[0]), group, 4)
    panels = panels_of(me[0], 8) if fast else list(range(outs[0].shape[0]))
    for ref in outs:
        for i in range(ref.shape[0]):
            panel = panels.pop(0)
            per = ref.shape[2] // block
            for j in range(per):
                ref[i, :, j * block : (j + 1) * block] = acc[panel * per + j].astype(ref.dtype)


def grad_kernel(first, shards, heads, cuts, tokens, per, tab, groups, me, count, *refs):
    if first:
        x_in, refs = refs[:shards], refs[shards:]
    else:
        x_ref, sum_ref, refs = refs[0], refs[1], refs[2:]
    n = sum(heads)
    h_in, refs = refs[:n], refs[n:]
    out_ref = refs[0]
    copies = []
    if first:
        x_ref, sems = refs[1:]
        copies = copy_shards(x_in, x_ref, me[0], per, sems)
    slots, part, block = out_ref.shape

    def clear(s, carry):
        out_ref[s] = jnp.zeros((part, block), out_ref.dtype)
        return carry

    lax.fori_loop(jnp.minimum(count[0], slots), slots, clear, 0)
    for copy in copies:
        copy.wait()
    lo = jnp.int32(0)
    for k, head in enumerate(heads):
        mine, h_in = h_in[:head], h_in[head:]
        hi = lo + total(groups, cuts[k], cuts[k + 1])

        def group(g):
            ids, rows, col = unpack(tab, g)
            live = [s < slots for s in ids]
            ids = [jnp.where(l, s, ids[0]) for l, s in zip(live, ids)]
            rows = [jnp.where(l, r, rows[0]) for l, r in zip(live, rows)]
            x = jnp.concatenate([x_ref[r, :, tokens] for r in rows], axis=0)
            h = []
            for ref in mine:
                views = [ref] if len(ref.shape) == 2 else [ref.at[i] for i in range(ref.shape[0])]
                h += [lanes(v, col - cuts[k], block) for v in views]
            h = jnp.concatenate(h, axis=0)
            out = jnp.dot(x, h, preferred_element_type=jnp.float32)
            if not first:
                out += jnp.concatenate([sum_ref[s] for s in ids], axis=0)
            out = out.astype(out_ref.dtype)
            for i, s in enumerate(ids):
                out_ref[s] = out[i * part : (i + 1) * part]

        each(lo, hi, group, 4)
        lo = hi


def quarter_kernel(me, tok_ref, *refs):
    outs, scratch = refs[:-1], refs[-1]
    block = scratch.shape[1]
    part = outs[0].shape[1]
    for r in range(scratch.shape[0]):
        scratch[r] = tok_ref[:, r * block : (r + 1) * block].T
    for j, ref in enumerate(outs):
        at = pl.multiple_of((me[0] ^ j) * part, part)
        ref[...] = scratch[:, pl.ds(at, part), :]


def warm_kernel(w_ref, out_ref, sem):
    copy = pltpu.make_async_copy(w_ref.at[0, 0:8], out_ref, sem)
    copy.start()
    copy.wait()


def join_kernel(*refs):
    refs[-1][...] = jnp.concatenate([ref[...] for ref in refs[:-1]], axis=2)


def along_z(pairs):
    return [(a * 2 + c, b * 2 + c) for a, b in pairs for c in range(2)]


EVEN = along_z([(0, 1), (1, 0), (2, 3), (3, 2)])
ODD = along_z([(1, 2), (2, 1)])
OUTWARD = along_z([(1, 0), (2, 3)])
INWARD = along_z([(0, 1), (3, 2)])
CORES = [(b, b ^ 1) for b in range(8)]
TOK_X = [(t, t ^ 1) for t in range(4)]
TOK_Y = [(t, t ^ 2) for t in range(4)]
TOK_XY = [(t, t ^ 3) for t in range(4)]


def blk(x, pairs):
    return lax.ppermute(x, "blk", pairs)


def tok(x, pairs):
    return lax.ppermute(x, "tok", pairs)


def gather_line(x, middle):
    e1, o1 = blk(x, EVEN), blk(x, ODD)
    p0 = blk(x, CORES)
    o2, e2 = blk(e1, ODD), blk(o1, OUTWARD)
    p1 = blk(e1, CORES)
    e3 = blk(o2, OUTWARD)
    n2 = jnp.where(middle, o1, e2)
    p2 = blk(n2, CORES)
    n3 = jnp.where(middle, o2, e3)
    p3 = blk(n3, CORES)
    return [x, e1, n2, n3, p0, p1, p2, p3]


def call(body, out_shape, in_specs, out_specs, scratch, side=False, **kwargs):
    return pl.pallas_call(
        body,
        out_shape=out_shape,
        in_specs=in_specs,
        out_specs=out_specs,
        scratch_shapes=scratch,
        compiler_params=pltpu.CompilerParams(vmem_limit_bytes=LIMIT, has_side_effects=side),
        **kwargs,
    )


def on_device(n_tok, n_blk, tokens, w_blocks, blk_row, blk_col, blk_count, col_owner, cotangent):
    fast = (n_tok, n_blk) == (4, 8)
    rows_tok, width = tokens.shape
    slots, block, _ = w_blocks.shape
    cols = cotangent.shape[1] // block
    per = width // block
    n_rows = per * n_blk
    part = block // n_tok
    me_blk = lax.axis_index("blk").astype(jnp.int32)
    me_tok = lax.axis_index("tok").astype(jnp.int32)
    z = me_blk // 2
    middle = (z == 1) | (z == 2)
    me = me_blk[None]
    bf16 = tokens.dtype

    def shape(*dims, dtype=bf16):
        return jax.ShapeDtypeStruct(dims, dtype)

    if fast:
        shards = [s[None] for s in gather_line(tokens, middle)]
    else:
        shards = [lax.all_gather(tokens, "blk", axis=0)]

    mine = (col_owner == me_blk)[None, :]
    all_cols = jnp.arange(col_owner.shape[0], dtype=jnp.int32)[None, :]
    local = jnp.sum((mine & (all_cols < blk_col[:, None])).astype(jnp.int32), axis=1)
    live = jnp.arange(slots, dtype=jnp.int32) < blk_count[0]
    col_rank, col_groups = group_ranks(local, live, cols)
    row_rank, row_groups = group_ranks(blk_row, live, n_rows)
    col_tab = group_table(local, blk_row, live, col_rank, col_groups, n_rows)
    row_tab = group_table(blk_row, local, live, row_rank, row_groups, cols)

    xq = call(
        quarter_kernel,
        [shape(per, part, rows_tok)] * n_tok,
        [SMEM, VMEM],
        [VMEM] * n_tok,
        [pltpu.VMEM((per, block, rows_tok), bf16)],
    )(me_tok[None], tokens)
    if fast:
        moved = [tok(xq[1], TOK_X), tok(xq[2], TOK_Y), tok(xq[3], TOK_XY)]
        xq = call(
            join_kernel, shape(per, part, n_tok * rows_tok), [VMEM] * n_tok, VMEM, []
        )(xq[0], *moved)
        xq_shards = gather_line(xq, middle)
    else:
        order = me_tok ^ jnp.arange(n_tok)
        xq = jnp.take(jnp.stack(xq), order, axis=0)
        xq = lax.all_to_all(xq, "tok", split_axis=0, concat_axis=0, tiled=True)
        xq = xq.transpose(1, 2, 0, 3).reshape(per, part, n_tok * rows_tok)
        xq_shards = [lax.all_gather(xq, "blk", axis=0, tiled=True)]

    call(warm_kernel, shape(8, block), [HBM], VMEM, [pltpu.SemaphoreType.DMA], side=True)(w_blocks)

    cuts = (0, cols // 2, cols)
    hs = []
    x_all = act = None
    for k, (start, stop) in enumerate(zip(cuts[:-1], cuts[1:])):
        n = stop - start
        outs = [shape(*cotangent.shape), shape(rows_tok, n * block)]
        scratch = [
            pltpu.VMEM((n, rows_tok, block), jnp.float32),
            pltpu.VMEM((rows_tok, n * block), bf16),
        ]
        if k == 0:
            act, h, x_all = call(
                functools.partial(forward_kernel, len(shards), start, stop),
                outs + [shape(n_blk + 1, rows_tok, width)],
                [SMEM] * 3 + [ANY] * len(shards) + [VMEM, VMEM],
                [HBM, VMEM, VMEM],
                scratch + [pltpu.SemaphoreType.DMA((len(shards) + 1,))],
            )(col_tab, col_groups, me, *shards, w_blocks, cotangent)
        else:
            act, h = call(
                functools.partial(forward_kernel, 0, start, stop),
                outs,
                [SMEM] * 3 + [VMEM, VMEM, VMEM, HBM],
                [HBM, VMEM],
                scratch + [pltpu.SemaphoreType.DMA((1,))],
                input_output_aliases={6: 0},
            )(col_tab, col_groups, me, x_all, w_blocks, cotangent, act)
        hs.append(h)

    if fast:
        (a, b) = hs
        ax, ay = tok(a, TOK_X), tok(a, TOK_Y)
        bx, by = tok(b, TOK_X), tok(b, TOK_Y)
        ad, bd = tok(ax, TOK_Y), tok(by, TOK_X)
        near, far = [[a, ax, ay], [b, bx, by]], [[ad], [bd]]
    else:
        near, far = [[lax.all_gather(h, "tok", axis=0)] for h in hs], None

    outs = [4, 4] if fast else [n_blk]
    terms = call(
        functools.partial(term_kernel, len(hs), fast),
        [shape(n, rows_tok, width) for n in outs],
        [SMEM] * 3 + [VMEM] * (len(hs) + 1),
        [VMEM] * len(outs),
        [
            pltpu.VMEM((rows_tok, (cols + 1) * block), bf16),
            pltpu.VMEM((n_rows, rows_tok, block), jnp.float32),
        ],
    )(row_tab, row_groups, me, *hs, w_blocks)

    def add(*xs):
        return sum(x.astype(jnp.float32) for x in xs).astype(bf16)

    if fast:
        keep, send = terms
        q = add(keep, blk(send, CORES))
        own, close, mid, last = (q[i] for i in range(4))
        a1 = blk(last, INWARD)
        b1 = blk(mid, INWARD)
        a2 = blk(add(last, a1), ODD)
        e3 = blk(add(close, a2), EVEN)
        o3 = blk(add(mid, b1), ODD)
        input_grad = add(own, e3, o3)
    else:
        input_grad = lax.psum_scatter(terms[0], "blk", scatter_dimension=0, tiled=True)[0]

    n_tokens = n_tok * rows_tok
    split = n_tokens - rows_tok if fast else n_tokens
    tables = (col_tab, col_groups, me, blk_count)
    x_shape = (n_rows, part, n_tokens)
    heads = [len(h) for h in near]
    grad, xq_all = call(
        functools.partial(grad_kernel, True, len(xq_shards), heads, cuts, slice(0, split), per),
        [shape(slots, part, block, dtype=jnp.float32 if fast else bf16), shape(*x_shape)],
        [SMEM] * 4 + [ANY] * len(xq_shards) + [VMEM] * sum(heads),
        [VMEM, VMEM],
        [pltpu.SemaphoreType.DMA((len(xq_shards),))],
    )(*tables, *xq_shards, *sum(near, []))
    if fast:
        heads = [len(h) for h in far]
        grad = call(
            functools.partial(grad_kernel, False, 0, heads, cuts, slice(split, n_tokens), per),
            shape(slots, part, block),
            [SMEM] * 4 + [VMEM] * (2 + sum(heads)),
            VMEM,
            [],
        )(*tables, xq_all, grad, *sum(far, []))
    return act, input_grad, grad


def solution(mesh):
    n_tok, n_blk = mesh.shape["tok"], mesh.shape["blk"]

    def body(*args):
        return on_device(n_tok, n_blk, *args)

    return jax.shard_map(
        body,
        mesh=mesh,
        in_specs=(
            P("tok", "blk"),
            P("blk", None, None),
            P("blk"),
            P("blk"),
            P("blk"),
            P(),
            P("tok", "blk"),
        ),
        out_specs=(P("tok", "blk"), P("tok", "blk"), P("blk", "tok", None)),
        check_vma=False,
    )
```

time: 141 us -> 139 us (0.986)
  waiting for transfers between devices: 59.7 us -> 48.7 us
  Pallas kernels: 23.3 us -> 29.8 us
  local copies, waits for them, and re-layouts: 7.66 us -> 10.6 us
    ppermute x9, waiting for transfers between devices: 22 us -> 11.6 us  [tok(): return lax.ppermute(x, 'tok', pairs)]
    pallas_call x5 -> x8, Pallas kernels: 23.3 us -> 29.8 us  [the longest x1 7.95 us: on_device(): call(functools.partial(term_kernel, len(hs), fast), [shape(n, rows_tok, w...]
    unnamed x13 -> x12, local copies, waits for them, and re-layouts: 5.58 us -> 10.6 us
    another operation x1 -> x0, local copies, waits for them, and re-layouts: 2.02 us -> none  [on_device(): meta = jnp.stack([jnp.asarray(v, jnp.int32) for v in values + panels])]
    reduce_sum x3 -> x0, other arithmetic: 1.92 us -> none  [the longest x1 0.65 us: on_device(): jnp.sum(row_groups)]
  transfers between devices with their start and end apart: 33 -> 33, of which waited for: 14 -> 16; matrix products, arithmetic and copies ran while one was open for 7% -> 5% of each run, Pallas kernels for 6% -> 10%
where the time goes in v1:
time: 139 us; the launch traced here: 137 us
  waiting for transfers between devices  48.7 us (35%)
  starting transfers between devices  37.4 us (27%)
  Pallas kernels  29.8 us (21%)
  local copies, waits for them, and re-layouts  10.6 us (8%)
  other arithmetic  8.26 us (6%)
  between operations  1.74 us (1%)
    ppermute x24, waiting for transfers between devices, blk(): return lax.ppermute(x, 'blk', pairs)  37.2 us
    ppermute x24, starting transfers between devices, blk(): return lax.ppermute(x, 'blk', pairs)  30.1 us
    ppermute x9, waiting for transfers between devices, tok(): return lax.ppermute(x, 'tok', pairs)  11.6 us
    unnamed x12, local copies, waits for them, and re-layouts  10.6 us
    pallas_call x1, Pallas kernels, on_device(): call(functools.partial(term_kernel, len(hs), fast), [shape(n, rows_tok, w...  7.95 us
    ppermute x9, starting transfers between devices, tok(): return lax.ppermute(x, 'tok', pairs)  7.38 us
    pallas_call x1, Pallas kernels, on_device(): call(functools.partial(grad_kernel, False, 0, heads, cuts, slice(split, n...  6.23 us
    pallas_call x1, Pallas kernels, on_device(): call(functools.partial(grad_kernel, True, len(xq_shards), heads, cuts, sl...  6.15 us
  transfers between devices with their start and end apart: 33, of which 16 were waited for; matrix products, arithmetic and copies ran while one was open for 5% of the time, Pallas kernels for 10%

profile of v1, /device:TPU:0, one launch (start us, length us, event | category | flops | bytes accessed | tf_op | source)
XLA Modules:
  0.0 136.6 jit_solution(5665788929375777818)
XLA Ops:
  0.6 3.1 %collective-permute-start = (bf16[128,1024]{1,0:T(8,128)(2,1)}, bf16[128,1024]{1,0:T(8,128)(2,1)S(1)}, u32[]{:S(2)}, u32[]{:S(2)}) collective-permute-start(bf16[128,1024]{1,0:T(8,128)(2,1)} %tok_ref.1), channel_id=1, source_target_pairs={{0,2},{1,3},{2,0},{3,1},{4,6},{5,7},{6,4},{7,5},{8,10},{9,11},{10,... | collective-permute-start | bytes 786440 | tf_op jit(solution)/shard_map/ppermute | solution.py:253
  3.8 0.7 collective-permute-start.1
  5.2 0.7 broadcast_compare_fusion
  5.9 0.8 convert_reduce_fusion.2
  6.7 0.1 convert_reduce_fusion.4
  6.8 1.1 convert_reduce_fusion
  7.9 0.8 convert_reduce_fusion.3
  8.7 0.8 select_reduce_fusion.2
  9.5 0.1 select_reduce_fusion.3
  9.6 0.7 collective-permute-done
  10.3 0.7 collective-permute-start.3
  10.9 0.7 or_add_fusion
  11.6 1.3 collective-permute-start.2
  12.9 0.2 select_reduce_fusion.1
  13.1 1.3 collective-permute-start.4
  14.5 10.3 %collective-permute-done.2 = bf16[128,1024]{1,0:T(8,128)(2,1)S(1)} collective-permute-done((bf16[128,1024]{1,0:T(8,128)(2,1)S(1)}, bf16[128,1024]{1,0:T(8,128)(2,1)S(1)}, u32[]{:S(2)}, u32[]{:S(2)}) %collective-permute-start.2) | collective-permute-done | bytes 262176 | tf_op jit(solution)/shard_map/ppermute | solution.py:253
  25.0 7.0 %collective-permute-done.4 = bf16[128,1024]{1,0:T(8,128)(2,1)S(1)} collective-permute-done((bf16[128,1024]{1,0:T(8,128)(2,1)S(1)}, bf16[128,1024]{1,0:T(8,128)(2,1)S(1)}, u32[]{:S(2)}, u32[]{:S(2)}) %collective-permute-start.4) | collective-permute-done | bytes 262176 | tf_op jit(solution)/shard_map/ppermute | solution.py:253
  32.1 0.2 select_reduce_fusion
  32.3 1.3 collective-permute-done.8
  33.6 4.6 %copy-done = bf16[384,128,128]{2,1,0:T(8,128)(2,1)S(1)} copy-done((bf16[384,128,128]{2,1,0:T(8,128)(2,1)S(1)}, bf16[384,128,128]{2,1,0:T(8,128)(2,1)}, u32[]{:S(2)}) %copy-start) | copy-done | bytes 12582936
  38.2 0.9 copy-done.4
  39.1 4.3 %shard_map.95 = (bf16[128,5120]{1,0:T(8,128)(2,1)}, bf16[128,2560]{1,0:T(8,128)(2,1)S(1)}, bf16[9,128,1024]{2,1,0:T(8,128)(2,1)S(1)}) custom-call(s32[504]{0:T(512)S(1)} %broadcast_add_fusion.1.tab, s32[40]{0:T(128)S(1)} %and_select_fusion.1.groups, s32[1]{0:T(128)} %bitcast.1.me, bf16[1,128,1024]{2,1,0:T(8,128)(2,1)S(1)} %bitcast.31, ...), custom_call_target="tpu_custom_call" | custom-call | tf_op jit(solution)/shard_map/pallas_call | solution.py:350
  43.5 0.5 copy-done.1
  43.9 4.4 %shard_map.96 = (bf16[128,5120]{1,0:T(8,128)(2,1)}, bf16[128,2560]{1,0:T(8,128)(2,1)S(1)}) custom-call(s32[504]{0:T(512)S(1)} %broadcast_add_fusion.1.tab, s32[40]{0:T(128)S(1)} %and_select_fusion.1.groups, s32[1]{0:T(128)} %bitcast.1.me, bf16[9,128,1024]{2,1,0:T(8,128)(2,1)S(1)} %get-tuple-element.16.refs_0_, ...), custom_call_target="tpu_custom_call", output_to_operand_aliasing={{0}: (6, {})} | custom-call | tf_op jit(solution)/shard_map/pallas_call | solution.py:358
  48.3 8.0 %shard_map.97 = (bf16[4,128,1024]{2,1,0:T(8,128)(2,1)S(1)}, bf16[4,128,1024]{2,1,0:T(8,128)(2,1)}) custom-call(s32[576]{0:T(1024)S(1)} %broadcast_add_fusion.tab, s32[64]{0:T(128)S(1)} %and_select_fusion.groups, s32[1]{0:T(128)} %bitcast.1.me, bf16[128,2560]{1,0:T(8,128)(2,1)S(1)} %get-tuple-element.19.refs_0_.refs_8_, ...), custom_call_target="tpu_custom_call" | custom-call | tf_op jit(solution)/shard_map/pallas_call | solution.py:378
  56.3 7.8 %collective-permute-start.9 = (bf16[4,128,1024]{2,1,0:T(8,128)(2,1)}, bf16[4,128,1024]{2,1,0:T(8,128)(2,1)}, u32[]{:S(2)}, u32[]{:S(2)}) collective-permute-start(bf16[4,128,1024]{2,1,0:T(8,128)(2,1)} %get-tuple-element.22), channel_id=1, source_target_pairs={{0,1},{1,0},{2,3},{3,2},{4,5},{5,4},{6,7},{7,6},{8,9},{9,8},{10,11... | collective-permute-start | bytes 3145736 | tf_op jit(solution)/shard_map/ppermute | solution.py:253
  64.1 0.1 shard_map.98
  64.2 1.6 %collective-permute-start.15 = (bf16[8,32,128]{2,1,0:T(8,128)(2,1)S(1)}, bf16[8,32,128]{2,1,0:T(8,128)(2,1)S(1)}, u32[]{:S(2)}, u32[]{:S(2)}) collective-permute-start(bf16[8,32,128]{2,1,0:T(8,128)(2,1)S(1)} %get-tuple-element.24), channel_id=1, source_target_pairs={{0,8},{8,0},{16,24},{24,16},{1,9},{9,1},{17,25},{25,17},{2,10},{10... | collective-permute-start | bytes 196616 | tf_op jit(solution)/shard_map/ppermute | solution.py:257
  65.8 1.5 %collective-permute-start.16 = (bf16[8,32,128]{2,1,0:T(8,128)(2,1)S(1)}, bf16[8,32,128]{2,1,0:T(8,128)(2,1)S(1)}, u32[]{:S(2)}, u32[]{:S(2)}) collective-permute-start(bf16[8,32,128]{2,1,0:T(8,128)(2,1)S(1)} %get-tuple-element.25), channel_id=1, source_target_pairs={{0,16},{8,24},{16,0},{24,8},{1,17},{9,25},{17,1},{25,9},{2,18},{10... | collective-permute-start | bytes 196616 | tf_op jit(solution)/shard_map/ppermute | solution.py:257
  67.3 0.5 collective-permute-start.17
  67.8 0.8 collective-permute-done.15.refs_1_
  68.5 1.5 %collective-permute-done.16.refs_2_ = bf16[8,32,128]{2,1,0:T(8,128)(2,1)S(1)} collective-permute-done((bf16[8,32,128]{2,1,0:T(8,128)(2,1)S(1)}, bf16[8,32,128]{2,1,0:T(8,128)(2,1)S(1)}, u32[]{:S(2)}, u32[]{:S(2)}) %collective-permute-start.16) | collective-permute-done | bytes 65568 | tf_op jit(solution)/shard_map/ppermute | solution.py:257
  70.0 2.4 %collective-permute-done.17.refs_3_ = bf16[8,32,128]{2,1,0:T(8,128)(2,1)S(1)} collective-permute-done((bf16[8,32,128]{2,1,0:T(8,128)(2,1)S(1)}, bf16[8,32,128]{2,1,0:T(8,128)(2,1)S(1)}, u32[]{:S(2)}, u32[]{:S(2)}) %collective-permute-start.17) | collective-permute-done | bytes 65568 | tf_op jit(solution)/shard_map/ppermute | solution.py:257
  72.6 0.7 collective-permute-start.19
  73.3 5.7 %collective-permute-done.18.refs_1_ = bf16[8,32,512]{2,1,0:T(8,128)(2,1)S(1)} collective-permute-done((bf16[8,32,512]{2,1,0:T(8,128)(2,1)S(1)}, bf16[8,32,512]{2,1,0:T(8,128)(2,1)S(1)}, u32[]{:S(2)}, u32[]{:S(2)}) %collective-permute-start.18) | collective-permute-done | bytes 262176 | tf_op jit(solution)/shard_map/ppermute | solution.py:253
  79.1 0.7 collective-permute-start.21
  79.8 1.3 collective-permute-start.20
  81.1 0.6 collective-permute-start.30
  81.8 1.6 %add_convert_fusion = bf16[4,128,1024]{2,1,0:T(8,128)(2,1)S(1)} fusion(bf16[4,128,1024]{2,1,0:T(8,128)(2,1)} %collective-permute-done.9, bf16[4,128,1024]{2,1,0:T(8,128)(2,1)S(1)} %get-tuple-element.21), kind=kLoop, calls=%fused_computation | loop fusion | flops 2097152 | bytes 3145728 | tf_op jit(solution)/shard_map/convert_element_type | solution.py:390
  83.4 0.9 collective-permute-start.27
  84.3 1.3 collective-permute-start.22
  85.6 6.1 %collective-permute-done.20 = bf16[8,32,512]{2,1,0:T(8,128)(2,1)S(1)} collective-permute-done((bf16[8,32,512]{2,1,0:T(8,128)(2,1)S(1)}, bf16[8,32,512]{2,1,0:T(8,128)(2,1)S(1)}, u32[]{:S(2)}, u32[]{:S(2)}) %collective-permute-start.20) | collective-permute-done | bytes 262176 | tf_op jit(solution)/shard_map/ppermute | solution.py:253
  91.7 1.5 %collective-permute-start.10 = (bf16[128,1024]{1,0:T(8,128)(2,1)S(1)}, bf16[128,1024]{1,0:T(8,128)(2,1)S(1)}, u32[]{:S(2)}, u32[]{:S(2)}) collective-permute-start(bf16[128,1024]{1,0:T(8,128)(2,1)S(1)} %get-tuple-element.33), channel_id=1, source_target_pairs={{0,2},{1,3},{6,4},{7,5},{8,10},{9,11},{14,12},{15,13},{16,18},{17,... | collective-permute-start | bytes 786440 | tf_op jit(solution)/shard_map/ppermute | solution.py:253
  93.3 2.8 %collective-permute-done.22 = bf16[8,32,512]{2,1,0:T(8,128)(2,1)S(1)} collective-permute-done((bf16[8,32,512]{2,1,0:T(8,128)(2,1)S(1)}, bf16[8,32,512]{2,1,0:T(8,128)(2,1)S(1)}, u32[]{:S(2)}, u32[]{:S(2)}) %collective-permute-start.22) | collective-permute-done | bytes 262176 | tf_op jit(solution)/shard_map/ppermute | solution.py:253
  96.1 0.8 collective-permute-start.29
  96.8 0.2 collective-permute-done.10
  97.0 4.4 %collective-permute-start.13 = (bf16[128,1024]{1,0:T(8,128)(2,1)S(1)}, bf16[128,1024]{1,0:T(8,128)(2,1)S(1)}, u32[]{:S(2)}, u32[]{:S(2)}) collective-permute-start(bf16[128,1024]{1,0:T(8,128)(2,1)S(1)} %get-tuple-element.34), channel_id=1, source_target_pairs={{0,2},{1,3},{6,4},{7,5},{8,10},{9,11},{14,12},{15,13},{16,18},{17,... | collective-permute-start | bytes 786440 | tf_op jit(solution)/shard_map/ppermute | solution.py:253
  101.5 0.7 collective-permute-start.11
  102.2 0.3 collective-permute-start.28
  102.5 1.0 collective-permute-start.32
  103.5 1.7 %collective-permute-done.13 = bf16[128,1024]{1,0:T(8,128)(2,1)S(1)} collective-permute-done((bf16[128,1024]{1,0:T(8,128)(2,1)S(1)}, bf16[128,1024]{1,0:T(8,128)(2,1)S(1)}, u32[]{:S(2)}, u32[]{:S(2)}) %collective-permute-start.13) | collective-permute-done | bytes 262176 | tf_op jit(solution)/shard_map/ppermute | solution.py:253
  105.3 0.2 collective-permute-start.31
  105.6 0.2 fusion.4
  105.8 1.3 collective-permute-done.26.refs_7_
  107.1 3.5 %collective-permute-start.12 = (bf16[128,1024]{1,0:T(8,128)(2,1)S(1)}, bf16[128,1024]{1,0:T(8,128)(2,1)S(1)}, u32[]{:S(2)}, u32[]{:S(2)}) collective-permute-start(bf16[128,1024]{1,0:T(8,128)(2,1)S(1)} %get-tuple-element.31), channel_id=1, source_target_pairs={{0,2},{1,3},{2,0},{3,1},{4,6},{5,7},{6,4},{7,5},{8,10},{9,11},{10,... | collective-permute-start | bytes 786440 | tf_op jit(solution)/shard_map/ppermute | solution.py:253
  110.7 4.4 %collective-permute-done.29.refs_12_ = bf16[128,2560]{1,0:T(8,128)(2,1)S(1)} collective-permute-done((bf16[128,2560]{1,0:T(8,128)(2,1)S(1)}, bf16[128,2560]{1,0:T(8,128)(2,1)S(1)}, u32[]{:S(2)}, u32[]{:S(2)}) %collective-permute-start.29) | collective-permute-done | bytes 655392 | tf_op jit(solution)/shard_map/ppermute | solution.py:257
  115.1 0.7 collective-permute-start.14
  115.8 4.6 %copy-done.2 = bf16[384,128,128]{2,1,0:T(8,128)(2,1)S(1)} copy-done((bf16[384,128,128]{2,1,0:T(8,128)(2,1)S(1)}, bf16[384,128,128]{2,1,0:T(8,128)(2,1)}, u32[]{:S(2)}) %copy-start.2) | copy-done | bytes 12582936
  120.4 0.6 shard_map.94
  121.0 6.2 %shard_map.100 = (f32[384,32,128]{2,1,0:T(8,128)S(1)}, bf16[64,32,512]{2,1,0:T(8,128)(2,1)S(1)}) custom-call(s32[504]{0:T(512)S(1)} %broadcast_add_fusion.1.tab, s32[40]{0:T(128)S(1)} %and_select_fusion.1.groups, s32[1]{0:T(128)} %bitcast.1.me, s32[1]{0:T(128)} %copy.12.count, bf16[8,32,512]{2,1,0:T(8,128)(2,1)S(1)} %shard_map.99.refs_0_, ...), custom_call_target="tpu_custom_call" | custom-call | tf_op jit(solution)/shard_map/pallas_call | solution.py:410
  127.1 1.2 collective-permute-done.32.refs_3_
  128.4 1.2 collective-permute-done.31.refs_2_
  129.5 6.2 %shard_map.101 = bf16[384,32,128]{2,1,0:T(8,128)(2,1)} custom-call(s32[504]{0:T(512)S(1)} %broadcast_add_fusion.1.tab, s32[40]{0:T(128)S(1)} %and_select_fusion.1.groups, s32[1]{0:T(128)} %bitcast.1.me, s32[1]{0:T(128)} %copy.12.count, bf16[64,32,512]{2,1,0:T(8,128)(2,1)S(1)} %get-tuple-element.27.refs_0_, f32[384,32,128]{2,1,0:T(8,128)S(1)} %get-tuple-element.28.refs_1_, ...), custom_call_target="tpu_custom_call" | custom-call | tf_op jit(solution)/shard_map/pallas_call | solution.py:419
  135.8 0.8 fusion.6
  (47 shorter events, 1.0 us)
Async XLA Ops:
  0.6 33.0 %copy-start.3 = (bf16[128,5120]{1,0:T(8,128)(2,1)S(1)}, bf16[128,5120]{1,0:T(8,128)(2,1)}, u32[]{:S(2)}) copy-start(bf16[128,5120]{1,0:T(8,128)(2,1)} %refs_2_.2) | copy-start | bytes 3932164
  0.6 9.6 %collective-permute-start = (bf16[128,1024]{1,0:T(8,128)(2,1)}, bf16[128,1024]{1,0:T(8,128)(2,1)S(1)}, u32[]{:S(2)}, u32[]{:S(2)}) collective-permute-start(bf16[128,1024]{1,0:T(8,128)(2,1)} %tok_ref.1), channel_id=1, source_target_pairs={{0,2},{1,3},{2,0},{3,1},{4,6},{5,7},{6,4},{7,5},{8,10},{9,11},{10,... | collective-permute-start | bytes 786440 | tf_op jit(solution)/shard_map/ppermute | solution.py:253
  3.8 7.9 %collective-permute-start.1 = (bf16[128,1024]{1,0:T(8,128)(2,1)}, bf16[128,1024]{1,0:T(8,128)(2,1)S(1)}, u32[]{:S(2)}, u32[]{:S(2)}) collective-permute-start(bf16[128,1024]{1,0:T(8,128)(2,1)} %tok_ref.1), channel_id=1, source_target_pairs={{2,4},{3,5},{4,2},{5,3},{10,12},{11,13},{12,10},{13,11},{18,20},{1... | collective-permute-start | bytes 786440 | tf_op jit(solution)/shard_map/ppermute | solution.py:253
  4.4 27.8 %collective-permute-start.5 = (bf16[128,1024]{1,0:T(8,128)(2,1)}, bf16[128,1024]{1,0:T(8,128)(2,1)S(1)}, u32[]{:S(2)}, u32[]{:S(2)}) collective-permute-start(bf16[128,1024]{1,0:T(8,128)(2,1)} %tok_ref.1), channel_id=1, source_target_pairs={{0,1},{1,0},{2,3},{3,2},{4,5},{5,4},{6,7},{7,6},{8,9},{9,8},{10,11... | collective-permute-start | bytes 786440 | tf_op jit(solution)/shard_map/ppermute | solution.py:253
  10.3 2.8 %collective-permute-start.3 = (bf16[128,1024]{1,0:T(8,128)(2,1)S(1)}, bf16[128,1024]{1,0:T(8,128)(2,1)S(1)}, u32[]{:S(2)}, u32[]{:S(2)}) collective-permute-start(bf16[128,1024]{1,0:T(8,128)(2,1)S(1)} %collective-permute-done), channel_id=1, source_target_pairs={{2,4},{3,5},{4,2},{5,3},{10,12},{11,13},{12,10},{13,11},{18,20},{1... | collective-permute-start | bytes 786440 | tf_op jit(solution)/shard_map/ppermute | solution.py:253
  11.6 13.2 %collective-permute-start.2 = (bf16[128,1024]{1,0:T(8,128)(2,1)S(1)}, bf16[128,1024]{1,0:T(8,128)(2,1)S(1)}, u32[]{:S(2)}, u32[]{:S(2)}) collective-permute-start(bf16[128,1024]{1,0:T(8,128)(2,1)S(1)} %collective-permute-done.1), channel_id=1, source_target_pairs={{2,0},{3,1},{4,6},{5,7},{10,8},{11,9},{12,14},{13,15},{18,16},{19,... | collective-permute-start | bytes 786440 | tf_op jit(solution)/shard_map/ppermute | solution.py:253
  13.1 18.8 %collective-permute-start.4 = (bf16[128,1024]{1,0:T(8,128)(2,1)S(1)}, bf16[128,1024]{1,0:T(8,128)(2,1)S(1)}, u32[]{:S(2)}, u32[]{:S(2)}) collective-permute-start(bf16[128,1024]{1,0:T(8,128)(2,1)S(1)} %collective-permute-done.3), channel_id=1, source_target_pairs={{2,0},{3,1},{4,6},{5,7},{10,8},{11,9},{12,14},{13,15},{18,16},{19,... | collective-permute-start | bytes 786440 | tf_op jit(solution)/shard_map/ppermute | solution.py:253
  14.4 17.8 %collective-permute-start.6 = (bf16[128,1024]{1,0:T(8,128)(2,1)S(1)}, bf16[128,1024]{1,0:T(8,128)(2,1)S(1)}, u32[]{:S(2)}, u32[]{:S(2)}) collective-permute-start(bf16[128,1024]{1,0:T(8,128)(2,1)S(1)} %collective-permute-done), channel_id=1, source_target_pairs={{0,1},{1,0},{2,3},{3,2},{4,5},{5,4},{6,7},{7,6},{8,9},{9,8},{10,11... | collective-permute-start | bytes 786440 | tf_op jit(solution)/shard_map/ppermute | solution.py:253
  24.9 7.4 %collective-permute-start.7 = (bf16[128,1024]{1,0:T(8,128)(2,1)S(1)}, bf16[128,1024]{1,0:T(8,128)(2,1)S(1)}, u32[]{:S(2)}, u32[]{:S(2)}) collective-permute-start(bf16[128,1024]{1,0:T(8,128)(2,1)S(1)} %broadcast_select_fusion.3), channel_id=1, source_target_pairs={{0,1},{1,0},{2,3},{3,2},{4,5},{5,4},{6,7},{7,6},{8,9},{9,8},{10,11... | collective-permute-start | bytes 786440 | tf_op jit(solution)/shard_map/ppermute | solution.py:253
  32.0 1.6 %collective-permute-start.8 = (bf16[128,1024]{1,0:T(8,128)(2,1)S(1)}, bf16[128,1024]{1,0:T(8,128)(2,1)S(1)}, u32[]{:S(2)}, u32[]{:S(2)}) collective-permute-start(bf16[128,1024]{1,0:T(8,128)(2,1)S(1)} %broadcast_select_fusion.2), channel_id=1, source_target_pairs={{0,1},{1,0},{2,3},{3,2},{4,5},{5,4},{6,7},{7,6},{8,9},{9,8},{10,11... | collective-permute-start | bytes 786440 | tf_op jit(solution)/shard_map/ppermute | solution.py:253
  33.6 4.6 %copy-start = (bf16[384,128,128]{2,1,0:T(8,128)(2,1)S(1)}, bf16[384,128,128]{2,1,0:T(8,128)(2,1)}, u32[]{:S(2)}) copy-start(bf16[384,128,128]{2,1,0:T(8,128)(2,1)} %refs_2_.3) | copy-start | bytes 37748740
  38.2 0.9 copy-start.4
  39.1 4.8 %copy-start.1 = (bf16[384,128,128]{2,1,0:T(8,128)(2,1)S(1)}, bf16[384,128,128]{2,1,0:T(8,128)(2,1)}, u32[]{:S(2)}) copy-start(bf16[384,128,128]{2,1,0:T(8,128)(2,1)} %refs_2_.3) | copy-start | bytes 37748740
  48.3 15.7 %copy-start.5 = (bf16[128,1024]{1,0:T(8,128)(2,1)S(1)}, bf16[128,1024]{1,0:T(8,128)(2,1)}, u32[]{:S(2)}) copy-start(bf16[128,1024]{1,0:T(8,128)(2,1)} %tok_ref.1) | copy-start | bytes 786436
  56.3 24.9 %collective-permute-start.9 = (bf16[4,128,1024]{2,1,0:T(8,128)(2,1)}, bf16[4,128,1024]{2,1,0:T(8,128)(2,1)}, u32[]{:S(2)}, u32[]{:S(2)}) collective-permute-start(bf16[4,128,1024]{2,1,0:T(8,128)(2,1)} %get-tuple-element.22), channel_id=1, source_target_pairs={{0,1},{1,0},{2,3},{3,2},{4,5},{5,4},{6,7},{7,6},{8,9},{9,8},{10,11... | collective-permute-start | bytes 3145736 | tf_op jit(solution)/shard_map/ppermute | solution.py:253
  64.2 4.3 %collective-permute-start.15 = (bf16[8,32,128]{2,1,0:T(8,128)(2,1)S(1)}, bf16[8,32,128]{2,1,0:T(8,128)(2,1)S(1)}, u32[]{:S(2)}, u32[]{:S(2)}) collective-permute-start(bf16[8,32,128]{2,1,0:T(8,128)(2,1)S(1)} %get-tuple-element.24), channel_id=1, source_target_pairs={{0,8},{8,0},{16,24},{24,16},{1,9},{9,1},{17,25},{25,17},{2,10},{10... | collective-permute-start | bytes 196616 | tf_op jit(solution)/shard_map/ppermute | solution.py:257
  65.8 4.3 %collective-permute-start.16 = (bf16[8,32,128]{2,1,0:T(8,128)(2,1)S(1)}, bf16[8,32,128]{2,1,0:T(8,128)(2,1)S(1)}, u32[]{:S(2)}, u32[]{:S(2)}) collective-permute-start(bf16[8,32,128]{2,1,0:T(8,128)(2,1)S(1)} %get-tuple-element.25), channel_id=1, source_target_pairs={{0,16},{8,24},{16,0},{24,8},{1,17},{9,25},{17,1},{25,9},{2,18},{10... | collective-permute-start | bytes 196616 | tf_op jit(solution)/shard_map/ppermute | solution.py:257
  67.3 5.2 %collective-permute-start.17 = (bf16[8,32,128]{2,1,0:T(8,128)(2,1)S(1)}, bf16[8,32,128]{2,1,0:T(8,128)(2,1)S(1)}, u32[]{:S(2)}, u32[]{:S(2)}) collective-permute-start(bf16[8,32,128]{2,1,0:T(8,128)(2,1)S(1)} %get-tuple-element.26), channel_id=1, source_target_pairs={{0,24},{8,16},{16,8},{24,0},{1,25},{9,17},{17,9},{25,1},{2,26},{10... | collective-permute-start | bytes 196616 | tf_op jit(solution)/shard_map/ppermute | solution.py:257
  72.5 6.6 %collective-permute-start.18 = (bf16[8,32,512]{2,1,0:T(8,128)(2,1)S(1)}, bf16[8,32,512]{2,1,0:T(8,128)(2,1)S(1)}, u32[]{:S(2)}, u32[]{:S(2)}) collective-permute-start(bf16[8,32,512]{2,1,0:T(8,128)(2,1)S(1)} %shard_map.99.refs_0_), channel_id=1, source_target_pairs={{0,2},{1,3},{2,0},{3,1},{4,6},{5,7},{6,4},{7,5},{8,10},{9,11},{10,... | collective-permute-start | bytes 786440 | tf_op jit(solution)/shard_map/ppermute | solution.py:253
  72.6 7.2 %collective-permute-start.19 = (bf16[8,32,512]{2,1,0:T(8,128)(2,1)S(1)}, bf16[8,32,512]{2,1,0:T(8,128)(2,1)S(1)}, u32[]{:S(2)}, u32[]{:S(2)}) collective-permute-start(bf16[8,32,512]{2,1,0:T(8,128)(2,1)S(1)} %shard_map.99.refs_0_), channel_id=1, source_target_pairs={{2,4},{3,5},{4,2},{5,3},{10,12},{11,13},{12,10},{13,11},{18,20},{1... | collective-permute-start | bytes 786440 | tf_op jit(solution)/shard_map/ppermute | solution.py:253
  73.3 10.1 %collective-permute-start.23 = (bf16[8,32,512]{2,1,0:T(8,128)(2,1)S(1)}, bf16[8,32,512]{2,1,0:T(8,128)(2,1)S(1)}, u32[]{:S(2)}, u32[]{:S(2)}) collective-permute-start(bf16[8,32,512]{2,1,0:T(8,128)(2,1)S(1)} %shard_map.99.refs_0_), channel_id=1, source_target_pairs={{0,1},{1,0},{2,3},{3,2},{4,5},{5,4},{6,7},{7,6},{8,9},{9,8},{10,11... | collective-permute-start | bytes 786440 | tf_op jit(solution)/shard_map/ppermute | solution.py:253
  79.1 5.2 %collective-permute-start.21 = (bf16[8,32,512]{2,1,0:T(8,128)(2,1)S(1)}, bf16[8,32,512]{2,1,0:T(8,128)(2,1)S(1)}, u32[]{:S(2)}, u32[]{:S(2)}) collective-permute-start(bf16[8,32,512]{2,1,0:T(8,128)(2,1)S(1)} %collective-permute-done.18.refs_1_), channel_id=1, source_target_pairs={{2,4},{3,5},{4,2},{5,3},{10,12},{11,13},{12,10},{13,11},{18,20},{1... | collective-permute-start | bytes 786440 | tf_op jit(solution)/shard_map/ppermute | solution.py:253
  79.7 13.4 %collective-permute-start.24 = (bf16[8,32,512]{2,1,0:T(8,128)(2,1)S(1)}, bf16[8,32,512]{2,1,0:T(8,128)(2,1)S(1)}, u32[]{:S(2)}, u32[]{:S(2)}) collective-permute-start(bf16[8,32,512]{2,1,0:T(8,128)(2,1)S(1)} %collective-permute-done.18.refs_1_), channel_id=1, source_target_pairs={{0,1},{1,0},{2,3},{3,2},{4,5},{5,4},{6,7},{7,6},{8,9},{9,8},{10,11... | collective-permute-start | bytes 786440 | tf_op jit(solution)/shard_map/ppermute | solution.py:253
  79.8 11.9 %collective-permute-start.20 = (bf16[8,32,512]{2,1,0:T(8,128)(2,1)S(1)}, bf16[8,32,512]{2,1,0:T(8,128)(2,1)S(1)}, u32[]{:S(2)}, u32[]{:S(2)}) collective-permute-start(bf16[8,32,512]{2,1,0:T(8,128)(2,1)S(1)} %collective-permute-done.19), channel_id=1, source_target_pairs={{2,0},{3,1},{4,6},{5,7},{10,8},{11,9},{12,14},{13,15},{18,16},{19,... | collective-permute-start | bytes 786440 | tf_op jit(solution)/shard_map/ppermute | solution.py:253
  81.1 21.0 %collective-permute-start.30 = (bf16[128,2560]{1,0:T(8,128)(2,1)S(1)}, bf16[128,2560]{1,0:T(8,128)(2,1)S(1)}, u32[]{:S(2)}, u32[]{:S(2)}) collective-permute-start(bf16[128,2560]{1,0:T(8,128)(2,1)S(1)} %get-tuple-element.20.refs_1_.refs_11_), channel_id=1, source_target_pairs={{0,16},{8,24},{16,0},{24,8},{1,17},{9,25},{17,1},{25,9},{2,18},{10... | collective-permute-start | bytes 1966088 | tf_op jit(solution)/shard_map/ppermute | solution.py:257
  83.4 19.1 %collective-permute-start.27 = (bf16[128,2560]{1,0:T(8,128)(2,1)S(1)}, bf16[128,2560]{1,0:T(8,128)(2,1)S(1)}, u32[]{:S(2)}, u32[]{:S(2)}) collective-permute-start(bf16[128,2560]{1,0:T(8,128)(2,1)S(1)} %get-tuple-element.19.refs_0_.refs_8_), channel_id=1, source_target_pairs={{0,8},{8,0},{16,24},{24,16},{1,9},{9,1},{17,25},{25,17},{2,10},{10... | collective-permute-start | bytes 1966088 | tf_op jit(solution)/shard_map/ppermute | solution.py:257
  84.3 11.7 %collective-permute-start.22 = (bf16[8,32,512]{2,1,0:T(8,128)(2,1)S(1)}, bf16[8,32,512]{2,1,0:T(8,128)(2,1)S(1)}, u32[]{:S(2)}, u32[]{:S(2)}) collective-permute-start(bf16[8,32,512]{2,1,0:T(8,128)(2,1)S(1)} %collective-permute-done.21), channel_id=1, source_target_pairs={{2,0},{3,1},{4,6},{5,7},{10,8},{11,9},{12,14},{13,15},{18,16},{19,... | collective-permute-start | bytes 786440 | tf_op jit(solution)/shard_map/ppermute | solution.py:253
  91.7 5.3 %collective-permute-start.10 = (bf16[128,1024]{1,0:T(8,128)(2,1)S(1)}, bf16[128,1024]{1,0:T(8,128)(2,1)S(1)}, u32[]{:S(2)}, u32[]{:S(2)}) collective-permute-start(bf16[128,1024]{1,0:T(8,128)(2,1)S(1)} %get-tuple-element.33), channel_id=1, source_target_pairs={{0,2},{1,3},{6,4},{7,5},{8,10},{9,11},{14,12},{15,13},{16,18},{17,... | collective-permute-start | bytes 786440 | tf_op jit(solution)/shard_map/ppermute | solution.py:253
  93.2 8.3 %collective-permute-start.25 = (bf16[8,32,512]{2,1,0:T(8,128)(2,1)S(1)}, bf16[8,32,512]{2,1,0:T(8,128)(2,1)S(1)}, u32[]{:S(2)}, u32[]{:S(2)}) collective-permute-start(bf16[8,32,512]{2,1,0:T(8,128)(2,1)S(1)} %broadcast_select_fusion.1.refs_2_), channel_id=1, source_target_pairs={{0,1},{1,0},{2,3},{3,2},{4,5},{5,4},{6,7},{7,6},{8,9},{9,8},{10,11... | collective-permute-start | bytes 786440 | tf_op jit(solution)/shard_map/ppermute | solution.py:253
  96.1 19.0 %collective-permute-start.29 = (bf16[128,2560]{1,0:T(8,128)(2,1)S(1)}, bf16[128,2560]{1,0:T(8,128)(2,1)S(1)}, u32[]{:S(2)}, u32[]{:S(2)}) collective-permute-start(bf16[128,2560]{1,0:T(8,128)(2,1)S(1)} %get-tuple-element.20.refs_1_.refs_11_), channel_id=1, source_target_pairs={{0,8},{8,0},{16,24},{24,16},{1,9},{9,1},{17,25},{25,17},{2,10},{10... | collective-permute-start | bytes 1966088 | tf_op jit(solution)/shard_map/ppermute | solution.py:257
  97.0 8.3 %collective-permute-start.13 = (bf16[128,1024]{1,0:T(8,128)(2,1)S(1)}, bf16[128,1024]{1,0:T(8,128)(2,1)S(1)}, u32[]{:S(2)}, u32[]{:S(2)}) collective-permute-start(bf16[128,1024]{1,0:T(8,128)(2,1)S(1)} %get-tuple-element.34), channel_id=1, source_target_pairs={{0,2},{1,3},{6,4},{7,5},{8,10},{9,11},{14,12},{15,13},{16,18},{17,... | collective-permute-start | bytes 786440 | tf_op jit(solution)/shard_map/ppermute | solution.py:253
  101.5 4.0 %collective-permute-start.11 = (bf16[128,1024]{1,0:T(8,128)(2,1)S(1)}, bf16[128,1024]{1,0:T(8,128)(2,1)S(1)}, u32[]{:S(2)}, u32[]{:S(2)}) collective-permute-start(bf16[128,1024]{1,0:T(8,128)(2,1)S(1)} %add_convert_fusion.2), channel_id=1, source_target_pairs={{2,4},{3,5},{4,2},{5,3},{10,12},{11,13},{12,10},{13,11},{18,20},{1... | collective-permute-start | bytes 786440 | tf_op jit(solution)/shard_map/ppermute | solution.py:253
  102.2 18.8 %collective-permute-start.28 = (bf16[128,2560]{1,0:T(8,128)(2,1)S(1)}, bf16[128,2560]{1,0:T(8,128)(2,1)S(1)}, u32[]{:S(2)}, u32[]{:S(2)}) collective-permute-start(bf16[128,2560]{1,0:T(8,128)(2,1)S(1)} %get-tuple-element.19.refs_0_.refs_8_), channel_id=1, source_target_pairs={{0,16},{8,24},{16,0},{24,8},{1,17},{9,25},{17,1},{25,9},{2,18},{10... | collective-permute-start | bytes 1966088 | tf_op jit(solution)/shard_map/ppermute | solution.py:257
  102.5 25.9 %collective-permute-start.32 = (bf16[128,2560]{1,0:T(8,128)(2,1)S(1)}, bf16[128,2560]{1,0:T(8,128)(2,1)S(1)}, u32[]{:S(2)}, u32[]{:S(2)}) collective-permute-start(bf16[128,2560]{1,0:T(8,128)(2,1)S(1)} %collective-permute-done.30.refs_13_), channel_id=1, source_target_pairs={{0,8},{8,0},{16,24},{24,16},{1,9},{9,1},{17,25},{25,17},{2,10},{10... | collective-permute-start | bytes 1966088 | tf_op jit(solution)/shard_map/ppermute | solution.py:257
  105.3 24.3 %collective-permute-start.31 = (bf16[128,2560]{1,0:T(8,128)(2,1)S(1)}, bf16[128,2560]{1,0:T(8,128)(2,1)S(1)}, u32[]{:S(2)}, u32[]{:S(2)}) collective-permute-start(bf16[128,2560]{1,0:T(8,128)(2,1)S(1)} %collective-permute-done.27.refs_9_), channel_id=1, source_target_pairs={{0,16},{8,24},{16,0},{24,8},{1,17},{9,25},{17,1},{25,9},{2,18},{10... | collective-permute-start | bytes 1966088 | tf_op jit(solution)/shard_map/ppermute | solution.py:257
  105.5 1.6 %collective-permute-start.26 = (bf16[8,32,512]{2,1,0:T(8,128)(2,1)S(1)}, bf16[8,32,512]{2,1,0:T(8,128)(2,1)S(1)}, u32[]{:S(2)}, u32[]{:S(2)}) collective-permute-start(bf16[8,32,512]{2,1,0:T(8,128)(2,1)S(1)} %broadcast_select_fusion.refs_3_), channel_id=1, source_target_pairs={{0,1},{1,0},{2,3},{3,2},{4,5},{5,4},{6,7},{7,6},{8,9},{9,8},{10,11... | collective-permute-start | bytes 786440 | tf_op jit(solution)/shard_map/ppermute | solution.py:253
  107.1 28.6 %collective-permute-start.12 = (bf16[128,1024]{1,0:T(8,128)(2,1)S(1)}, bf16[128,1024]{1,0:T(8,128)(2,1)S(1)}, u32[]{:S(2)}, u32[]{:S(2)}) collective-permute-start(bf16[128,1024]{1,0:T(8,128)(2,1)S(1)} %get-tuple-element.31), channel_id=1, source_target_pairs={{0,2},{1,3},{2,0},{3,1},{4,6},{5,7},{6,4},{7,5},{8,10},{9,11},{10,... | collective-permute-start | bytes 786440 | tf_op jit(solution)/shard_map/ppermute | solution.py:253
  115.1 20.7 %collective-permute-start.14 = (bf16[128,1024]{1,0:T(8,128)(2,1)S(1)}, bf16[128,1024]{1,0:T(8,128)(2,1)S(1)}, u32[]{:S(2)}, u32[]{:S(2)}) collective-permute-start(bf16[128,1024]{1,0:T(8,128)(2,1)S(1)} %get-tuple-element.32), channel_id=1, source_target_pairs={{2,4},{3,5},{4,2},{5,3},{10,12},{11,13},{12,10},{13,11},{18,20},{1... | collective-permute-start | bytes 786440 | tf_op jit(solution)/shard_map/ppermute | solution.py:253
  115.8 4.6 %copy-start.2 = (bf16[384,128,128]{2,1,0:T(8,128)(2,1)S(1)}, bf16[384,128,128]{2,1,0:T(8,128)(2,1)}, u32[]{:S(2)}) copy-start(bf16[384,128,128]{2,1,0:T(8,128)(2,1)} %refs_2_.3) | copy-start | bytes 37748740

commit v2 on v1

--- a/solution.py
+++ b/solution.py
@@ -85,11 +85,16 @@
     return n
 
 
-def copy_shards(shards, dst, me, per, sem):
+def copy_shards(shards, dst, me, per, sems):
+    whole = len(shards) == 1
+    panels = panels_of(me, 1 if whole else 8)
     copies = []
-    for i, (ref, panel) in enumerate(zip(shards, panels_of(me, len(shards)))):
-        at = dst.at[pl.ds(panel * per, ref.shape[0])]
-        copies.append(pltpu.make_async_copy(ref, at, sem.at[i]))
+    for ref in shards:
+        n = ref.shape[0] if whole else per
+        for i in range(ref.shape[0] // n):
+            at = dst.at[pl.ds(panels.pop(0) * per, n)]
+            sem = sems.at[len(copies)]
+            copies.append(pltpu.make_async_copy(ref.at[pl.ds(i * n, n)], at, sem))
     for copy in copies:
         copy.start()
     return copies
@@ -98,13 +103,16 @@
 def forward_kernel(shards, start, stop, tab, groups, me, *refs):
     if shards:
         x_in, refs = refs[:shards], refs[shards:]
-        w_ref, cot_ref, act_out, h_ref, x_ref, acc, act_ref, sems = refs
+        w_ref, cot_ref, act_ref, h_ref, x_ref, acc, sems = refs
         copies = copy_shards(x_in, x_ref, me[0], 1, sems)
     else:
-        x_ref, w_ref, cot_ref, _, act_out, h_ref, acc, act_ref, sems = refs
+        x_ref, w_ref, cot_ref, before, act_out, h_ref, acc, act_ref, sems = refs
         copies = []
     slots, block, _ = w_ref.shape
     per = x_ref.shape[2] // block
+    if not shards:
+        left = pltpu.make_async_copy(before, act_out.at[:, : start * block], sems.at[0])
+        left.start()
     acc[...] = jnp.zeros_like(acc)
     if shards:
         x_ref[x_ref.shape[0] - 1, :, 0:block] = jnp.zeros((x_ref.shape[1], block), x_ref.dtype)
@@ -128,11 +136,13 @@
         slope = gate * (1.0 + hidden * (1.0 - gate))
         cot = cot_ref[:, (start + c) * block : (start + c + 1) * block]
         h_ref[:, at] = (cot.astype(jnp.float32) * slope).astype(h_ref.dtype)
-    copy = pltpu.make_async_copy(
-        act_ref, act_out.at[:, start * block : stop * block], sems.at[sems.shape[0] - 1]
-    )
-    copy.start()
-    copy.wait()
+    if not shards:
+        right = pltpu.make_async_copy(
+            act_ref, act_out.at[:, start * block : stop * block], sems.at[1]
+        )
+        right.start()
+        left.wait()
+        right.wait()
 
 
 def term_kernel(chunks, fast, tab, groups, me, *refs):
@@ -141,6 +151,7 @@
     outs = refs[chunks + 1 : -2]
     h_ref, acc = refs[-2:]
     slots, block, _ = w_ref.shape
+    per = outs[0].shape[2] // block
     acc[...] = jnp.zeros_like(acc)
     at = 0
     for ref in h_in:
@@ -161,7 +172,6 @@
     for ref in outs:
         for i in range(ref.shape[0]):
             panel = panels.pop(0)
-            per = ref.shape[2] // block
             for j in range(per):
                 ref[i, :, j * block : (j + 1) * block] = acc[panel * per + j].astype(ref.dtype)
 
@@ -214,12 +224,14 @@
         lo = hi
 
 
-def quarter_kernel(me, tok_ref, *refs):
-    outs, scratch = refs[:-1], refs[-1]
+def quarter_kernel(shards, me, *refs):
+    x_in, outs, scratch = refs[:shards], refs[shards:-1], refs[-1]
     block = scratch.shape[1]
     part = outs[0].shape[1]
-    for r in range(scratch.shape[0]):
-        scratch[r] = tok_ref[:, r * block : (r + 1) * block].T
+    per = scratch.shape[0] // shards
+    for i, ref in enumerate(x_in):
+        for r in range(per):
+            scratch[i * per + r] = ref[:, r * block : (r + 1) * block].T
     for j, ref in enumerate(outs):
         at = pl.multiple_of((me[0] ^ j) * part, part)
         ref[...] = scratch[:, pl.ds(at, part), :]
@@ -314,20 +326,29 @@
     col_tab = group_table(local, blk_row, live, col_rank, col_groups, n_rows)
     row_tab = group_table(blk_row, local, live, row_rank, row_groups, cols)
 
-    xq = call(
-        quarter_kernel,
-        [shape(per, part, rows_tok)] * n_tok,
-        [SMEM, VMEM],
-        [VMEM] * n_tok,
-        [pltpu.VMEM((per, block, rows_tok), bf16)],
-    )(me_tok[None], tokens)
+    def quarter(parts):
+        n = len(parts) * per
+        return call(
+            functools.partial(quarter_kernel, len(parts)),
+            [shape(n, part, rows_tok)] * n_tok,
+            [SMEM] + [VMEM] * len(parts),
+            [VMEM] * n_tok,
+            [pltpu.VMEM((n, block, rows_tok), bf16)],
+        )(me_tok[None], *parts)
+
     if fast:
-        moved = [tok(xq[1], TOK_X), tok(xq[2], TOK_Y), tok(xq[3], TOK_XY)]
-        xq = call(
-            join_kernel, shape(per, part, n_tok * rows_tok), [VMEM] * n_tok, VMEM, []
-        )(xq[0], *moved)
-        xq_shards = gather_line(xq, middle)
-    else:
+        mine, theirs = [], []
+        for k in range(2):
+            xq = quarter([s[0] for s in shards[2 * k : 2 * k + 2]])
+            xq = [xq[0], tok(xq[1], TOK_X), tok(xq[2], TOK_Y), tok(xq[3], TOK_XY)]
+            xq = call(
+                join_kernel, shape(2 * per, part, n_tok * rows_tok), [VMEM] * n_tok, VMEM, []
+            )(*xq)
+            mine.append(xq)
+            theirs.append(blk(xq, CORES))
+        xq_shards = mine + theirs
+    else:
+        xq = quarter([tokens])
         order = me_tok ^ jnp.arange(n_tok)
         xq = jnp.take(jnp.stack(xq), order, axis=0)
         xq = lax.all_to_all(xq, "tok", split_axis=0, concat_axis=0, tiled=True)
@@ -341,27 +362,24 @@
     x_all = act = None
     for k, (start, stop) in enumerate(zip(cuts[:-1], cuts[1:])):
         n = stop - start
-        outs = [shape(*cotangent.shape), shape(rows_tok, n * block)]
-        scratch = [
-            pltpu.VMEM((n, rows_tok, block), jnp.float32),
-            pltpu.VMEM((rows_tok, n * block), bf16),
-        ]
+        half = shape(rows_tok, n * block)
+        scratch = [pltpu.VMEM((n, rows_tok, block), jnp.float32)]
         if k == 0:
             act, h, x_all = call(
                 functools.partial(forward_kernel, len(shards), start, stop),
-                outs + [shape(n_blk + 1, rows_tok, width)],
+                [half, half, shape(n_blk + 1, rows_tok, width)],
                 [SMEM] * 3 + [ANY] * len(shards) + [VMEM, VMEM],
-                [HBM, VMEM, VMEM],
-                scratch + [pltpu.SemaphoreType.DMA((len(shards) + 1,))],
+                [VMEM] * 3,
+                scratch + [pltpu.SemaphoreType.DMA((8,))],
             )(col_tab, col_groups, me, *shards, w_blocks, cotangent)
         else:
             act, h = call(
                 functools.partial(forward_kernel, 0, start, stop),
-                outs,
-                [SMEM] * 3 + [VMEM, VMEM, VMEM, HBM],
+                [shape(*cotangent.shape), half],
+                [SMEM] * 3 + [VMEM] * 4,
                 [HBM, VMEM],
-                scratch + [pltpu.SemaphoreType.DMA((1,))],
-                input_output_aliases={6: 0},
+                scratch
+                + [pltpu.VMEM((rows_tok, n * block), bf16), pltpu.SemaphoreType.DMA((2,))],
             )(col_tab, col_groups, me, x_all, w_blocks, cotangent, act)
         hs.append(h)
 
@@ -374,23 +392,23 @@
     else:
         near, far = [[lax.all_gather(h, "tok", axis=0)] for h in hs], None
 
-    outs = [4, 4] if fast else [n_blk]
-    terms = call(
-        functools.partial(term_kernel, len(hs), fast),
-        [shape(n, rows_tok, width) for n in outs],
-        [SMEM] * 3 + [VMEM] * (len(hs) + 1),
-        [VMEM] * len(outs),
-        [
-            pltpu.VMEM((rows_tok, (cols + 1) * block), bf16),
-            pltpu.VMEM((n_rows, rows_tok, block), jnp.float32),
-        ],
-    )(row_tab, row_groups, me, *hs, w_blocks)
+    def term(outs):
+        return call(
+            functools.partial(term_kernel, len(hs), fast),
+            [shape(n, rows_tok, width) for n in outs],
+            [SMEM] * 3 + [VMEM] * (len(hs) + 1),
+            [VMEM] * len(outs),
+            [
+                pltpu.VMEM((rows_tok, (cols + 1) * block), bf16),
+                pltpu.VMEM((sum(outs) * per, rows_tok, block), jnp.float32),
+            ],
+        )(row_tab, row_groups, me, *hs, w_blocks)
 
     def add(*xs):
         return sum(x.astype(jnp.float32) for x in xs).astype(bf16)
 
     if fast:
-        keep, send = terms
+        keep, send = term([4, 4])
         q = add(keep, blk(send, CORES))
         own, close, mid, last = (q[i] for i in range(4))
         a1 = blk(last, INWARD)
@@ -400,7 +418,8 @@
         o3 = blk(add(mid, b1), ODD)
         input_grad = add(own, e3, o3)
     else:
-        input_grad = lax.psum_scatter(terms[0], "blk", scatter_dimension=0, tiled=True)[0]
+        (terms,) = term([n_blk])
+        input_grad = lax.psum_scatter(terms, "blk", scatter_dimension=0, tiled=True)[0]
 
     n_tokens = n_tok * rows_tok
     split = n_tokens - rows_tok if fast else n_tokens
@@ -412,7 +431,7 @@
         [shape(slots, part, block, dtype=jnp.float32 if fast else bf16), shape(*x_shape)],
         [SMEM] * 4 + [ANY] * len(xq_shards) + [VMEM] * sum(heads),
         [VMEM, VMEM],
-        [pltpu.SemaphoreType.DMA((len(xq_shards),))],
+        [pltpu.SemaphoreType.DMA((8,))],
     )(*tables, *xq_shards, *sum(near, []))
     if fast:
         heads = [len(h) for h in far]

time: 139 us -> 149 us (1.072)
  waiting for transfers between devices: 48.7 us -> 61.8 us
  starting transfers between devices: 37.4 us -> 34.5 us
    ppermute x9 -> x12, waiting for transfers between devices: 11.6 us -> 41.2 us  [tok(): return lax.ppermute(x, 'tok', pairs)]
    ppermute x24 -> x17, waiting for transfers between devices: 37.2 us -> 20.5 us  [blk(): return lax.ppermute(x, 'blk', pairs)]
    ppermute x24 -> x17, starting transfers between devices: 30.1 us -> 21.5 us  [blk(): return lax.ppermute(x, 'blk', pairs)]
    ppermute x9 -> x12, starting transfers between devices: 7.38 us -> 13 us  [tok(): return lax.ppermute(x, 'tok', pairs)]
    pallas_call x5 -> x7, Pallas kernels: 16.8 us -> 16.8 us  [the longest x1 7.96 us: term(): call(functools.partial(term_kernel, len(hs), fast), [shape(n, rows_tok, w...]
  transfers between devices with their start and end apart: 33 -> 29, of which waited for: 16 -> 11; matrix products, arithmetic and copies ran while one was open for 5% -> 6% of each run, Pallas kernels for 10% -> 9%
where the time goes in v2:
time: 149 us; the launch traced here: 148 us
  waiting for transfers between devices  61.8 us (41%)
  starting transfers between devices  34.5 us (23%)
  Pallas kernels  29.7 us (20%)
  local copies, waits for them, and re-layouts  10.9 us (7%)
  other arithmetic  9.15 us (6%)
  between operations  1.67 us (1%)
    ppermute x12, waiting for transfers between devices, tok(): return lax.ppermute(x, 'tok', pairs)  41.2 us
    ppermute x17, starting transfers between devices, blk(): return lax.ppermute(x, 'blk', pairs)  21.5 us
    ppermute x17, waiting for transfers between devices, blk(): return lax.ppermute(x, 'blk', pairs)  20.5 us
    ppermute x12, starting transfers between devices, tok(): return lax.ppermute(x, 'tok', pairs)  13 us
    unnamed x12, local copies, waits for them, and re-layouts  10.8 us
    pallas_call x1, Pallas kernels, term(): call(functools.partial(term_kernel, len(hs), fast), [shape(n, rows_tok, w...  7.96 us
    pallas_call x1, Pallas kernels, on_device(): call(functools.partial(grad_kernel, False, 0, heads, cuts, slice(split, n...  6.23 us
    pallas_call x1, Pallas kernels, on_device(): call(functools.partial(grad_kernel, True, len(xq_shards), heads, cuts, sl...  6.06 us
  transfers between devices with their start and end apart: 29, of which 11 were waited for; matrix products, arithmetic and copies ran while one was open for 6% of the time, Pallas kernels for 9%

profile of v2, /device:TPU:0, one launch (start us, length us, event | category | flops | bytes accessed | tf_op | source)
XLA Modules:
  0.0 147.6 jit_solution(1594587992058097129)
XLA Ops:
  0.6 3.1 %collective-permute-start = (bf16[128,1024]{1,0:T(8,128)(2,1)}, bf16[128,1024]{1,0:T(8,128)(2,1)S(1)}, u32[]{:S(2)}, u32[]{:S(2)}) collective-permute-start(bf16[128,1024]{1,0:T(8,128)(2,1)} %refs_0_.1), channel_id=1, source_target_pairs={{0,2},{1,3},{2,0},{3,1},{4,6},{5,7},{6,4},{7,5},{8,10},{9,11},{10,... | collective-permute-start | bytes 786440 | tf_op jit(solution)/shard_map/ppermute | solution.py:265
  3.8 0.7 collective-permute-start.1
  4.4 0.1 collective-permute-start.5
  5.2 0.7 broadcast_compare_fusion
  5.9 0.8 convert_reduce_fusion.2
  6.7 0.1 convert_reduce_fusion.4
  6.8 1.1 convert_reduce_fusion
  7.9 0.8 convert_reduce_fusion.3
  8.7 0.8 select_reduce_fusion.2
  9.5 0.1 select_reduce_fusion.3
  9.6 0.7 collective-permute-done.refs_1_
  10.3 0.7 collective-permute-start.3
  10.9 0.7 or_add_fusion
  11.6 1.3 collective-permute-start.2
  12.9 0.2 select_reduce_fusion.1
  13.1 1.3 collective-permute-start.4
  14.4 0.1 collective-permute-start.6
  14.5 10.3 %collective-permute-done.2 = bf16[128,1024]{1,0:T(8,128)(2,1)S(1)} collective-permute-done((bf16[128,1024]{1,0:T(8,128)(2,1)S(1)}, bf16[128,1024]{1,0:T(8,128)(2,1)S(1)}, u32[]{:S(2)}, u32[]{:S(2)}) %collective-permute-start.2) | collective-permute-done | bytes 262176 | tf_op jit(solution)/shard_map/ppermute | solution.py:265
  25.0 7.1 %collective-permute-done.4 = bf16[128,1024]{1,0:T(8,128)(2,1)} collective-permute-done((bf16[128,1024]{1,0:T(8,128)(2,1)S(1)}, bf16[128,1024]{1,0:T(8,128)(2,1)}, u32[]{:S(2)}, u32[]{:S(2)}) %collective-permute-start.4) | collective-permute-done | bytes 262176 | tf_op jit(solution)/shard_map/ppermute | solution.py:265
  32.1 1.0 broadcast_select_fusion.refs_1_
  33.1 0.2 select_reduce_fusion
  33.3 1.3 collective-permute-done.8
  34.6 4.6 %copy-done = bf16[384,128,128]{2,1,0:T(8,128)(2,1)S(1)} copy-done((bf16[384,128,128]{2,1,0:T(8,128)(2,1)S(1)}, bf16[384,128,128]{2,1,0:T(8,128)(2,1)}, u32[]{:S(2)}) %copy-start) | copy-done | bytes 12582936
  39.2 0.9 copy-done.4
  40.2 3.9 %shard_map.95 = (bf16[128,2560]{1,0:T(8,128)(2,1)S(1)}, bf16[128,2560]{1,0:T(8,128)(2,1)S(1)}, bf16[9,128,1024]{2,1,0:T(8,128)(2,1)S(1)}) custom-call(s32[504]{0:T(512)S(1)} %broadcast_add_fusion.1.tab, s32[40]{0:T(128)S(1)} %and_select_fusion.1.groups, s32[1]{0:T(128)} %bitcast.1.me, bf16[1,128,1024]{2,1,0:T(8,128)(2,1)S(1)} %bitcast.33, ...), custom_call_target="tpu_custom_call" | custom-call | tf_op jit(solution)/shard_map/pallas_call | solution.py:368
  44.0 0.7 copy-done.1
  44.7 4.4 %shard_map.96 = (bf16[128,5120]{1,0:T(8,128)(2,1)}, bf16[128,2560]{1,0:T(8,128)(2,1)S(1)}) custom-call(s32[504]{0:T(512)S(1)} %broadcast_add_fusion.1.tab, s32[40]{0:T(128)S(1)} %and_select_fusion.1.groups, s32[1]{0:T(128)} %bitcast.1.me, bf16[9,128,1024]{2,1,0:T(8,128)(2,1)S(1)} %get-tuple-element.20.refs_0_, bf16[384,128,128]{2,1,0:T(8,128)(2,1)S(1)} %copy-done.1, ...), custom_call_target="tpu_custom_call" | custom-call | tf_op jit(solution)/shard_map/pallas_call | solution.py:376
  49.2 8.0 %shard_map.97 = (bf16[4,128,1024]{2,1,0:T(8,128)(2,1)S(1)}, bf16[4,128,1024]{2,1,0:T(8,128)(2,1)}) custom-call(s32[576]{0:T(1024)S(1)} %broadcast_add_fusion.tab, s32[64]{0:T(128)S(1)} %and_select_fusion.groups, s32[1]{0:T(128)} %bitcast.1.me, bf16[128,2560]{1,0:T(8,128)(2,1)S(1)} %get-tuple-element.23.refs_0_.refs_4_, ...), custom_call_target="tpu_custom_call" | custom-call | tf_op jit(solution)/shard_map/pallas_call | solution.py:396
  57.1 7.5 %collective-permute-start.9 = (bf16[4,128,1024]{2,1,0:T(8,128)(2,1)}, bf16[4,128,1024]{2,1,0:T(8,128)(2,1)}, u32[]{:S(2)}, u32[]{:S(2)}) collective-permute-start(bf16[4,128,1024]{2,1,0:T(8,128)(2,1)} %get-tuple-element.26), channel_id=1, source_target_pairs={{0,1},{1,0},{2,3},{3,2},{4,5},{5,4},{6,7},{7,6},{8,9},{9,8},{10,11... | collective-permute-start | bytes 3145736 | tf_op jit(solution)/shard_map/ppermute | solution.py:265
  64.7 0.2 shard_map.98
  64.9 1.6 %collective-permute-start.15 = (bf16[16,32,128]{2,1,0:T(8,128)(2,1)S(1)}, bf16[16,32,128]{2,1,0:T(8,128)(2,1)S(1)}, u32[]{:S(2)}, u32[]{:S(2)}) collective-permute-start(bf16[16,32,128]{2,1,0:T(8,128)(2,1)S(1)} %get-tuple-element.28), channel_id=1, source_target_pairs={{0,8},{8,0},{16,24},{24,16},{1,9},{9,1},{17,25},{25,17},{2,10},{10... | collective-permute-start | bytes 393224 | tf_op jit(solution)/shard_map/ppermute | solution.py:269
  66.4 1.5 %collective-permute-start.16 = (bf16[16,32,128]{2,1,0:T(8,128)(2,1)S(1)}, bf16[16,32,128]{2,1,0:T(8,128)(2,1)S(1)}, u32[]{:S(2)}, u32[]{:S(2)}) collective-permute-start(bf16[16,32,128]{2,1,0:T(8,128)(2,1)S(1)} %get-tuple-element.29), channel_id=1, source_target_pairs={{0,16},{8,24},{16,0},{24,8},{1,17},{9,25},{17,1},{25,9},{2,18},{10... | collective-permute-start | bytes 393224 | tf_op jit(solution)/shard_map/ppermute | solution.py:269
  68.0 0.5 collective-permute-start.17
  68.4 2.3 %collective-permute-done.15.refs_1_ = bf16[16,32,128]{2,1,0:T(8,128)(2,1)S(1)} collective-permute-done((bf16[16,32,128]{2,1,0:T(8,128)(2,1)S(1)}, bf16[16,32,128]{2,1,0:T(8,128)(2,1)S(1)}, u32[]{:S(2)}, u32[]{:S(2)}) %collective-permute-start.15) | collective-permute-done | bytes 131104 | tf_op jit(solution)/shard_map/ppermute | solution.py:269
  70.8 3.6 %collective-permute-done.16.refs_2_ = bf16[16,32,128]{2,1,0:T(8,128)(2,1)S(1)} collective-permute-done((bf16[16,32,128]{2,1,0:T(8,128)(2,1)S(1)}, bf16[16,32,128]{2,1,0:T(8,128)(2,1)S(1)}, u32[]{:S(2)}, u32[]{:S(2)}) %collective-permute-start.16) | collective-permute-done | bytes 131104 | tf_op jit(solution)/shard_map/ppermute | solution.py:269
  74.5 0.1 collective-permute-start.21
  74.5 1.6 %collective-permute-start.26 = (bf16[128,2560]{1,0:T(8,128)(2,1)S(1)}, bf16[128,2560]{1,0:T(8,128)(2,1)S(1)}, u32[]{:S(2)}, u32[]{:S(2)}) collective-permute-start(bf16[128,2560]{1,0:T(8,128)(2,1)S(1)} %get-tuple-element.24.refs_1_.refs_7_), channel_id=1, source_target_pairs={{0,16},{8,24},{16,0},{24,8},{1,17},{9,25},{17,1},{25,9},{2,18},{10... | collective-permute-start | bytes 1966088 | tf_op jit(solution)/shard_map/ppermute | solution.py:269
  76.1 1.6 %add_convert_fusion = bf16[4,128,1024]{2,1,0:T(8,128)(2,1)S(1)} fusion(bf16[4,128,1024]{2,1,0:T(8,128)(2,1)} %collective-permute-done.9, bf16[4,128,1024]{2,1,0:T(8,128)(2,1)S(1)} %get-tuple-element.25), kind=kLoop, calls=%fused_computation | loop fusion | flops 2097152 | bytes 3145728 | tf_op jit(solution)/shard_map/convert_element_type | solution.py:408
  77.8 1.3 collective-permute-start.10
  79.1 0.6 collective-permute-start.23
  79.7 0.2 shard_map.100
  79.9 1.6 %collective-permute-start.18 = (bf16[16,32,128]{2,1,0:T(8,128)(2,1)S(1)}, bf16[16,32,128]{2,1,0:T(8,128)(2,1)S(1)}, u32[]{:S(2)}, u32[]{:S(2)}) collective-permute-start(bf16[16,32,128]{2,1,0:T(8,128)(2,1)S(1)} %get-tuple-element.32), channel_id=1, source_target_pairs={{0,8},{8,0},{16,24},{24,16},{1,9},{9,1},{17,25},{25,17},{2,10},{10... | collective-permute-start | bytes 393224 | tf_op jit(solution)/shard_map/ppermute | solution.py:269
  81.5 17.3 %collective-permute-done.18.refs_1_ = bf16[16,32,128]{2,1,0:T(8,128)(2,1)S(1)} collective-permute-done((bf16[16,32,128]{2,1,0:T(8,128)(2,1)S(1)}, bf16[16,32,128]{2,1,0:T(8,128)(2,1)S(1)}, u32[]{:S(2)}, u32[]{:S(2)}) %collective-permute-start.18) | collective-permute-done | bytes 131104 | tf_op jit(solution)/shard_map/ppermute | solution.py:269
  98.8 0.5 collective-permute-start.19
  99.3 1.5 %collective-permute-start.20 = (bf16[16,32,128]{2,1,0:T(8,128)(2,1)S(1)}, bf16[16,32,128]{2,1,0:T(8,128)(2,1)S(1)}, u32[]{:S(2)}, u32[]{:S(2)}) collective-permute-start(bf16[16,32,128]{2,1,0:T(8,128)(2,1)S(1)} %get-tuple-element.34), channel_id=1, source_target_pairs={{0,24},{8,16},{16,8},{24,0},{1,25},{9,17},{17,9},{25,1},{2,26},{10... | collective-permute-start | bytes 393224 | tf_op jit(solution)/shard_map/ppermute | solution.py:269
  100.8 5.4 %collective-permute-done.19.refs_2_ = bf16[16,32,128]{2,1,0:T(8,128)(2,1)S(1)} collective-permute-done((bf16[16,32,128]{2,1,0:T(8,128)(2,1)S(1)}, bf16[16,32,128]{2,1,0:T(8,128)(2,1)S(1)}, u32[]{:S(2)}, u32[]{:S(2)}) %collective-permute-start.19) | collective-permute-done | bytes 131104 | tf_op jit(solution)/shard_map/ppermute | solution.py:269
  106.3 1.3 collective-permute-start.13
  107.6 0.7 collective-permute-start.11
  108.3 0.9 collective-permute-start.25
  109.2 0.1 collective-permute-start.22
  109.3 1.0 collective-permute-start.24
  110.4 1.1 collective-permute-done.13
  111.4 0.8 collective-permute-start.28
  112.2 1.0 collective-permute-start.27
  113.2 0.2 fusion.4
  113.4 2.5 %collective-permute-start.12 = (bf16[128,1024]{1,0:T(8,128)(2,1)S(1)}, bf16[128,1024]{1,0:T(8,128)(2,1)S(1)}, u32[]{:S(2)}, u32[]{:S(2)}) collective-permute-start(bf16[128,1024]{1,0:T(8,128)(2,1)S(1)} %get-tuple-element.39), channel_id=1, source_target_pairs={{0,2},{1,3},{2,0},{3,1},{4,6},{5,7},{6,4},{7,5},{8,10},{9,11},{10,... | collective-permute-start | bytes 786440 | tf_op jit(solution)/shard_map/ppermute | solution.py:265
  116.0 10.0 %collective-permute-done.25.refs_8_ = bf16[128,2560]{1,0:T(8,128)(2,1)S(1)} collective-permute-done((bf16[128,2560]{1,0:T(8,128)(2,1)S(1)}, bf16[128,2560]{1,0:T(8,128)(2,1)S(1)}, u32[]{:S(2)}, u32[]{:S(2)}) %collective-permute-start.25) | collective-permute-done | bytes 655392 | tf_op jit(solution)/shard_map/ppermute | solution.py:269
  125.9 0.7 collective-permute-start.14
  126.6 4.6 %copy-done.2 = bf16[384,128,128]{2,1,0:T(8,128)(2,1)S(1)} copy-done((bf16[384,128,128]{2,1,0:T(8,128)(2,1)S(1)}, bf16[384,128,128]{2,1,0:T(8,128)(2,1)}, u32[]{:S(2)}) %copy-start.2) | copy-done | bytes 12582936
  131.2 0.6 shard_map.94
  131.8 6.1 %shard_map.102 = (f32[384,32,128]{2,1,0:T(8,128)S(1)}, bf16[64,32,512]{2,1,0:T(8,128)(2,1)S(1)}) custom-call(s32[504]{0:T(512)S(1)} %broadcast_add_fusion.1.tab, s32[40]{0:T(128)S(1)} %and_select_fusion.1.groups, s32[1]{0:T(128)} %bitcast.1.me, s32[1]{0:T(128)} %copy.10.count, bf16[16,32,512]{2,1,0:T(8,128)(2,1)S(1)} %shard_map.99.refs_0_, ...), custom_call_target="tpu_custom_call" | custom-call | tf_op jit(solution)/shard_map/pallas_call | solution.py:429
  137.9 2.6 %collective-permute-done.27.refs_2_ = bf16[128,2560]{1,0:T(8,128)(2,1)S(1)} collective-permute-done((bf16[128,2560]{1,0:T(8,128)(2,1)S(1)}, bf16[128,2560]{1,0:T(8,128)(2,1)S(1)}, u32[]{:S(2)}, u32[]{:S(2)}) %collective-permute-start.27) | collective-permute-done | bytes 655392 | tf_op jit(solution)/shard_map/ppermute | solution.py:269
  140.5 6.2 %shard_map.103 = bf16[384,32,128]{2,1,0:T(8,128)(2,1)} custom-call(s32[504]{0:T(512)S(1)} %broadcast_add_fusion.1.tab, s32[40]{0:T(128)S(1)} %and_select_fusion.1.groups, s32[1]{0:T(128)} %bitcast.1.me, s32[1]{0:T(128)} %copy.10.count, bf16[64,32,512]{2,1,0:T(8,128)(2,1)S(1)} %get-tuple-element.35.refs_0_, f32[384,32,128]{2,1,0:T(8,128)S(1)} %get-tuple-element.36.refs_1_, ...), custom_call_target="tpu_custom_call" | custom-call | tf_op jit(solution)/shard_map/pallas_call | solution.py:438
  146.7 0.8 fusion.6
  (39 shorter events, 0.5 us)
Async XLA Ops:
  0.6 34.0 %copy-start.3 = (bf16[128,5120]{1,0:T(8,128)(2,1)S(1)}, bf16[128,5120]{1,0:T(8,128)(2,1)}, u32[]{:S(2)}) copy-start(bf16[128,5120]{1,0:T(8,128)(2,1)} %refs_2_.2) | copy-start | bytes 3932164
  0.6 9.6 %collective-permute-start = (bf16[128,1024]{1,0:T(8,128)(2,1)}, bf16[128,1024]{1,0:T(8,128)(2,1)S(1)}, u32[]{:S(2)}, u32[]{:S(2)}) collective-permute-start(bf16[128,1024]{1,0:T(8,128)(2,1)} %refs_0_.1), channel_id=1, source_target_pairs={{0,2},{1,3},{2,0},{3,1},{4,6},{5,7},{6,4},{7,5},{8,10},{9,11},{10,... | collective-permute-start | bytes 786440 | tf_op jit(solution)/shard_map/ppermute | solution.py:265
  3.8 7.9 %collective-permute-start.1 = (bf16[128,1024]{1,0:T(8,128)(2,1)}, bf16[128,1024]{1,0:T(8,128)(2,1)S(1)}, u32[]{:S(2)}, u32[]{:S(2)}) collective-permute-start(bf16[128,1024]{1,0:T(8,128)(2,1)} %refs_0_.1), channel_id=1, source_target_pairs={{2,4},{3,5},{4,2},{5,3},{10,12},{11,13},{12,10},{13,11},{18,20},{1... | collective-permute-start | bytes 786440 | tf_op jit(solution)/shard_map/ppermute | solution.py:265
  4.4 28.9 %collective-permute-start.5 = (bf16[128,1024]{1,0:T(8,128)(2,1)}, bf16[128,1024]{1,0:T(8,128)(2,1)S(1)}, u32[]{:S(2)}, u32[]{:S(2)}) collective-permute-start(bf16[128,1024]{1,0:T(8,128)(2,1)} %refs_0_.1), channel_id=1, source_target_pairs={{0,1},{1,0},{2,3},{3,2},{4,5},{5,4},{6,7},{7,6},{8,9},{9,8},{10,11... | collective-permute-start | bytes 786440 | tf_op jit(solution)/shard_map/ppermute | solution.py:265
  10.3 2.8 %collective-permute-start.3 = (bf16[128,1024]{1,0:T(8,128)(2,1)S(1)}, bf16[128,1024]{1,0:T(8,128)(2,1)S(1)}, u32[]{:S(2)}, u32[]{:S(2)}) collective-permute-start(bf16[128,1024]{1,0:T(8,128)(2,1)S(1)} %collective-permute-done.refs_1_), channel_id=1, source_target_pairs={{2,4},{3,5},{4,2},{5,3},{10,12},{11,13},{12,10},{13,11},{18,20},{1... | collective-permute-start | bytes 786440 | tf_op jit(solution)/shard_map/ppermute | solution.py:265
  11.6 13.2 %collective-permute-start.2 = (bf16[128,1024]{1,0:T(8,128)(2,1)S(1)}, bf16[128,1024]{1,0:T(8,128)(2,1)S(1)}, u32[]{:S(2)}, u32[]{:S(2)}) collective-permute-start(bf16[128,1024]{1,0:T(8,128)(2,1)S(1)} %collective-permute-done.1), channel_id=1, source_target_pairs={{2,0},{3,1},{4,6},{5,7},{10,8},{11,9},{12,14},{13,15},{18,16},{19,... | collective-permute-start | bytes 786440 | tf_op jit(solution)/shard_map/ppermute | solution.py:265
  13.1 18.9 %collective-permute-start.4 = (bf16[128,1024]{1,0:T(8,128)(2,1)S(1)}, bf16[128,1024]{1,0:T(8,128)(2,1)}, u32[]{:S(2)}, u32[]{:S(2)}) collective-permute-start(bf16[128,1024]{1,0:T(8,128)(2,1)S(1)} %collective-permute-done.3), channel_id=1, source_target_pairs={{2,0},{3,1},{4,6},{5,7},{10,8},{11,9},{12,14},{13,15},{18,16},{19,... | collective-permute-start | bytes 786440 | tf_op jit(solution)/shard_map/ppermute | solution.py:265
  14.4 18.9 %collective-permute-start.6 = (bf16[128,1024]{1,0:T(8,128)(2,1)S(1)}, bf16[128,1024]{1,0:T(8,128)(2,1)S(1)}, u32[]{:S(2)}, u32[]{:S(2)}) collective-permute-start(bf16[128,1024]{1,0:T(8,128)(2,1)S(1)} %collective-permute-done.refs_1_), channel_id=1, source_target_pairs={{0,1},{1,0},{2,3},{3,2},{4,5},{5,4},{6,7},{7,6},{8,9},{9,8},{10,11... | collective-permute-start | bytes 786440 | tf_op jit(solution)/shard_map/ppermute | solution.py:265
  24.9 8.5 %collective-permute-start.7 = (bf16[128,1024]{1,0:T(8,128)(2,1)S(1)}, bf16[128,1024]{1,0:T(8,128)(2,1)S(1)}, u32[]{:S(2)}, u32[]{:S(2)}) collective-permute-start(bf16[128,1024]{1,0:T(8,128)(2,1)S(1)} %broadcast_select_fusion.1.refs_0_), channel_id=1, source_target_pairs={{0,1},{1,0},{2,3},{3,2},{4,5},{5,4},{6,7},{7,6},{8,9},{9,8},{10,11... | collective-permute-start | bytes 786440 | tf_op jit(solution)/shard_map/ppermute | solution.py:265
  33.0 1.6 %collective-permute-start.8 = (bf16[128,1024]{1,0:T(8,128)(2,1)S(1)}, bf16[128,1024]{1,0:T(8,128)(2,1)S(1)}, u32[]{:S(2)}, u32[]{:S(2)}) collective-permute-start(bf16[128,1024]{1,0:T(8,128)(2,1)S(1)} %broadcast_select_fusion.refs_1_), channel_id=1, source_target_pairs={{0,1},{1,0},{2,3},{3,2},{4,5},{5,4},{6,7},{7,6},{8,9},{9,8},{10,11... | collective-permute-start | bytes 786440 | tf_op jit(solution)/shard_map/ppermute | solution.py:265
  34.6 4.6 %copy-start = (bf16[384,128,128]{2,1,0:T(8,128)(2,1)S(1)}, bf16[384,128,128]{2,1,0:T(8,128)(2,1)}, u32[]{:S(2)}) copy-start(bf16[384,128,128]{2,1,0:T(8,128)(2,1)} %refs_2_.3) | copy-start | bytes 37748740
  39.2 0.9 copy-start.4
  40.2 4.6 %copy-start.1 = (bf16[384,128,128]{2,1,0:T(8,128)(2,1)S(1)}, bf16[384,128,128]{2,1,0:T(8,128)(2,1)}, u32[]{:S(2)}) copy-start(bf16[384,128,128]{2,1,0:T(8,128)(2,1)} %refs_2_.3) | copy-start | bytes 37748740
  49.1 15.5 %copy-start.5 = (bf16[128,1024]{1,0:T(8,128)(2,1)S(1)}, bf16[128,1024]{1,0:T(8,128)(2,1)}, u32[]{:S(2)}) copy-start(bf16[128,1024]{1,0:T(8,128)(2,1)} %refs_0_.1) | copy-start | bytes 786436
  57.1 19.0 %collective-permute-start.9 = (bf16[4,128,1024]{2,1,0:T(8,128)(2,1)}, bf16[4,128,1024]{2,1,0:T(8,128)(2,1)}, u32[]{:S(2)}, u32[]{:S(2)}) collective-permute-start(bf16[4,128,1024]{2,1,0:T(8,128)(2,1)} %get-tuple-element.26), channel_id=1, source_target_pairs={{0,1},{1,0},{2,3},{3,2},{4,5},{5,4},{6,7},{7,6},{8,9},{9,8},{10,11... | collective-permute-start | bytes 3145736 | tf_op jit(solution)/shard_map/ppermute | solution.py:265
  64.9 5.9 %collective-permute-start.15 = (bf16[16,32,128]{2,1,0:T(8,128)(2,1)S(1)}, bf16[16,32,128]{2,1,0:T(8,128)(2,1)S(1)}, u32[]{:S(2)}, u32[]{:S(2)}) collective-permute-start(bf16[16,32,128]{2,1,0:T(8,128)(2,1)S(1)} %get-tuple-element.28), channel_id=1, source_target_pairs={{0,8},{8,0},{16,24},{24,16},{1,9},{9,1},{17,25},{25,17},{2,10},{10... | collective-permute-start | bytes 393224 | tf_op jit(solution)/shard_map/ppermute | solution.py:269
  66.4 7.9 %collective-permute-start.16 = (bf16[16,32,128]{2,1,0:T(8,128)(2,1)S(1)}, bf16[16,32,128]{2,1,0:T(8,128)(2,1)S(1)}, u32[]{:S(2)}, u32[]{:S(2)}) collective-permute-start(bf16[16,32,128]{2,1,0:T(8,128)(2,1)S(1)} %get-tuple-element.29), channel_id=1, source_target_pairs={{0,16},{8,24},{16,0},{24,8},{1,17},{9,25},{17,1},{25,9},{2,18},{10... | collective-permute-start | bytes 393224 | tf_op jit(solution)/shard_map/ppermute | solution.py:269
  68.0 6.4 %collective-permute-start.17 = (bf16[16,32,128]{2,1,0:T(8,128)(2,1)S(1)}, bf16[16,32,128]{2,1,0:T(8,128)(2,1)S(1)}, u32[]{:S(2)}, u32[]{:S(2)}) collective-permute-start(bf16[16,32,128]{2,1,0:T(8,128)(2,1)S(1)} %get-tuple-element.30), channel_id=1, source_target_pairs={{0,24},{8,16},{16,8},{24,0},{1,25},{9,17},{17,9},{25,1},{2,26},{10... | collective-permute-start | bytes 393224 | tf_op jit(solution)/shard_map/ppermute | solution.py:269
  74.5 33.8 %collective-permute-start.21 = (bf16[16,32,512]{2,1,0:T(8,128)(2,1)S(1)}, bf16[16,32,512]{2,1,0:T(8,128)(2,1)S(1)}, u32[]{:S(2)}, u32[]{:S(2)}) collective-permute-start(bf16[16,32,512]{2,1,0:T(8,128)(2,1)S(1)} %shard_map.99.refs_0_), channel_id=1, source_target_pairs={{0,1},{1,0},{2,3},{3,2},{4,5},{5,4},{6,7},{7,6},{8,9},{9,8},{10,11... | collective-permute-start | bytes 1572872 | tf_op jit(solution)/shard_map/ppermute | solution.py:265
  74.5 34.7 %collective-permute-start.26 = (bf16[128,2560]{1,0:T(8,128)(2,1)S(1)}, bf16[128,2560]{1,0:T(8,128)(2,1)S(1)}, u32[]{:S(2)}, u32[]{:S(2)}) collective-permute-start(bf16[128,2560]{1,0:T(8,128)(2,1)S(1)} %get-tuple-element.24.refs_1_.refs_7_), channel_id=1, source_target_pairs={{0,16},{8,24},{16,0},{24,8},{1,17},{9,25},{17,1},{25,9},{2,18},{10... | collective-permute-start | bytes 1966088 | tf_op jit(solution)/shard_map/ppermute | solution.py:269
  77.8 21.5 %collective-permute-start.10 = (bf16[128,1024]{1,0:T(8,128)(2,1)S(1)}, bf16[128,1024]{1,0:T(8,128)(2,1)S(1)}, u32[]{:S(2)}, u32[]{:S(2)}) collective-permute-start(bf16[128,1024]{1,0:T(8,128)(2,1)S(1)} %get-tuple-element.41), channel_id=1, source_target_pairs={{0,2},{1,3},{6,4},{7,5},{8,10},{9,11},{14,12},{15,13},{16,18},{17,... | collective-permute-start | bytes 786440 | tf_op jit(solution)/shard_map/ppermute | solution.py:265
  79.1 30.2 %collective-permute-start.23 = (bf16[128,2560]{1,0:T(8,128)(2,1)S(1)}, bf16[128,2560]{1,0:T(8,128)(2,1)S(1)}, u32[]{:S(2)}, u32[]{:S(2)}) collective-permute-start(bf16[128,2560]{1,0:T(8,128)(2,1)S(1)} %get-tuple-element.23.refs_0_.refs_4_), channel_id=1, source_target_pairs={{0,8},{8,0},{16,24},{24,16},{1,9},{9,1},{17,25},{25,17},{2,10},{10... | collective-permute-start | bytes 1966088 | tf_op jit(solution)/shard_map/ppermute | solution.py:269
  79.9 18.8 %collective-permute-start.18 = (bf16[16,32,128]{2,1,0:T(8,128)(2,1)S(1)}, bf16[16,32,128]{2,1,0:T(8,128)(2,1)S(1)}, u32[]{:S(2)}, u32[]{:S(2)}) collective-permute-start(bf16[16,32,128]{2,1,0:T(8,128)(2,1)S(1)} %get-tuple-element.32), channel_id=1, source_target_pairs={{0,8},{8,0},{16,24},{24,16},{1,9},{9,1},{17,25},{25,17},{2,10},{10... | collective-permute-start | bytes 393224 | tf_op jit(solution)/shard_map/ppermute | solution.py:269
  98.8 7.5 %collective-permute-start.19 = (bf16[16,32,128]{2,1,0:T(8,128)(2,1)S(1)}, bf16[16,32,128]{2,1,0:T(8,128)(2,1)S(1)}, u32[]{:S(2)}, u32[]{:S(2)}) collective-permute-start(bf16[16,32,128]{2,1,0:T(8,128)(2,1)S(1)} %get-tuple-element.33), channel_id=1, source_target_pairs={{0,16},{8,24},{16,0},{24,8},{1,17},{9,25},{17,1},{25,9},{2,18},{10... | collective-permute-start | bytes 393224 | tf_op jit(solution)/shard_map/ppermute | solution.py:269
  99.3 8.3 %collective-permute-start.20 = (bf16[16,32,128]{2,1,0:T(8,128)(2,1)S(1)}, bf16[16,32,128]{2,1,0:T(8,128)(2,1)S(1)}, u32[]{:S(2)}, u32[]{:S(2)}) collective-permute-start(bf16[16,32,128]{2,1,0:T(8,128)(2,1)S(1)} %get-tuple-element.34), channel_id=1, source_target_pairs={{0,24},{8,16},{16,8},{24,0},{1,25},{9,17},{17,9},{25,1},{2,26},{10... | collective-permute-start | bytes 393224 | tf_op jit(solution)/shard_map/ppermute | solution.py:269
  106.3 5.2 %collective-permute-start.13 = (bf16[128,1024]{1,0:T(8,128)(2,1)S(1)}, bf16[128,1024]{1,0:T(8,128)(2,1)S(1)}, u32[]{:S(2)}, u32[]{:S(2)}) collective-permute-start(bf16[128,1024]{1,0:T(8,128)(2,1)S(1)} %get-tuple-element.42), channel_id=1, source_target_pairs={{0,2},{1,3},{6,4},{7,5},{8,10},{9,11},{14,12},{15,13},{16,18},{17,... | collective-permute-start | bytes 786440 | tf_op jit(solution)/shard_map/ppermute | solution.py:265
  107.6 4.7 %collective-permute-start.11 = (bf16[128,1024]{1,0:T(8,128)(2,1)S(1)}, bf16[128,1024]{1,0:T(8,128)(2,1)S(1)}, u32[]{:S(2)}, u32[]{:S(2)}) collective-permute-start(bf16[128,1024]{1,0:T(8,128)(2,1)S(1)} %add_convert_fusion.2), channel_id=1, source_target_pairs={{2,4},{3,5},{4,2},{5,3},{10,12},{11,13},{12,10},{13,11},{18,20},{1... | collective-permute-start | bytes 786440 | tf_op jit(solution)/shard_map/ppermute | solution.py:265
  108.3 17.7 %collective-permute-start.25 = (bf16[128,2560]{1,0:T(8,128)(2,1)S(1)}, bf16[128,2560]{1,0:T(8,128)(2,1)S(1)}, u32[]{:S(2)}, u32[]{:S(2)}) collective-permute-start(bf16[128,2560]{1,0:T(8,128)(2,1)S(1)} %get-tuple-element.24.refs_1_.refs_7_), channel_id=1, source_target_pairs={{0,8},{8,0},{16,24},{24,16},{1,9},{9,1},{17,25},{25,17},{2,10},{10... | collective-permute-start | bytes 1966088 | tf_op jit(solution)/shard_map/ppermute | solution.py:269
  109.2 4.2 %collective-permute-start.22 = (bf16[16,32,512]{2,1,0:T(8,128)(2,1)S(1)}, bf16[16,32,512]{2,1,0:T(8,128)(2,1)S(1)}, u32[]{:S(2)}, u32[]{:S(2)}) collective-permute-start(bf16[16,32,512]{2,1,0:T(8,128)(2,1)S(1)} %shard_map.101.refs_1_), channel_id=1, source_target_pairs={{0,1},{1,0},{2,3},{3,2},{4,5},{5,4},{6,7},{7,6},{8,9},{9,8},{10,11... | collective-permute-start | bytes 1572872 | tf_op jit(solution)/shard_map/ppermute | solution.py:265
  109.3 22.5 %collective-permute-start.24 = (bf16[128,2560]{1,0:T(8,128)(2,1)S(1)}, bf16[128,2560]{1,0:T(8,128)(2,1)S(1)}, u32[]{:S(2)}, u32[]{:S(2)}) collective-permute-start(bf16[128,2560]{1,0:T(8,128)(2,1)S(1)} %get-tuple-element.23.refs_0_.refs_4_), channel_id=1, source_target_pairs={{0,16},{8,24},{16,0},{24,8},{1,17},{9,25},{17,1},{25,9},{2,18},{10... | collective-permute-start | bytes 1966088 | tf_op jit(solution)/shard_map/ppermute | solution.py:269
  111.4 26.5 %collective-permute-start.28 = (bf16[128,2560]{1,0:T(8,128)(2,1)S(1)}, bf16[128,2560]{1,0:T(8,128)(2,1)S(1)}, u32[]{:S(2)}, u32[]{:S(2)}) collective-permute-start(bf16[128,2560]{1,0:T(8,128)(2,1)S(1)} %collective-permute-done.26.refs_9_), channel_id=1, source_target_pairs={{0,8},{8,0},{16,24},{24,16},{1,9},{9,1},{17,25},{25,17},{2,10},{10... | collective-permute-start | bytes 1966088 | tf_op jit(solution)/shard_map/ppermute | solution.py:269
  112.2 28.3 %collective-permute-start.27 = (bf16[128,2560]{1,0:T(8,128)(2,1)S(1)}, bf16[128,2560]{1,0:T(8,128)(2,1)S(1)}, u32[]{:S(2)}, u32[]{:S(2)}) collective-permute-start(bf16[128,2560]{1,0:T(8,128)(2,1)S(1)} %collective-permute-done.23.refs_5_), channel_id=1, source_target_pairs={{0,16},{8,24},{16,0},{24,8},{1,17},{9,25},{17,1},{25,9},{2,18},{10... | collective-permute-start | bytes 1966088 | tf_op jit(solution)/shard_map/ppermute | solution.py:269
  113.4 33.3 %collective-permute-start.12 = (bf16[128,1024]{1,0:T(8,128)(2,1)S(1)}, bf16[128,1024]{1,0:T(8,128)(2,1)S(1)}, u32[]{:S(2)}, u32[]{:S(2)}) collective-permute-start(bf16[128,1024]{1,0:T(8,128)(2,1)S(1)} %get-tuple-element.39), channel_id=1, source_target_pairs={{0,2},{1,3},{2,0},{3,1},{4,6},{5,7},{6,4},{7,5},{8,10},{9,11},{10,... | collective-permute-start | bytes 786440 | tf_op jit(solution)/shard_map/ppermute | solution.py:265
  125.9 20.8 %collective-permute-start.14 = (bf16[128,1024]{1,0:T(8,128)(2,1)S(1)}, bf16[128,1024]{1,0:T(8,128)(2,1)S(1)}, u32[]{:S(2)}, u32[]{:S(2)}) collective-permute-start(bf16[128,1024]{1,0:T(8,128)(2,1)S(1)} %get-tuple-element.40), channel_id=1, source_target_pairs={{2,4},{3,5},{4,2},{5,3},{10,12},{11,13},{12,10},{13,11},{18,20},{1... | collective-permute-start | bytes 786440 | tf_op jit(solution)/shard_map/ppermute | solution.py:265
  126.6 4.6 %copy-start.2 = (bf16[384,128,128]{2,1,0:T(8,128)(2,1)S(1)}, bf16[384,128,128]{2,1,0:T(8,128)(2,1)}, u32[]{:S(2)}) copy-start(bf16[384,128,128]{2,1,0:T(8,128)(2,1)} %refs_2_.3) | copy-start | bytes 37748740

commit v3 on v2

--- a/solution.py
+++ b/solution.py
@@ -9,6 +9,7 @@
 
 
 GROUP = 4
+UNROLL = (16, 4, 1)
 LIMIT = 16 * 1024 * 1024
 VMEM = pl.BlockSpec(memory_space=pltpu.VMEM)
 SMEM = pl.BlockSpec(memory_space=pltpu.SMEM)
@@ -40,21 +41,17 @@
     )
 
 
-def each(lo, hi, body, unroll):
-    n = hi - lo
-    main = n // unroll
-
-    def many(i, carry):
-        for u in range(unroll):
-            body(lo + i * unroll + u)
-        return carry
-
-    def one(i, carry):
-        body(i)
-        return carry
-
-    lax.fori_loop(0, main, many, 0)
-    lax.fori_loop(lo + main * unroll, hi, one, 0)
+def each(lo, hi, body):
+    for unroll in UNROLL:
+        n = (hi - lo) // unroll
+
+        def many(i, carry, lo=lo, unroll=unroll):
+            for u in range(unroll):
+                body(lo + i * unroll + u)
+            return carry
+
+        lax.fori_loop(0, n, many, 0)
+        lo = lo + n * unroll
 
 
 def unpack(tab, g):
@@ -127,7 +124,7 @@
         w = jnp.concatenate([w_ref[jnp.minimum(s, slots - 1)] for s in ids], axis=0)
         acc[col - start] += jnp.dot(x, w, preferred_element_type=jnp.float32)
 
-    each(lo, hi, group, 4)
+    each(lo, hi, group)
     for c in range(stop - start):
         at = slice(c * block, (c + 1) * block)
         hidden = acc[c]
@@ -167,7 +164,7 @@
             h, w, (((1,), (1,)), ((), ())), preferred_element_type=jnp.float32
         )
 
-    each(0, total(groups, 0, groups.shape[0]), group, 4)
+    each(0, total(groups, 0, groups.shape[0]), group)
     panels = panels_of(me[0], 8) if fast else list(range(outs[0].shape[0]))
     for ref in outs:
         for i in range(ref.shape[0]):
@@ -220,7 +217,7 @@
             for i, s in enumerate(ids):
                 out_ref[s] = out[i * part : (i + 1) * part]
 
-        each(lo, hi, group, 4)
+        each(lo, hi, group)
         lo = hi
 
 
@@ -355,7 +352,9 @@
         xq = xq.transpose(1, 2, 0, 3).reshape(per, part, n_tok * rows_tok)
         xq_shards = [lax.all_gather(xq, "blk", axis=0, tiled=True)]
 
-    call(warm_kernel, shape(8, block), [HBM], VMEM, [pltpu.SemaphoreType.DMA], side=True)(w_blocks)
+    call(
+        warm_kernel, shape(8, block), [HBM], VMEM, [pltpu.SemaphoreType.DMA], side=True
+    )(pltpu.with_memory_space_constraint(w_blocks, pltpu.HBM))
 
     cuts = (0, cols // 2, cols)
     hs = []
@@ -387,7 +386,7 @@
         (a, b) = hs
         ax, ay = tok(a, TOK_X), tok(a, TOK_Y)
         bx, by = tok(b, TOK_X), tok(b, TOK_Y)
-        ad, bd = tok(ax, TOK_Y), tok(by, TOK_X)
+        ad, bd = tok(ay, TOK_X), tok(bx, TOK_Y)
         near, far = [[a, ax, ay], [b, bx, by]], [[ad], [bd]]
     else:
         near, far = [[lax.all_gather(h, "tok", axis=0)] for h in hs], None

time: 149 us -> 138 us (0.926)
  Pallas kernels: 29.7 us -> 24.8 us
  local copies, waits for them, and re-layouts: 10.9 us -> 6.7 us
  starting transfers between devices: 34.5 us -> 33 us
    unnamed x12 -> x10, local copies, waits for them, and re-layouts: 10.8 us -> 6.66 us
    ppermute x17, starting transfers between devices: 21.5 us -> 18.3 us  [blk(): return lax.ppermute(x, 'blk', pairs)]
    pallas_call x1, Pallas kernels: 7.96 us -> 6.09 us  [term(): call(functools.partial(term_kernel, len(hs), fast), [shape(n, rows_tok, w...]
    ppermute x12, starting transfers between devices: 13 us -> 14.7 us  [tok(): return lax.ppermute(x, 'tok', pairs)]
  transfers between devices with their start and end apart: 29 -> 29, of which waited for: 11 -> 12; matrix products, arithmetic and copies ran while one was open for 6% -> 6% of each run, Pallas kernels for 9% -> 8%
where the time goes in v3:
time: 138 us; the launch traced here: 137 us
  waiting for transfers between devices  62 us (45%)
  starting transfers between devices  33 us (24%)
  Pallas kernels  24.8 us (18%)
  other arithmetic  9.14 us (7%)
  local copies, waits for them, and re-layouts  6.7 us (5%)
  between operations  1.65 us (1%)
    ppermute x12, waiting for transfers between devices, tok(): return lax.ppermute(x, 'tok', pairs)  41.8 us
    ppermute x17, waiting for transfers between devices, blk(): return lax.ppermute(x, 'blk', pairs)  20.2 us
    ppermute x17, starting transfers between devices, blk(): return lax.ppermute(x, 'blk', pairs)  18.3 us
    ppermute x12, starting transfers between devices, tok(): return lax.ppermute(x, 'tok', pairs)  14.7 us
    unnamed x10, local copies, waits for them, and re-layouts  6.66 us
    pallas_call x1, Pallas kernels, term(): call(functools.partial(term_kernel, len(hs), fast), [shape(n, rows_tok, w...  6.09 us
    pallas_call x1, Pallas kernels, on_device(): call(functools.partial(grad_kernel, False, 0, heads, cuts, slice(split, n...  5.13 us
    pallas_call x1, Pallas kernels, on_device(): call(functools.partial(grad_kernel, True, len(xq_shards), heads, cuts, sl...  4.67 us
  transfers between devices with their start and end apart: 29, of which 12 were waited for; matrix products, arithmetic and copies ran while one was open for 6% of the time, Pallas kernels for 8%

profile of v3, /device:TPU:0, one launch (start us, length us, event | category | flops | bytes accessed | tf_op | source)
XLA Modules:
  0.0 137.3 jit_solution(956676243841857548)
XLA Ops:
  0.6 3.1 %collective-permute-start = (bf16[128,1024]{1,0:T(8,128)(2,1)}, bf16[128,1024]{1,0:T(8,128)(2,1)S(1)}, u32[]{:S(2)}, u32[]{:S(2)}) collective-permute-start(bf16[128,1024]{1,0:T(8,128)(2,1)} %refs_0_.1), channel_id=1, source_target_pairs={{0,2},{1,3},{2,0},{3,1},{4,6},{5,7},{6,4},{7,5},{8,10},{9,11},{10,... | collective-permute-start | bytes 786440 | tf_op jit(solution)/shard_map/ppermute | solution.py:262
  3.8 0.7 collective-permute-start.1
  4.4 0.1 collective-permute-start.5
  5.2 0.7 broadcast_compare_fusion
  5.9 0.8 convert_reduce_fusion.2
  6.7 0.1 convert_reduce_fusion.4
  6.8 1.1 convert_reduce_fusion
  7.9 0.8 convert_reduce_fusion.3
  8.7 0.8 select_reduce_fusion.2
  9.5 0.1 select_reduce_fusion.3
  9.6 0.7 collective-permute-done.refs_1_
  10.3 0.7 collective-permute-start.3
  10.9 0.7 or_add_fusion
  11.6 1.3 collective-permute-start.2
  12.9 0.2 select_reduce_fusion.1
  13.1 1.3 collective-permute-start.4
  14.4 0.1 collective-permute-start.6
  14.5 10.3 %collective-permute-done.2 = bf16[128,1024]{1,0:T(8,128)(2,1)S(1)} collective-permute-done((bf16[128,1024]{1,0:T(8,128)(2,1)S(1)}, bf16[128,1024]{1,0:T(8,128)(2,1)S(1)}, u32[]{:S(2)}, u32[]{:S(2)}) %collective-permute-start.2) | collective-permute-done | bytes 262176 | tf_op jit(solution)/shard_map/ppermute | solution.py:262
  24.9 0.1 collective-permute-start.7
  25.0 7.1 %collective-permute-done.4 = bf16[128,1024]{1,0:T(8,128)(2,1)} collective-permute-done((bf16[128,1024]{1,0:T(8,128)(2,1)S(1)}, bf16[128,1024]{1,0:T(8,128)(2,1)}, u32[]{:S(2)}, u32[]{:S(2)}) %collective-permute-start.4) | collective-permute-done | bytes 262176 | tf_op jit(solution)/shard_map/ppermute | solution.py:262
  32.1 1.0 broadcast_select_fusion.refs_1_
  33.0 0.1 collective-permute-start.8
  33.1 0.2 select_reduce_fusion
  33.3 1.3 collective-permute-done.8
  34.6 4.6 %copy-done = bf16[384,128,128]{2,1,0:T(8,128)(2,1)S(1)} copy-done((bf16[384,128,128]{2,1,0:T(8,128)(2,1)S(1)}, bf16[384,128,128]{2,1,0:T(8,128)(2,1)}, u32[]{:S(2)}) %copy-start) | copy-done | bytes 12582936
  39.2 0.9 copy-done.3
  40.2 3.4 %shard_map.95 = (bf16[128,2560]{1,0:T(8,128)(2,1)S(1)}, bf16[128,2560]{1,0:T(8,128)(2,1)S(1)}, bf16[9,128,1024]{2,1,0:T(8,128)(2,1)S(1)}) custom-call(s32[504]{0:T(512)S(1)} %broadcast_add_fusion.1.tab, s32[40]{0:T(128)S(1)} %and_select_fusion.1.groups, s32[1]{0:T(128)} %bitcast.1.me, bf16[1,128,1024]{2,1,0:T(8,128)(2,1)S(1)} %bitcast.33, ...), custom_call_target="tpu_custom_call" | custom-call | tf_op jit(solution)/shard_map/pallas_call | solution.py:367
  43.6 1.1 copy-done.1
  44.7 3.6 %shard_map.96 = (bf16[128,5120]{1,0:T(8,128)(2,1)}, bf16[128,2560]{1,0:T(8,128)(2,1)S(1)}) custom-call(s32[504]{0:T(512)S(1)} %broadcast_add_fusion.1.tab, s32[40]{0:T(128)S(1)} %and_select_fusion.1.groups, s32[1]{0:T(128)} %bitcast.1.me, bf16[9,128,1024]{2,1,0:T(8,128)(2,1)S(1)} %get-tuple-element.20.refs_0_, bf16[384,128,128]{2,1,0:T(8,128)(2,1)S(1)} %copy-done.1, ...), custom_call_target="tpu_custom_call" | custom-call | tf_op jit(solution)/shard_map/pallas_call | solution.py:375
  48.4 6.1 %shard_map.97 = (bf16[4,128,1024]{2,1,0:T(8,128)(2,1)S(1)}, bf16[4,128,1024]{2,1,0:T(8,128)(2,1)}) custom-call(s32[576]{0:T(1024)S(1)} %broadcast_add_fusion.tab, s32[64]{0:T(128)S(1)} %and_select_fusion.groups, s32[1]{0:T(128)} %bitcast.1.me, bf16[128,2560]{1,0:T(8,128)(2,1)S(1)} %get-tuple-element.23.refs_0_.refs_4_, ...), custom_call_target="tpu_custom_call" | custom-call | tf_op jit(solution)/shard_map/pallas_call | solution.py:395
  54.4 4.4 %collective-permute-start.9 = (bf16[4,128,1024]{2,1,0:T(8,128)(2,1)}, bf16[4,128,1024]{2,1,0:T(8,128)(2,1)}, u32[]{:S(2)}, u32[]{:S(2)}) collective-permute-start(bf16[4,128,1024]{2,1,0:T(8,128)(2,1)} %get-tuple-element.26), channel_id=1, source_target_pairs={{0,1},{1,0},{2,3},{3,2},{4,5},{5,4},{6,7},{7,6},{8,9},{9,8},{10,11... | collective-permute-start | bytes 3145736 | tf_op jit(solution)/shard_map/ppermute | solution.py:262
  58.8 0.2 shard_map.98
  59.1 1.6 %collective-permute-start.15 = (bf16[16,32,128]{2,1,0:T(8,128)(2,1)S(1)}, bf16[16,32,128]{2,1,0:T(8,128)(2,1)S(1)}, u32[]{:S(2)}, u32[]{:S(2)}) collective-permute-start(bf16[16,32,128]{2,1,0:T(8,128)(2,1)S(1)} %get-tuple-element.28), channel_id=1, source_target_pairs={{0,8},{8,0},{16,24},{24,16},{1,9},{9,1},{17,25},{25,17},{2,10},{10... | collective-permute-start | bytes 393224 | tf_op jit(solution)/shard_map/ppermute | solution.py:266
  60.6 1.5 %collective-permute-start.16 = (bf16[16,32,128]{2,1,0:T(8,128)(2,1)S(1)}, bf16[16,32,128]{2,1,0:T(8,128)(2,1)S(1)}, u32[]{:S(2)}, u32[]{:S(2)}) collective-permute-start(bf16[16,32,128]{2,1,0:T(8,128)(2,1)S(1)} %get-tuple-element.29), channel_id=1, source_target_pairs={{0,16},{8,24},{16,0},{24,8},{1,17},{9,25},{17,1},{25,9},{2,18},{10... | collective-permute-start | bytes 393224 | tf_op jit(solution)/shard_map/ppermute | solution.py:266
  62.1 0.5 collective-permute-start.17
  62.6 2.3 %collective-permute-done.15.refs_1_ = bf16[16,32,128]{2,1,0:T(8,128)(2,1)S(1)} collective-permute-done((bf16[16,32,128]{2,1,0:T(8,128)(2,1)S(1)}, bf16[16,32,128]{2,1,0:T(8,128)(2,1)S(1)}, u32[]{:S(2)}, u32[]{:S(2)}) %collective-permute-start.15) | collective-permute-done | bytes 131104 | tf_op jit(solution)/shard_map/ppermute | solution.py:266
  64.9 3.6 %collective-permute-done.16.refs_2_ = bf16[16,32,128]{2,1,0:T(8,128)(2,1)S(1)} collective-permute-done((bf16[16,32,128]{2,1,0:T(8,128)(2,1)S(1)}, bf16[16,32,128]{2,1,0:T(8,128)(2,1)S(1)}, u32[]{:S(2)}, u32[]{:S(2)}) %collective-permute-start.16) | collective-permute-done | bytes 131104 | tf_op jit(solution)/shard_map/ppermute | solution.py:266
  68.6 0.1 collective-permute-start.21
  68.7 1.3 collective-permute-start.25
  70.0 1.6 %add_convert_fusion = bf16[4,128,1024]{2,1,0:T(8,128)(2,1)S(1)} fusion(bf16[4,128,1024]{2,1,0:T(8,128)(2,1)} %collective-permute-done.9, bf16[4,128,1024]{2,1,0:T(8,128)(2,1)S(1)} %get-tuple-element.25), kind=kLoop, calls=%fused_computation | loop fusion | flops 2097152 | bytes 3145728 | tf_op jit(solution)/shard_map/convert_element_type | solution.py:407
  71.7 1.3 collective-permute-start.10
  73.0 0.9 collective-permute-start.24
  73.9 0.2 shard_map.100
  74.1 1.6 %collective-permute-start.18 = (bf16[16,32,128]{2,1,0:T(8,128)(2,1)S(1)}, bf16[16,32,128]{2,1,0:T(8,128)(2,1)S(1)}, u32[]{:S(2)}, u32[]{:S(2)}) collective-permute-start(bf16[16,32,128]{2,1,0:T(8,128)(2,1)S(1)} %get-tuple-element.32), channel_id=1, source_target_pairs={{0,8},{8,0},{16,24},{24,16},{1,9},{9,1},{17,25},{25,17},{2,10},{10... | collective-permute-start | bytes 393224 | tf_op jit(solution)/shard_map/ppermute | solution.py:266
  75.7 13.0 %collective-permute-done.18.refs_1_ = bf16[16,32,128]{2,1,0:T(8,128)(2,1)S(1)} collective-permute-done((bf16[16,32,128]{2,1,0:T(8,128)(2,1)S(1)}, bf16[16,32,128]{2,1,0:T(8,128)(2,1)S(1)}, u32[]{:S(2)}, u32[]{:S(2)}) %collective-permute-start.18) | collective-permute-done | bytes 131104 | tf_op jit(solution)/shard_map/ppermute | solution.py:266
  88.6 1.5 %collective-permute-start.19 = (bf16[16,32,128]{2,1,0:T(8,128)(2,1)S(1)}, bf16[16,32,128]{2,1,0:T(8,128)(2,1)S(1)}, u32[]{:S(2)}, u32[]{:S(2)}) collective-permute-start(bf16[16,32,128]{2,1,0:T(8,128)(2,1)S(1)} %get-tuple-element.33), channel_id=1, source_target_pairs={{0,16},{8,24},{16,0},{24,8},{1,17},{9,25},{17,1},{25,9},{2,18},{10... | collective-permute-start | bytes 393224 | tf_op jit(solution)/shard_map/ppermute | solution.py:266
  90.2 1.2 collective-permute-start.20
  91.4 5.0 %collective-permute-done.19.refs_2_ = bf16[16,32,128]{2,1,0:T(8,128)(2,1)S(1)} collective-permute-done((bf16[16,32,128]{2,1,0:T(8,128)(2,1)S(1)}, bf16[16,32,128]{2,1,0:T(8,128)(2,1)S(1)}, u32[]{:S(2)}, u32[]{:S(2)}) %collective-permute-start.19) | collective-permute-done | bytes 131104 | tf_op jit(solution)/shard_map/ppermute | solution.py:266
  96.4 1.3 collective-permute-start.13
  97.7 0.7 collective-permute-start.11
  98.4 1.6 %collective-permute-start.26 = (bf16[128,2560]{1,0:T(8,128)(2,1)S(1)}, bf16[128,2560]{1,0:T(8,128)(2,1)S(1)}, u32[]{:S(2)}, u32[]{:S(2)}) collective-permute-start(bf16[128,2560]{1,0:T(8,128)(2,1)S(1)} %get-tuple-element.24.refs_1_.refs_7_), channel_id=1, source_target_pairs={{0,16},{8,24},{16,0},{24,8},{1,17},{9,25},{17,1},{25,9},{2,18},{10... | collective-permute-start | bytes 1966088 | tf_op jit(solution)/shard_map/ppermute | solution.py:266
  100.2 0.6 collective-permute-start.23
  100.8 0.8 collective-permute-done.13
  101.6 2.5 %collective-permute-start.28 = (bf16[128,2560]{1,0:T(8,128)(2,1)S(1)}, bf16[128,2560]{1,0:T(8,128)(2,1)S(1)}, u32[]{:S(2)}, u32[]{:S(2)}) collective-permute-start(bf16[128,2560]{1,0:T(8,128)(2,1)S(1)} %collective-permute-done.25.refs_8_), channel_id=1, source_target_pairs={{0,16},{8,24},{16,0},{24,8},{1,17},{9,25},{17,1},{25,9},{2,18},{10... | collective-permute-start | bytes 1966088 | tf_op jit(solution)/shard_map/ppermute | solution.py:266
  104.1 0.2 fusion.4
  104.3 2.5 %collective-permute-start.12 = (bf16[128,1024]{1,0:T(8,128)(2,1)S(1)}, bf16[128,1024]{1,0:T(8,128)(2,1)S(1)}, u32[]{:S(2)}, u32[]{:S(2)}) collective-permute-start(bf16[128,1024]{1,0:T(8,128)(2,1)S(1)} %get-tuple-element.39), channel_id=1, source_target_pairs={{0,2},{1,3},{2,0},{3,1},{4,6},{5,7},{6,4},{7,5},{8,10},{9,11},{10,... | collective-permute-start | bytes 786440 | tf_op jit(solution)/shard_map/ppermute | solution.py:262
  106.9 9.2 %collective-permute-done.26.refs_9_ = bf16[128,2560]{1,0:T(8,128)(2,1)S(1)} collective-permute-done((bf16[128,2560]{1,0:T(8,128)(2,1)S(1)}, bf16[128,2560]{1,0:T(8,128)(2,1)S(1)}, u32[]{:S(2)}, u32[]{:S(2)}) %collective-permute-start.26) | collective-permute-done | bytes 655392 | tf_op jit(solution)/shard_map/ppermute | solution.py:266
  116.1 0.7 collective-permute-start.14
  116.8 1.3 shard_map.94
  118.1 4.7 %shard_map.102 = (f32[384,32,128]{2,1,0:T(8,128)S(1)}, bf16[64,32,512]{2,1,0:T(8,128)(2,1)S(1)}) custom-call(s32[504]{0:T(512)S(1)} %broadcast_add_fusion.1.tab, s32[40]{0:T(128)S(1)} %and_select_fusion.1.groups, s32[1]{0:T(128)} %bitcast.1.me, s32[1]{0:T(128)} %copy.10.count, bf16[16,32,512]{2,1,0:T(8,128)(2,1)S(1)} %shard_map.99.refs_0_, ...), custom_call_target="tpu_custom_call" | custom-call | tf_op jit(solution)/shard_map/pallas_call | solution.py:428
  122.7 5.1 %collective-permute-done.28.refs_3_ = bf16[128,2560]{1,0:T(8,128)(2,1)S(1)} collective-permute-done((bf16[128,2560]{1,0:T(8,128)(2,1)S(1)}, bf16[128,2560]{1,0:T(8,128)(2,1)S(1)}, u32[]{:S(2)}, u32[]{:S(2)}) %collective-permute-start.28) | collective-permute-done | bytes 655392 | tf_op jit(solution)/shard_map/ppermute | solution.py:266
  127.9 3.5 %collective-permute-done.27.refs_2_ = bf16[128,2560]{1,0:T(8,128)(2,1)S(1)} collective-permute-done((bf16[128,2560]{1,0:T(8,128)(2,1)S(1)}, bf16[128,2560]{1,0:T(8,128)(2,1)S(1)}, u32[]{:S(2)}, u32[]{:S(2)}) %collective-permute-start.27) | collective-permute-done | bytes 655392 | tf_op jit(solution)/shard_map/ppermute | solution.py:266
  131.4 5.1 %shard_map.103 = bf16[384,32,128]{2,1,0:T(8,128)(2,1)} custom-call(s32[504]{0:T(512)S(1)} %broadcast_add_fusion.1.tab, s32[40]{0:T(128)S(1)} %and_select_fusion.1.groups, s32[1]{0:T(128)} %bitcast.1.me, s32[1]{0:T(128)} %copy.10.count, bf16[64,32,512]{2,1,0:T(8,128)(2,1)S(1)} %get-tuple-element.35.refs_0_, f32[384,32,128]{2,1,0:T(8,128)S(1)} %get-tuple-element.36.refs_1_, ...), custom_call_target="tpu_custom_call" | custom-call | tf_op jit(solution)/shard_map/pallas_call | solution.py:437
  136.5 0.8 fusion.6
  (37 shorter events, 0.4 us)
Async XLA Ops:
  0.6 34.0 %copy-start.2 = (bf16[128,5120]{1,0:T(8,128)(2,1)S(1)}, bf16[128,5120]{1,0:T(8,128)(2,1)}, u32[]{:S(2)}) copy-start(bf16[128,5120]{1,0:T(8,128)(2,1)} %refs_2_.2) | copy-start | bytes 3932164
  0.6 9.6 %collective-permute-start = (bf16[128,1024]{1,0:T(8,128)(2,1)}, bf16[128,1024]{1,0:T(8,128)(2,1)S(1)}, u32[]{:S(2)}, u32[]{:S(2)}) collective-permute-start(bf16[128,1024]{1,0:T(8,128)(2,1)} %refs_0_.1), channel_id=1, source_target_pairs={{0,2},{1,3},{2,0},{3,1},{4,6},{5,7},{6,4},{7,5},{8,10},{9,11},{10,... | collective-permute-start | bytes 786440 | tf_op jit(solution)/shard_map/ppermute | solution.py:262
  3.8 7.9 %collective-permute-start.1 = (bf16[128,1024]{1,0:T(8,128)(2,1)}, bf16[128,1024]{1,0:T(8,128)(2,1)S(1)}, u32[]{:S(2)}, u32[]{:S(2)}) collective-permute-start(bf16[128,1024]{1,0:T(8,128)(2,1)} %refs_0_.1), channel_id=1, source_target_pairs={{2,4},{3,5},{4,2},{5,3},{10,12},{11,13},{12,10},{13,11},{18,20},{1... | collective-permute-start | bytes 786440 | tf_op jit(solution)/shard_map/ppermute | solution.py:262
  4.4 28.9 %collective-permute-start.5 = (bf16[128,1024]{1,0:T(8,128)(2,1)}, bf16[128,1024]{1,0:T(8,128)(2,1)S(1)}, u32[]{:S(2)}, u32[]{:S(2)}) collective-permute-start(bf16[128,1024]{1,0:T(8,128)(2,1)} %refs_0_.1), channel_id=1, source_target_pairs={{0,1},{1,0},{2,3},{3,2},{4,5},{5,4},{6,7},{7,6},{8,9},{9,8},{10,11... | collective-permute-start | bytes 786440 | tf_op jit(solution)/shard_map/ppermute | solution.py:262
  10.3 2.8 %collective-permute-start.3 = (bf16[128,1024]{1,0:T(8,128)(2,1)S(1)}, bf16[128,1024]{1,0:T(8,128)(2,1)S(1)}, u32[]{:S(2)}, u32[]{:S(2)}) collective-permute-start(bf16[128,1024]{1,0:T(8,128)(2,1)S(1)} %collective-permute-done.refs_1_), channel_id=1, source_target_pairs={{2,4},{3,5},{4,2},{5,3},{10,12},{11,13},{12,10},{13,11},{18,20},{1... | collective-permute-start | bytes 786440 | tf_op jit(solution)/shard_map/ppermute | solution.py:262
  11.6 13.2 %collective-permute-start.2 = (bf16[128,1024]{1,0:T(8,128)(2,1)S(1)}, bf16[128,1024]{1,0:T(8,128)(2,1)S(1)}, u32[]{:S(2)}, u32[]{:S(2)}) collective-permute-start(bf16[128,1024]{1,0:T(8,128)(2,1)S(1)} %collective-permute-done.1), channel_id=1, source_target_pairs={{2,0},{3,1},{4,6},{5,7},{10,8},{11,9},{12,14},{13,15},{18,16},{19,... | collective-permute-start | bytes 786440 | tf_op jit(solution)/shard_map/ppermute | solution.py:262
  13.1 18.9 %collective-permute-start.4 = (bf16[128,1024]{1,0:T(8,128)(2,1)S(1)}, bf16[128,1024]{1,0:T(8,128)(2,1)}, u32[]{:S(2)}, u32[]{:S(2)}) collective-permute-start(bf16[128,1024]{1,0:T(8,128)(2,1)S(1)} %collective-permute-done.3), channel_id=1, source_target_pairs={{2,0},{3,1},{4,6},{5,7},{10,8},{11,9},{12,14},{13,15},{18,16},{19,... | collective-permute-start | bytes 786440 | tf_op jit(solution)/shard_map/ppermute | solution.py:262
  14.4 18.9 %collective-permute-start.6 = (bf16[128,1024]{1,0:T(8,128)(2,1)S(1)}, bf16[128,1024]{1,0:T(8,128)(2,1)S(1)}, u32[]{:S(2)}, u32[]{:S(2)}) collective-permute-start(bf16[128,1024]{1,0:T(8,128)(2,1)S(1)} %collective-permute-done.refs_1_), channel_id=1, source_target_pairs={{0,1},{1,0},{2,3},{3,2},{4,5},{5,4},{6,7},{7,6},{8,9},{9,8},{10,11... | collective-permute-start | bytes 786440 | tf_op jit(solution)/shard_map/ppermute | solution.py:262
  24.9 8.5 %collective-permute-start.7 = (bf16[128,1024]{1,0:T(8,128)(2,1)S(1)}, bf16[128,1024]{1,0:T(8,128)(2,1)S(1)}, u32[]{:S(2)}, u32[]{:S(2)}) collective-permute-start(bf16[128,1024]{1,0:T(8,128)(2,1)S(1)} %broadcast_select_fusion.1.refs_0_), channel_id=1, source_target_pairs={{0,1},{1,0},{2,3},{3,2},{4,5},{5,4},{6,7},{7,6},{8,9},{9,8},{10,11... | collective-permute-start | bytes 786440 | tf_op jit(solution)/shard_map/ppermute | solution.py:262
  33.0 1.6 %collective-permute-start.8 = (bf16[128,1024]{1,0:T(8,128)(2,1)S(1)}, bf16[128,1024]{1,0:T(8,128)(2,1)S(1)}, u32[]{:S(2)}, u32[]{:S(2)}) collective-permute-start(bf16[128,1024]{1,0:T(8,128)(2,1)S(1)} %broadcast_select_fusion.refs_1_), channel_id=1, source_target_pairs={{0,1},{1,0},{2,3},{3,2},{4,5},{5,4},{6,7},{7,6},{8,9},{9,8},{10,11... | collective-permute-start | bytes 786440 | tf_op jit(solution)/shard_map/ppermute | solution.py:262
  34.6 4.6 %copy-start = (bf16[384,128,128]{2,1,0:T(8,128)(2,1)S(1)}, bf16[384,128,128]{2,1,0:T(8,128)(2,1)}, u32[]{:S(2)}) copy-start(bf16[384,128,128]{2,1,0:T(8,128)(2,1)} %refs_2_.3) | copy-start | bytes 37748740
  39.2 0.9 copy-start.3
  40.2 4.6 %copy-start.1 = (bf16[384,128,128]{2,1,0:T(8,128)(2,1)S(1)}, bf16[384,128,128]{2,1,0:T(8,128)(2,1)}, u32[]{:S(2)}) copy-start(bf16[384,128,128]{2,1,0:T(8,128)(2,1)} %refs_2_.3) | copy-start | bytes 37748740
  48.3 10.5 %copy-start.4 = (bf16[128,1024]{1,0:T(8,128)(2,1)S(1)}, bf16[128,1024]{1,0:T(8,128)(2,1)}, u32[]{:S(2)}) copy-start(bf16[128,1024]{1,0:T(8,128)(2,1)} %refs_0_.1) | copy-start | bytes 786436
  54.4 15.6 %collective-permute-start.9 = (bf16[4,128,1024]{2,1,0:T(8,128)(2,1)}, bf16[4,128,1024]{2,1,0:T(8,128)(2,1)}, u32[]{:S(2)}, u32[]{:S(2)}) collective-permute-start(bf16[4,128,1024]{2,1,0:T(8,128)(2,1)} %get-tuple-element.26), channel_id=1, source_target_pairs={{0,1},{1,0},{2,3},{3,2},{4,5},{5,4},{6,7},{7,6},{8,9},{9,8},{10,11... | collective-permute-start | bytes 3145736 | tf_op jit(solution)/shard_map/ppermute | solution.py:262
  59.1 5.9 %collective-permute-start.15 = (bf16[16,32,128]{2,1,0:T(8,128)(2,1)S(1)}, bf16[16,32,128]{2,1,0:T(8,128)(2,1)S(1)}, u32[]{:S(2)}, u32[]{:S(2)}) collective-permute-start(bf16[16,32,128]{2,1,0:T(8,128)(2,1)S(1)} %get-tuple-element.28), channel_id=1, source_target_pairs={{0,8},{8,0},{16,24},{24,16},{1,9},{9,1},{17,25},{25,17},{2,10},{10... | collective-permute-start | bytes 393224 | tf_op jit(solution)/shard_map/ppermute | solution.py:266
  60.6 7.9 %collective-permute-start.16 = (bf16[16,32,128]{2,1,0:T(8,128)(2,1)S(1)}, bf16[16,32,128]{2,1,0:T(8,128)(2,1)S(1)}, u32[]{:S(2)}, u32[]{:S(2)}) collective-permute-start(bf16[16,32,128]{2,1,0:T(8,128)(2,1)S(1)} %get-tuple-element.29), channel_id=1, source_target_pairs={{0,16},{8,24},{16,0},{24,8},{1,17},{9,25},{17,1},{25,9},{2,18},{10... | collective-permute-start | bytes 393224 | tf_op jit(solution)/shard_map/ppermute | solution.py:266
  62.1 6.4 %collective-permute-start.17 = (bf16[16,32,128]{2,1,0:T(8,128)(2,1)S(1)}, bf16[16,32,128]{2,1,0:T(8,128)(2,1)S(1)}, u32[]{:S(2)}, u32[]{:S(2)}) collective-permute-start(bf16[16,32,128]{2,1,0:T(8,128)(2,1)S(1)} %get-tuple-element.30), channel_id=1, source_target_pairs={{0,24},{8,16},{16,8},{24,0},{1,25},{9,17},{17,9},{25,1},{2,26},{10... | collective-permute-start | bytes 393224 | tf_op jit(solution)/shard_map/ppermute | solution.py:266
  68.6 29.8 %collective-permute-start.21 = (bf16[16,32,512]{2,1,0:T(8,128)(2,1)S(1)}, bf16[16,32,512]{2,1,0:T(8,128)(2,1)S(1)}, u32[]{:S(2)}, u32[]{:S(2)}) collective-permute-start(bf16[16,32,512]{2,1,0:T(8,128)(2,1)S(1)} %shard_map.99.refs_0_), channel_id=1, source_target_pairs={{0,1},{1,0},{2,3},{3,2},{4,5},{5,4},{6,7},{7,6},{8,9},{9,8},{10,11... | collective-permute-start | bytes 1572872 | tf_op jit(solution)/shard_map/ppermute | solution.py:262
  68.7 31.4 %collective-permute-start.25 = (bf16[128,2560]{1,0:T(8,128)(2,1)S(1)}, bf16[128,2560]{1,0:T(8,128)(2,1)S(1)}, u32[]{:S(2)}, u32[]{:S(2)}) collective-permute-start(bf16[128,2560]{1,0:T(8,128)(2,1)S(1)} %get-tuple-element.24.refs_1_.refs_7_), channel_id=1, source_target_pairs={{0,8},{8,0},{16,24},{24,16},{1,9},{9,1},{17,25},{25,17},{2,10},{10... | collective-permute-start | bytes 1966088 | tf_op jit(solution)/shard_map/ppermute | solution.py:266
  71.7 18.5 %collective-permute-start.10 = (bf16[128,1024]{1,0:T(8,128)(2,1)S(1)}, bf16[128,1024]{1,0:T(8,128)(2,1)S(1)}, u32[]{:S(2)}, u32[]{:S(2)}) collective-permute-start(bf16[128,1024]{1,0:T(8,128)(2,1)S(1)} %get-tuple-element.41), channel_id=1, source_target_pairs={{0,2},{1,3},{6,4},{7,5},{8,10},{9,11},{14,12},{15,13},{16,18},{17,... | collective-permute-start | bytes 786440 | tf_op jit(solution)/shard_map/ppermute | solution.py:262
  73.0 27.2 %collective-permute-start.24 = (bf16[128,2560]{1,0:T(8,128)(2,1)S(1)}, bf16[128,2560]{1,0:T(8,128)(2,1)S(1)}, u32[]{:S(2)}, u32[]{:S(2)}) collective-permute-start(bf16[128,2560]{1,0:T(8,128)(2,1)S(1)} %get-tuple-element.23.refs_0_.refs_4_), channel_id=1, source_target_pairs={{0,16},{8,24},{16,0},{24,8},{1,17},{9,25},{17,1},{25,9},{2,18},{10... | collective-permute-start | bytes 1966088 | tf_op jit(solution)/shard_map/ppermute | solution.py:266
  74.1 14.5 %collective-permute-start.18 = (bf16[16,32,128]{2,1,0:T(8,128)(2,1)S(1)}, bf16[16,32,128]{2,1,0:T(8,128)(2,1)S(1)}, u32[]{:S(2)}, u32[]{:S(2)}) collective-permute-start(bf16[16,32,128]{2,1,0:T(8,128)(2,1)S(1)} %get-tuple-element.32), channel_id=1, source_target_pairs={{0,8},{8,0},{16,24},{24,16},{1,9},{9,1},{17,25},{25,17},{2,10},{10... | collective-permute-start | bytes 393224 | tf_op jit(solution)/shard_map/ppermute | solution.py:266
  88.6 7.8 %collective-permute-start.19 = (bf16[16,32,128]{2,1,0:T(8,128)(2,1)S(1)}, bf16[16,32,128]{2,1,0:T(8,128)(2,1)S(1)}, u32[]{:S(2)}, u32[]{:S(2)}) collective-permute-start(bf16[16,32,128]{2,1,0:T(8,128)(2,1)S(1)} %get-tuple-element.33), channel_id=1, source_target_pairs={{0,16},{8,24},{16,0},{24,8},{1,17},{9,25},{17,1},{25,9},{2,18},{10... | collective-permute-start | bytes 393224 | tf_op jit(solution)/shard_map/ppermute | solution.py:266
  90.2 7.6 %collective-permute-start.20 = (bf16[16,32,128]{2,1,0:T(8,128)(2,1)S(1)}, bf16[16,32,128]{2,1,0:T(8,128)(2,1)S(1)}, u32[]{:S(2)}, u32[]{:S(2)}) collective-permute-start(bf16[16,32,128]{2,1,0:T(8,128)(2,1)S(1)} %get-tuple-element.34), channel_id=1, source_target_pairs={{0,24},{8,16},{16,8},{24,0},{1,25},{9,17},{17,9},{25,1},{2,26},{10... | collective-permute-start | bytes 393224 | tf_op jit(solution)/shard_map/ppermute | solution.py:266
  96.4 5.2 %collective-permute-start.13 = (bf16[128,1024]{1,0:T(8,128)(2,1)S(1)}, bf16[128,1024]{1,0:T(8,128)(2,1)S(1)}, u32[]{:S(2)}, u32[]{:S(2)}) collective-permute-start(bf16[128,1024]{1,0:T(8,128)(2,1)S(1)} %get-tuple-element.42), channel_id=1, source_target_pairs={{0,2},{1,3},{6,4},{7,5},{8,10},{9,11},{14,12},{15,13},{16,18},{17,... | collective-permute-start | bytes 786440 | tf_op jit(solution)/shard_map/ppermute | solution.py:262
  97.7 6.4 %collective-permute-start.11 = (bf16[128,1024]{1,0:T(8,128)(2,1)S(1)}, bf16[128,1024]{1,0:T(8,128)(2,1)S(1)}, u32[]{:S(2)}, u32[]{:S(2)}) collective-permute-start(bf16[128,1024]{1,0:T(8,128)(2,1)S(1)} %add_convert_fusion.2), channel_id=1, source_target_pairs={{2,4},{3,5},{4,2},{5,3},{10,12},{11,13},{12,10},{13,11},{18,20},{1... | collective-permute-start | bytes 786440 | tf_op jit(solution)/shard_map/ppermute | solution.py:262
  98.4 17.7 %collective-permute-start.26 = (bf16[128,2560]{1,0:T(8,128)(2,1)S(1)}, bf16[128,2560]{1,0:T(8,128)(2,1)S(1)}, u32[]{:S(2)}, u32[]{:S(2)}) collective-permute-start(bf16[128,2560]{1,0:T(8,128)(2,1)S(1)} %get-tuple-element.24.refs_1_.refs_7_), channel_id=1, source_target_pairs={{0,16},{8,24},{16,0},{24,8},{1,17},{9,25},{17,1},{25,9},{2,18},{10... | collective-permute-start | bytes 1966088 | tf_op jit(solution)/shard_map/ppermute | solution.py:266
  100.1 4.2 %collective-permute-start.22 = (bf16[16,32,512]{2,1,0:T(8,128)(2,1)S(1)}, bf16[16,32,512]{2,1,0:T(8,128)(2,1)S(1)}, u32[]{:S(2)}, u32[]{:S(2)}) collective-permute-start(bf16[16,32,512]{2,1,0:T(8,128)(2,1)S(1)} %shard_map.101.refs_1_), channel_id=1, source_target_pairs={{0,1},{1,0},{2,3},{3,2},{4,5},{5,4},{6,7},{7,6},{8,9},{9,8},{10,11... | collective-permute-start | bytes 1572872 | tf_op jit(solution)/shard_map/ppermute | solution.py:262
  100.2 17.9 %collective-permute-start.23 = (bf16[128,2560]{1,0:T(8,128)(2,1)S(1)}, bf16[128,2560]{1,0:T(8,128)(2,1)S(1)}, u32[]{:S(2)}, u32[]{:S(2)}) collective-permute-start(bf16[128,2560]{1,0:T(8,128)(2,1)S(1)} %get-tuple-element.23.refs_0_.refs_4_), channel_id=1, source_target_pairs={{0,8},{8,0},{16,24},{24,16},{1,9},{9,1},{17,25},{25,17},{2,10},{10... | collective-permute-start | bytes 1966088 | tf_op jit(solution)/shard_map/ppermute | solution.py:266
  101.6 26.3 %collective-permute-start.28 = (bf16[128,2560]{1,0:T(8,128)(2,1)S(1)}, bf16[128,2560]{1,0:T(8,128)(2,1)S(1)}, u32[]{:S(2)}, u32[]{:S(2)}) collective-permute-start(bf16[128,2560]{1,0:T(8,128)(2,1)S(1)} %collective-permute-done.25.refs_8_), channel_id=1, source_target_pairs={{0,16},{8,24},{16,0},{24,8},{1,17},{9,25},{17,1},{25,9},{2,18},{10... | collective-permute-start | bytes 1966088 | tf_op jit(solution)/shard_map/ppermute | solution.py:266
  104.1 27.2 %collective-permute-start.27 = (bf16[128,2560]{1,0:T(8,128)(2,1)S(1)}, bf16[128,2560]{1,0:T(8,128)(2,1)S(1)}, u32[]{:S(2)}, u32[]{:S(2)}) collective-permute-start(bf16[128,2560]{1,0:T(8,128)(2,1)S(1)} %collective-permute-done.24.refs_6_), channel_id=1, source_target_pairs={{0,8},{8,0},{16,24},{24,16},{1,9},{9,1},{17,25},{25,17},{2,10},{10... | collective-permute-start | bytes 1966088 | tf_op jit(solution)/shard_map/ppermute | solution.py:266
  104.3 32.2 %collective-permute-start.12 = (bf16[128,1024]{1,0:T(8,128)(2,1)S(1)}, bf16[128,1024]{1,0:T(8,128)(2,1)S(1)}, u32[]{:S(2)}, u32[]{:S(2)}) collective-permute-start(bf16[128,1024]{1,0:T(8,128)(2,1)S(1)} %get-tuple-element.39), channel_id=1, source_target_pairs={{0,2},{1,3},{2,0},{3,1},{4,6},{5,7},{6,4},{7,5},{8,10},{9,11},{10,... | collective-permute-start | bytes 786440 | tf_op jit(solution)/shard_map/ppermute | solution.py:262
  116.1 20.4 %collective-permute-start.14 = (bf16[128,1024]{1,0:T(8,128)(2,1)S(1)}, bf16[128,1024]{1,0:T(8,128)(2,1)S(1)}, u32[]{:S(2)}, u32[]{:S(2)}) collective-permute-start(bf16[128,1024]{1,0:T(8,128)(2,1)S(1)} %get-tuple-element.40), channel_id=1, source_target_pairs={{2,4},{3,5},{4,2},{5,3},{10,12},{11,13},{12,10},{13,11},{18,20},{1... | collective-permute-start | bytes 786440 | tf_op jit(solution)/shard_map/ppermute | solution.py:262

commit v4 on v3

--- a/solution.py
+++ b/solution.py
@@ -187,11 +187,10 @@
         copies = copy_shards(x_in, x_ref, me[0], per, sems)
     slots, part, block = out_ref.shape
 
-    def clear(s, carry):
+    def clear(s):
         out_ref[s] = jnp.zeros((part, block), out_ref.dtype)
-        return carry
-
-    lax.fori_loop(jnp.minimum(count[0], slots), slots, clear, 0)
+
+    each(jnp.minimum(count[0], slots), slots, clear)
     for copy in copies:
         copy.wait()
     lo = jnp.int32(0)
@@ -319,9 +318,7 @@
     local = jnp.sum((mine & (all_cols < blk_col[:, None])).astype(jnp.int32), axis=1)
     live = jnp.arange(slots, dtype=jnp.int32) < blk_count[0]
     col_rank, col_groups = group_ranks(local, live, cols)
-    row_rank, row_groups = group_ranks(blk_row, live, n_rows)
     col_tab = group_table(local, blk_row, live, col_rank, col_groups, n_rows)
-    row_tab = group_table(blk_row, local, live, row_rank, row_groups, cols)
 
     def quarter(parts):
         n = len(parts) * per
@@ -391,6 +388,10 @@
     else:
         near, far = [[lax.all_gather(h, "tok", axis=0)] for h in hs], None
 
+    rows_late, hs[0] = lax.optimization_barrier((blk_row, hs[0]))
+    row_rank, row_groups = group_ranks(rows_late, live, n_rows)
+    row_tab = group_table(rows_late, local, live, row_rank, row_groups, cols)
+
     def term(outs):
         return call(
             functools.partial(term_kernel, len(hs), fast),

time: 138 us -> 134 us (0.971)
  other arithmetic: 9.14 us -> 7.18 us
  starting transfers between devices: 33 us -> 34.7 us
  Pallas kernels: 24.8 us -> 23.2 us
  waiting for transfers between devices: 62 us -> 60.4 us
    ppermute x17, starting transfers between devices: 18.3 us -> 20.3 us  [blk(): return lax.ppermute(x, 'blk', pairs)]
    ppermute x17, waiting for transfers between devices: 20.2 us -> 18.3 us  [blk(): return lax.ppermute(x, 'blk', pairs)]
    unnamed x10 -> x12, local copies, waits for them, and re-layouts: 6.66 us -> 5.99 us
  transfers between devices with their start and end apart: 29 -> 29, of which waited for: 12 -> 12; matrix products, arithmetic and copies ran while one was open for 6% -> 4% of each run, Pallas kernels for 8% -> 8%
where the time goes in v4:
time: 134 us; the launch traced here: 133 us
  waiting for transfers between devices  60.4 us (45%)
  starting transfers between devices  34.7 us (26%)
  Pallas kernels  23.2 us (17%)
  other arithmetic  7.18 us (5%)
  local copies, waits for them, and re-layouts  6.03 us (4%)
  between operations  1.62 us (1%)
    ppermute x12, waiting for transfers between devices, tok(): return lax.ppermute(x, 'tok', pairs)  42.1 us
    ppermute x17, starting transfers between devices, blk(): return lax.ppermute(x, 'blk', pairs)  20.3 us
    ppermute x17, waiting for transfers between devices, blk(): return lax.ppermute(x, 'blk', pairs)  18.3 us
    ppermute x12, starting transfers between devices, tok(): return lax.ppermute(x, 'tok', pairs)  14.4 us
    pallas_call x1, Pallas kernels, term(): call(functools.partial(term_kernel, len(hs), fast), [shape(n, rows_tok, w...  6.09 us
    unnamed x12, local copies, waits for them, and re-layouts  5.99 us
    pallas_call x1, Pallas kernels, on_device(): call(functools.partial(grad_kernel, False, 0, heads, cuts, slice(split, n...  4.33 us
    pallas_call x1, Pallas kernels, on_device(): call(functools.partial(grad_kernel, True, len(xq_shards), heads, cuts, sl...  3.86 us
  transfers between devices with their start and end apart: 29, of which 12 were waited for; matrix products, arithmetic and copies ran while one was open for 4% of the time, Pallas kernels for 8%

profile of v4, /device:TPU:0, one launch (start us, length us, event | category | flops | bytes accessed | tf_op | source)
XLA Modules:
  0.0 133.1 jit_solution(11487636269805072103)
XLA Ops:
  0.6 3.1 %collective-permute-start = (bf16[128,1024]{1,0:T(8,128)(2,1)}, bf16[128,1024]{1,0:T(8,128)(2,1)S(1)}, u32[]{:S(2)}, u32[]{:S(2)}) collective-permute-start(bf16[128,1024]{1,0:T(8,128)(2,1)} %refs_0_.1), channel_id=1, source_target_pairs={{0,2},{1,3},{2,0},{3,1},{4,6},{5,7},{6,4},{7,5},{8,10},{9,11},{10,... | collective-permute-start | bytes 786440 | tf_op jit(solution)/shard_map/ppermute | solution.py:261
  3.8 0.7 collective-permute-start.1
  4.4 0.1 collective-permute-start.5
  5.2 0.7 broadcast_compare_fusion
  5.9 0.8 convert_reduce_fusion.2
  6.7 0.1 convert_reduce_fusion.4
  6.8 3.5 %collective-permute-done.refs_1_ = bf16[128,1024]{1,0:T(8,128)(2,1)S(1)} collective-permute-done((bf16[128,1024]{1,0:T(8,128)(2,1)}, bf16[128,1024]{1,0:T(8,128)(2,1)S(1)}, u32[]{:S(2)}, u32[]{:S(2)}) %collective-permute-start) | collective-permute-done | bytes 262176 | tf_op jit(solution)/shard_map/ppermute | solution.py:261
  10.3 0.7 collective-permute-start.3
  11.0 0.2 convert_reduce_fusion.1
  11.2 1.3 collective-permute-start.2
  12.5 0.1 select_reduce_fusion.3
  12.6 1.3 collective-permute-start.4
  13.9 0.7 or_add_fusion.1
  14.6 7.7 %collective-permute-done.2 = bf16[128,1024]{1,0:T(8,128)(2,1)} collective-permute-done((bf16[128,1024]{1,0:T(8,128)(2,1)S(1)}, bf16[128,1024]{1,0:T(8,128)(2,1)}, u32[]{:S(2)}, u32[]{:S(2)}) %collective-permute-start.2) | collective-permute-done | bytes 262176 | tf_op jit(solution)/shard_map/ppermute | solution.py:261
  22.3 1.0 broadcast_select_fusion.1.refs_0_
  23.3 0.1 collective-permute-start.7
  23.4 5.0 %collective-permute-done.4 = bf16[128,1024]{1,0:T(8,128)(2,1)S(1)} collective-permute-done((bf16[128,1024]{1,0:T(8,128)(2,1)S(1)}, bf16[128,1024]{1,0:T(8,128)(2,1)S(1)}, u32[]{:S(2)}, u32[]{:S(2)}) %collective-permute-start.4) | collective-permute-done | bytes 262176 | tf_op jit(solution)/shard_map/ppermute | solution.py:261
  28.4 0.1 collective-permute-start.8
  28.4 0.2 select_reduce_fusion.1
  28.6 1.3 collective-permute-done.8
  30.0 4.6 %copy-done = bf16[384,128,128]{2,1,0:T(8,128)(2,1)S(1)} copy-done((bf16[384,128,128]{2,1,0:T(8,128)(2,1)S(1)}, bf16[384,128,128]{2,1,0:T(8,128)(2,1)}, u32[]{:S(2)}) %copy-start) | copy-done | bytes 12582936
  34.5 0.9 copy-done.3
  35.5 3.4 %shard_map.95 = (bf16[128,2560]{1,0:T(8,128)(2,1)S(1)}, bf16[128,2560]{1,0:T(8,128)(2,1)S(1)}, bf16[9,128,1024]{2,1,0:T(8,128)(2,1)S(1)}) custom-call(s32[504]{0:T(512)S(1)} %broadcast_add_fusion.1.tab, s32[40]{0:T(128)S(1)} %and_select_fusion.1.groups, s32[1]{0:T(128)} %bitcast.1.me, bf16[1,128,1024]{2,1,0:T(8,128)(2,1)S(1)} %bitcast.34, ...), custom_call_target="tpu_custom_call" | custom-call | tf_op jit(solution)/shard_map/pallas_call | solution.py:364
  39.0 0.1 convert_reduce_fusion.3
  39.1 0.2 convert_reduce_fusion
  39.3 0.1 select_reduce_fusion.2
  39.4 0.2 select_reduce_fusion
  39.6 0.5 copy-done.1
  40.1 3.6 %shard_map.96 = (bf16[128,5120]{1,0:T(8,128)(2,1)}, bf16[128,2560]{1,0:T(8,128)(2,1)S(1)}) custom-call(s32[504]{0:T(512)S(1)} %broadcast_add_fusion.1.tab, s32[40]{0:T(128)S(1)} %and_select_fusion.1.groups, s32[1]{0:T(128)} %bitcast.1.me, bf16[9,128,1024]{2,1,0:T(8,128)(2,1)S(1)} %get-tuple-element.22.refs_0_, bf16[384,128,128]{2,1,0:T(8,128)(2,1)S(1)} %copy-done.1, ...), custom_call_target="tpu_custom_call" | custom-call | tf_op jit(solution)/shard_map/pallas_call | solution.py:372
  43.7 6.1 %shard_map.97 = (bf16[4,128,1024]{2,1,0:T(8,128)(2,1)S(1)}, bf16[4,128,1024]{2,1,0:T(8,128)(2,1)}) custom-call(s32[576]{0:T(1024)S(1)} %broadcast_add_fusion.tab, s32[64]{0:T(128)S(1)} %and_select_fusion.groups, s32[1]{0:T(128)} %bitcast.1.me, bf16[128,2560]{1,0:T(8,128)(2,1)S(1)} %get-tuple-element.27.refs_0_.refs_4_, ...), custom_call_target="tpu_custom_call" | custom-call | tf_op jit(solution)/shard_map/pallas_call | solution.py:396
  49.8 5.0 %collective-permute-start.9 = (bf16[4,128,1024]{2,1,0:T(8,128)(2,1)}, bf16[4,128,1024]{2,1,0:T(8,128)(2,1)}, u32[]{:S(2)}, u32[]{:S(2)}) collective-permute-start(bf16[4,128,1024]{2,1,0:T(8,128)(2,1)} %get-tuple-element.30), channel_id=1, source_target_pairs={{0,1},{1,0},{2,3},{3,2},{4,5},{5,4},{6,7},{7,6},{8,9},{9,8},{10,11... | collective-permute-start | bytes 3145736 | tf_op jit(solution)/shard_map/ppermute | solution.py:261
  54.8 0.2 shard_map.98
  55.1 1.6 %collective-permute-start.15 = (bf16[16,32,128]{2,1,0:T(8,128)(2,1)S(1)}, bf16[16,32,128]{2,1,0:T(8,128)(2,1)S(1)}, u32[]{:S(2)}, u32[]{:S(2)}) collective-permute-start(bf16[16,32,128]{2,1,0:T(8,128)(2,1)S(1)} %get-tuple-element.32), channel_id=1, source_target_pairs={{0,8},{8,0},{16,24},{24,16},{1,9},{9,1},{17,25},{25,17},{2,10},{10... | collective-permute-start | bytes 393224 | tf_op jit(solution)/shard_map/ppermute | solution.py:265
  56.6 1.5 %collective-permute-start.16 = (bf16[16,32,128]{2,1,0:T(8,128)(2,1)S(1)}, bf16[16,32,128]{2,1,0:T(8,128)(2,1)S(1)}, u32[]{:S(2)}, u32[]{:S(2)}) collective-permute-start(bf16[16,32,128]{2,1,0:T(8,128)(2,1)S(1)} %get-tuple-element.33), channel_id=1, source_target_pairs={{0,16},{8,24},{16,0},{24,8},{1,17},{9,25},{17,1},{25,9},{2,18},{10... | collective-permute-start | bytes 393224 | tf_op jit(solution)/shard_map/ppermute | solution.py:265
  58.1 0.5 collective-permute-start.17
  58.6 2.3 %collective-permute-done.15.refs_1_ = bf16[16,32,128]{2,1,0:T(8,128)(2,1)S(1)} collective-permute-done((bf16[16,32,128]{2,1,0:T(8,128)(2,1)S(1)}, bf16[16,32,128]{2,1,0:T(8,128)(2,1)S(1)}, u32[]{:S(2)}, u32[]{:S(2)}) %collective-permute-start.15) | collective-permute-done | bytes 131104 | tf_op jit(solution)/shard_map/ppermute | solution.py:265
  60.9 3.6 %collective-permute-done.16.refs_2_ = bf16[16,32,128]{2,1,0:T(8,128)(2,1)S(1)} collective-permute-done((bf16[16,32,128]{2,1,0:T(8,128)(2,1)S(1)}, bf16[16,32,128]{2,1,0:T(8,128)(2,1)S(1)}, u32[]{:S(2)}, u32[]{:S(2)}) %collective-permute-start.16) | collective-permute-done | bytes 131104 | tf_op jit(solution)/shard_map/ppermute | solution.py:265
  64.7 1.3 collective-permute-start.25
  66.0 1.6 %add_convert_fusion = bf16[4,128,1024]{2,1,0:T(8,128)(2,1)S(1)} fusion(bf16[4,128,1024]{2,1,0:T(8,128)(2,1)} %collective-permute-done.9, bf16[4,128,1024]{2,1,0:T(8,128)(2,1)S(1)} %get-tuple-element.29), kind=kLoop, calls=%fused_computation | loop fusion | flops 2097152 | bytes 3145728 | tf_op jit(solution)/shard_map/convert_element_type | solution.py:408
  67.7 1.8 %collective-permute-start.10 = (bf16[128,1024]{1,0:T(8,128)(2,1)S(1)}, bf16[128,1024]{1,0:T(8,128)(2,1)S(1)}, u32[]{:S(2)}, u32[]{:S(2)}) collective-permute-start(bf16[128,1024]{1,0:T(8,128)(2,1)S(1)} %get-tuple-element.43), channel_id=1, source_target_pairs={{0,2},{1,3},{6,4},{7,5},{8,10},{9,11},{14,12},{15,13},{16,18},{17,... | collective-permute-start | bytes 786440 | tf_op jit(solution)/shard_map/ppermute | solution.py:261
  69.5 0.9 collective-permute-start.24
  70.4 0.2 shard_map.100
  70.6 1.6 %collective-permute-start.18 = (bf16[16,32,128]{2,1,0:T(8,128)(2,1)S(1)}, bf16[16,32,128]{2,1,0:T(8,128)(2,1)S(1)}, u32[]{:S(2)}, u32[]{:S(2)}) collective-permute-start(bf16[16,32,128]{2,1,0:T(8,128)(2,1)S(1)} %get-tuple-element.36), channel_id=1, source_target_pairs={{0,8},{8,0},{16,24},{24,16},{1,9},{9,1},{17,25},{25,17},{2,10},{10... | collective-permute-start | bytes 393224 | tf_op jit(solution)/shard_map/ppermute | solution.py:265
  72.2 12.4 %collective-permute-done.18.refs_1_ = bf16[16,32,128]{2,1,0:T(8,128)(2,1)S(1)} collective-permute-done((bf16[16,32,128]{2,1,0:T(8,128)(2,1)S(1)}, bf16[16,32,128]{2,1,0:T(8,128)(2,1)S(1)}, u32[]{:S(2)}, u32[]{:S(2)}) %collective-permute-start.18) | collective-permute-done | bytes 131104 | tf_op jit(solution)/shard_map/ppermute | solution.py:265
  84.7 1.5 %collective-permute-start.19 = (bf16[16,32,128]{2,1,0:T(8,128)(2,1)S(1)}, bf16[16,32,128]{2,1,0:T(8,128)(2,1)S(1)}, u32[]{:S(2)}, u32[]{:S(2)}) collective-permute-start(bf16[16,32,128]{2,1,0:T(8,128)(2,1)S(1)} %get-tuple-element.37), channel_id=1, source_target_pairs={{0,16},{8,24},{16,0},{24,8},{1,17},{9,25},{17,1},{25,9},{2,18},{10... | collective-permute-start | bytes 393224 | tf_op jit(solution)/shard_map/ppermute | solution.py:265
  86.2 1.2 collective-permute-start.20
  87.4 5.0 %collective-permute-done.19.refs_2_ = bf16[16,32,128]{2,1,0:T(8,128)(2,1)S(1)} collective-permute-done((bf16[16,32,128]{2,1,0:T(8,128)(2,1)S(1)}, bf16[16,32,128]{2,1,0:T(8,128)(2,1)S(1)}, u32[]{:S(2)}, u32[]{:S(2)}) %collective-permute-start.19) | collective-permute-done | bytes 131104 | tf_op jit(solution)/shard_map/ppermute | solution.py:265
  92.4 1.8 %collective-permute-start.13 = (bf16[128,1024]{1,0:T(8,128)(2,1)S(1)}, bf16[128,1024]{1,0:T(8,128)(2,1)S(1)}, u32[]{:S(2)}, u32[]{:S(2)}) collective-permute-start(bf16[128,1024]{1,0:T(8,128)(2,1)S(1)} %get-tuple-element.44), channel_id=1, source_target_pairs={{0,2},{1,3},{6,4},{7,5},{8,10},{9,11},{14,12},{15,13},{16,18},{17,... | collective-permute-start | bytes 786440 | tf_op jit(solution)/shard_map/ppermute | solution.py:261
  94.3 0.7 collective-permute-start.11
  95.0 1.6 %collective-permute-start.26 = (bf16[128,2560]{1,0:T(8,128)(2,1)S(1)}, bf16[128,2560]{1,0:T(8,128)(2,1)S(1)}, u32[]{:S(2)}, u32[]{:S(2)}) collective-permute-start(bf16[128,2560]{1,0:T(8,128)(2,1)S(1)} %get-tuple-element.28.refs_1_.refs_7_), channel_id=1, source_target_pairs={{0,16},{8,24},{16,0},{24,8},{1,17},{9,25},{17,1},{25,9},{2,18},{10... | collective-permute-start | bytes 1966088 | tf_op jit(solution)/shard_map/ppermute | solution.py:265
  96.7 0.1 collective-permute-start.22
  96.7 0.6 collective-permute-start.23
  97.3 0.8 collective-permute-done.13
  98.1 2.2 %collective-permute-start.28 = (bf16[128,2560]{1,0:T(8,128)(2,1)S(1)}, bf16[128,2560]{1,0:T(8,128)(2,1)S(1)}, u32[]{:S(2)}, u32[]{:S(2)}) collective-permute-start(bf16[128,2560]{1,0:T(8,128)(2,1)S(1)} %collective-permute-done.25.refs_8_), channel_id=1, source_target_pairs={{0,16},{8,24},{16,0},{24,8},{1,17},{9,25},{17,1},{25,9},{2,18},{10... | collective-permute-start | bytes 1966088 | tf_op jit(solution)/shard_map/ppermute | solution.py:265
  100.4 0.2 fusion.4
  100.6 2.8 %collective-permute-start.12 = (bf16[128,1024]{1,0:T(8,128)(2,1)S(1)}, bf16[128,1024]{1,0:T(8,128)(2,1)S(1)}, u32[]{:S(2)}, u32[]{:S(2)}) collective-permute-start(bf16[128,1024]{1,0:T(8,128)(2,1)S(1)} %get-tuple-element.41), channel_id=1, source_target_pairs={{0,2},{1,3},{2,0},{3,1},{4,6},{5,7},{6,4},{7,5},{8,10},{9,11},{10,... | collective-permute-start | bytes 786440 | tf_op jit(solution)/shard_map/ppermute | solution.py:261
  103.4 9.2 %collective-permute-done.26.refs_9_ = bf16[128,2560]{1,0:T(8,128)(2,1)S(1)} collective-permute-done((bf16[128,2560]{1,0:T(8,128)(2,1)S(1)}, bf16[128,2560]{1,0:T(8,128)(2,1)S(1)}, u32[]{:S(2)}, u32[]{:S(2)}) %collective-permute-start.26) | collective-permute-done | bytes 655392 | tf_op jit(solution)/shard_map/ppermute | solution.py:265
  112.7 0.7 collective-permute-start.14
  113.3 1.3 shard_map.94
  114.6 3.9 %shard_map.102 = (f32[384,32,128]{2,1,0:T(8,128)S(1)}, bf16[64,32,512]{2,1,0:T(8,128)(2,1)S(1)}) custom-call(s32[504]{0:T(512)S(1)} %broadcast_add_fusion.1.tab, s32[40]{0:T(128)S(1)} %and_select_fusion.1.groups, s32[1]{0:T(128)} %bitcast.1.me, s32[1]{0:T(128)} %copy.10.count, bf16[16,32,512]{2,1,0:T(8,128)(2,1)S(1)} %shard_map.99.refs_0_, ...), custom_call_target="tpu_custom_call" | custom-call | tf_op jit(solution)/shard_map/pallas_call | solution.py:429
  118.5 5.6 %collective-permute-done.28.refs_3_ = bf16[128,2560]{1,0:T(8,128)(2,1)S(1)} collective-permute-done((bf16[128,2560]{1,0:T(8,128)(2,1)S(1)}, bf16[128,2560]{1,0:T(8,128)(2,1)S(1)}, u32[]{:S(2)}, u32[]{:S(2)}) %collective-permute-start.28) | collective-permute-done | bytes 655392 | tf_op jit(solution)/shard_map/ppermute | solution.py:265
  124.1 3.8 %collective-permute-done.27.refs_2_ = bf16[128,2560]{1,0:T(8,128)(2,1)S(1)} collective-permute-done((bf16[128,2560]{1,0:T(8,128)(2,1)S(1)}, bf16[128,2560]{1,0:T(8,128)(2,1)S(1)}, u32[]{:S(2)}, u32[]{:S(2)}) %collective-permute-start.27) | collective-permute-done | bytes 655392 | tf_op jit(solution)/shard_map/ppermute | solution.py:265
  127.9 4.3 %shard_map.103 = bf16[384,32,128]{2,1,0:T(8,128)(2,1)} custom-call(s32[504]{0:T(512)S(1)} %broadcast_add_fusion.1.tab, s32[40]{0:T(128)S(1)} %and_select_fusion.1.groups, s32[1]{0:T(128)} %bitcast.1.me, s32[1]{0:T(128)} %copy.10.count, bf16[64,32,512]{2,1,0:T(8,128)(2,1)S(1)} %get-tuple-element.39.refs_0_, f32[384,32,128]{2,1,0:T(8,128)S(1)} %get-tuple-element.40.refs_1_, ...), custom_call_target="tpu_custom_call" | custom-call | tf_op jit(solution)/shard_map/pallas_call | solution.py:438
  132.3 0.8 fusion.6
  (41 shorter events, 0.5 us)
Async XLA Ops:
  0.6 29.3 %copy-start.2 = (bf16[128,5120]{1,0:T(8,128)(2,1)S(1)}, bf16[128,5120]{1,0:T(8,128)(2,1)}, u32[]{:S(2)}) copy-start(bf16[128,5120]{1,0:T(8,128)(2,1)} %refs_2_.2) | copy-start | bytes 3932164
  0.6 9.6 %collective-permute-start = (bf16[128,1024]{1,0:T(8,128)(2,1)}, bf16[128,1024]{1,0:T(8,128)(2,1)S(1)}, u32[]{:S(2)}, u32[]{:S(2)}) collective-permute-start(bf16[128,1024]{1,0:T(8,128)(2,1)} %refs_0_.1), channel_id=1, source_target_pairs={{0,2},{1,3},{2,0},{3,1},{4,6},{5,7},{6,4},{7,5},{8,10},{9,11},{10,... | collective-permute-start | bytes 786440 | tf_op jit(solution)/shard_map/ppermute | solution.py:261
  3.8 7.4 %collective-permute-start.1 = (bf16[128,1024]{1,0:T(8,128)(2,1)}, bf16[128,1024]{1,0:T(8,128)(2,1)S(1)}, u32[]{:S(2)}, u32[]{:S(2)}) collective-permute-start(bf16[128,1024]{1,0:T(8,128)(2,1)} %refs_0_.1), channel_id=1, source_target_pairs={{2,4},{3,5},{4,2},{5,3},{10,12},{11,13},{12,10},{13,11},{18,20},{1... | collective-permute-start | bytes 786440 | tf_op jit(solution)/shard_map/ppermute | solution.py:261
  4.4 24.2 %collective-permute-start.5 = (bf16[128,1024]{1,0:T(8,128)(2,1)}, bf16[128,1024]{1,0:T(8,128)(2,1)S(1)}, u32[]{:S(2)}, u32[]{:S(2)}) collective-permute-start(bf16[128,1024]{1,0:T(8,128)(2,1)} %refs_0_.1), channel_id=1, source_target_pairs={{0,1},{1,0},{2,3},{3,2},{4,5},{5,4},{6,7},{7,6},{8,9},{9,8},{10,11... | collective-permute-start | bytes 786440 | tf_op jit(solution)/shard_map/ppermute | solution.py:261
  10.3 2.3 %collective-permute-start.3 = (bf16[128,1024]{1,0:T(8,128)(2,1)S(1)}, bf16[128,1024]{1,0:T(8,128)(2,1)S(1)}, u32[]{:S(2)}, u32[]{:S(2)}) collective-permute-start(bf16[128,1024]{1,0:T(8,128)(2,1)S(1)} %collective-permute-done.refs_1_), channel_id=1, source_target_pairs={{2,4},{3,5},{4,2},{5,3},{10,12},{11,13},{12,10},{13,11},{18,20},{1... | collective-permute-start | bytes 786440 | tf_op jit(solution)/shard_map/ppermute | solution.py:261
  11.2 11.1 %collective-permute-start.2 = (bf16[128,1024]{1,0:T(8,128)(2,1)S(1)}, bf16[128,1024]{1,0:T(8,128)(2,1)}, u32[]{:S(2)}, u32[]{:S(2)}) collective-permute-start(bf16[128,1024]{1,0:T(8,128)(2,1)S(1)} %collective-permute-done.1), channel_id=1, source_target_pairs={{2,0},{3,1},{4,6},{5,7},{10,8},{11,9},{12,14},{13,15},{18,16},{19,... | collective-permute-start | bytes 786440 | tf_op jit(solution)/shard_map/ppermute | solution.py:261
  12.6 15.7 %collective-permute-start.4 = (bf16[128,1024]{1,0:T(8,128)(2,1)S(1)}, bf16[128,1024]{1,0:T(8,128)(2,1)S(1)}, u32[]{:S(2)}, u32[]{:S(2)}) collective-permute-start(bf16[128,1024]{1,0:T(8,128)(2,1)S(1)} %collective-permute-done.3), channel_id=1, source_target_pairs={{2,0},{3,1},{4,6},{5,7},{10,8},{11,9},{12,14},{13,15},{18,16},{19,... | collective-permute-start | bytes 786440 | tf_op jit(solution)/shard_map/ppermute | solution.py:261
  14.6 14.0 %collective-permute-start.6 = (bf16[128,1024]{1,0:T(8,128)(2,1)S(1)}, bf16[128,1024]{1,0:T(8,128)(2,1)S(1)}, u32[]{:S(2)}, u32[]{:S(2)}) collective-permute-start(bf16[128,1024]{1,0:T(8,128)(2,1)S(1)} %collective-permute-done.refs_1_), channel_id=1, source_target_pairs={{0,1},{1,0},{2,3},{3,2},{4,5},{5,4},{6,7},{7,6},{8,9},{9,8},{10,11... | collective-permute-start | bytes 786440 | tf_op jit(solution)/shard_map/ppermute | solution.py:261
  23.3 5.3 %collective-permute-start.7 = (bf16[128,1024]{1,0:T(8,128)(2,1)S(1)}, bf16[128,1024]{1,0:T(8,128)(2,1)S(1)}, u32[]{:S(2)}, u32[]{:S(2)}) collective-permute-start(bf16[128,1024]{1,0:T(8,128)(2,1)S(1)} %broadcast_select_fusion.1.refs_0_), channel_id=1, source_target_pairs={{0,1},{1,0},{2,3},{3,2},{4,5},{5,4},{6,7},{7,6},{8,9},{9,8},{10,11... | collective-permute-start | bytes 786440 | tf_op jit(solution)/shard_map/ppermute | solution.py:261
  28.4 1.6 %collective-permute-start.8 = (bf16[128,1024]{1,0:T(8,128)(2,1)S(1)}, bf16[128,1024]{1,0:T(8,128)(2,1)S(1)}, u32[]{:S(2)}, u32[]{:S(2)}) collective-permute-start(bf16[128,1024]{1,0:T(8,128)(2,1)S(1)} %broadcast_select_fusion.refs_1_), channel_id=1, source_target_pairs={{0,1},{1,0},{2,3},{3,2},{4,5},{5,4},{6,7},{7,6},{8,9},{9,8},{10,11... | collective-permute-start | bytes 786440 | tf_op jit(solution)/shard_map/ppermute | solution.py:261
  30.0 4.6 %copy-start = (bf16[384,128,128]{2,1,0:T(8,128)(2,1)S(1)}, bf16[384,128,128]{2,1,0:T(8,128)(2,1)}, u32[]{:S(2)}) copy-start(bf16[384,128,128]{2,1,0:T(8,128)(2,1)} %refs_2_.3) | copy-start | bytes 37748740
  34.5 0.9 copy-start.3
  35.5 3.5 %copy-start.5 = (s32[384]{0:T(512)S(1)}, s32[384]{0:T(512)}, u32[]{:S(2)}) copy-start(s32[384]{0:T(512)} %param.9) | copy-start | bytes 4612
  35.5 4.6 %copy-start.1 = (bf16[384,128,128]{2,1,0:T(8,128)(2,1)S(1)}, bf16[384,128,128]{2,1,0:T(8,128)(2,1)}, u32[]{:S(2)}) copy-start(bf16[384,128,128]{2,1,0:T(8,128)(2,1)} %refs_2_.3) | copy-start | bytes 37748740
  43.7 11.1 %copy-start.4 = (bf16[128,1024]{1,0:T(8,128)(2,1)S(1)}, bf16[128,1024]{1,0:T(8,128)(2,1)}, u32[]{:S(2)}) copy-start(bf16[128,1024]{1,0:T(8,128)(2,1)} %refs_0_.1) | copy-start | bytes 786436
  49.8 16.2 %collective-permute-start.9 = (bf16[4,128,1024]{2,1,0:T(8,128)(2,1)}, bf16[4,128,1024]{2,1,0:T(8,128)(2,1)}, u32[]{:S(2)}, u32[]{:S(2)}) collective-permute-start(bf16[4,128,1024]{2,1,0:T(8,128)(2,1)} %get-tuple-element.30), channel_id=1, source_target_pairs={{0,1},{1,0},{2,3},{3,2},{4,5},{5,4},{6,7},{7,6},{8,9},{9,8},{10,11... | collective-permute-start | bytes 3145736 | tf_op jit(solution)/shard_map/ppermute | solution.py:261
  55.1 5.9 %collective-permute-start.15 = (bf16[16,32,128]{2,1,0:T(8,128)(2,1)S(1)}, bf16[16,32,128]{2,1,0:T(8,128)(2,1)S(1)}, u32[]{:S(2)}, u32[]{:S(2)}) collective-permute-start(bf16[16,32,128]{2,1,0:T(8,128)(2,1)S(1)} %get-tuple-element.32), channel_id=1, source_target_pairs={{0,8},{8,0},{16,24},{24,16},{1,9},{9,1},{17,25},{25,17},{2,10},{10... | collective-permute-start | bytes 393224 | tf_op jit(solution)/shard_map/ppermute | solution.py:265
  56.6 7.9 %collective-permute-start.16 = (bf16[16,32,128]{2,1,0:T(8,128)(2,1)S(1)}, bf16[16,32,128]{2,1,0:T(8,128)(2,1)S(1)}, u32[]{:S(2)}, u32[]{:S(2)}) collective-permute-start(bf16[16,32,128]{2,1,0:T(8,128)(2,1)S(1)} %get-tuple-element.33), channel_id=1, source_target_pairs={{0,16},{8,24},{16,0},{24,8},{1,17},{9,25},{17,1},{25,9},{2,18},{10... | collective-permute-start | bytes 393224 | tf_op jit(solution)/shard_map/ppermute | solution.py:265
  58.1 6.4 %collective-permute-start.17 = (bf16[16,32,128]{2,1,0:T(8,128)(2,1)S(1)}, bf16[16,32,128]{2,1,0:T(8,128)(2,1)S(1)}, u32[]{:S(2)}, u32[]{:S(2)}) collective-permute-start(bf16[16,32,128]{2,1,0:T(8,128)(2,1)S(1)} %get-tuple-element.34), channel_id=1, source_target_pairs={{0,24},{8,16},{16,8},{24,0},{1,25},{9,17},{17,9},{25,1},{2,26},{10... | collective-permute-start | bytes 393224 | tf_op jit(solution)/shard_map/ppermute | solution.py:265
  64.6 30.3 %collective-permute-start.21 = (bf16[16,32,512]{2,1,0:T(8,128)(2,1)S(1)}, bf16[16,32,512]{2,1,0:T(8,128)(2,1)S(1)}, u32[]{:S(2)}, u32[]{:S(2)}) collective-permute-start(bf16[16,32,512]{2,1,0:T(8,128)(2,1)S(1)} %shard_map.99.refs_0_), channel_id=1, source_target_pairs={{0,1},{1,0},{2,3},{3,2},{4,5},{5,4},{6,7},{7,6},{8,9},{9,8},{10,11... | collective-permute-start | bytes 1572872 | tf_op jit(solution)/shard_map/ppermute | solution.py:261
  64.7 31.9 %collective-permute-start.25 = (bf16[128,2560]{1,0:T(8,128)(2,1)S(1)}, bf16[128,2560]{1,0:T(8,128)(2,1)S(1)}, u32[]{:S(2)}, u32[]{:S(2)}) collective-permute-start(bf16[128,2560]{1,0:T(8,128)(2,1)S(1)} %get-tuple-element.28.refs_1_.refs_7_), channel_id=1, source_target_pairs={{0,8},{8,0},{16,24},{24,16},{1,9},{9,1},{17,25},{25,17},{2,10},{10... | collective-permute-start | bytes 1966088 | tf_op jit(solution)/shard_map/ppermute | solution.py:265
  67.7 18.5 %collective-permute-start.10 = (bf16[128,1024]{1,0:T(8,128)(2,1)S(1)}, bf16[128,1024]{1,0:T(8,128)(2,1)S(1)}, u32[]{:S(2)}, u32[]{:S(2)}) collective-permute-start(bf16[128,1024]{1,0:T(8,128)(2,1)S(1)} %get-tuple-element.43), channel_id=1, source_target_pairs={{0,2},{1,3},{6,4},{7,5},{8,10},{9,11},{14,12},{15,13},{16,18},{17,... | collective-permute-start | bytes 786440 | tf_op jit(solution)/shard_map/ppermute | solution.py:261
  69.5 27.2 %collective-permute-start.24 = (bf16[128,2560]{1,0:T(8,128)(2,1)S(1)}, bf16[128,2560]{1,0:T(8,128)(2,1)S(1)}, u32[]{:S(2)}, u32[]{:S(2)}) collective-permute-start(bf16[128,2560]{1,0:T(8,128)(2,1)S(1)} %get-tuple-element.27.refs_0_.refs_4_), channel_id=1, source_target_pairs={{0,16},{8,24},{16,0},{24,8},{1,17},{9,25},{17,1},{25,9},{2,18},{10... | collective-permute-start | bytes 1966088 | tf_op jit(solution)/shard_map/ppermute | solution.py:265
  70.6 14.0 %collective-permute-start.18 = (bf16[16,32,128]{2,1,0:T(8,128)(2,1)S(1)}, bf16[16,32,128]{2,1,0:T(8,128)(2,1)S(1)}, u32[]{:S(2)}, u32[]{:S(2)}) collective-permute-start(bf16[16,32,128]{2,1,0:T(8,128)(2,1)S(1)} %get-tuple-element.36), channel_id=1, source_target_pairs={{0,8},{8,0},{16,24},{24,16},{1,9},{9,1},{17,25},{25,17},{2,10},{10... | collective-permute-start | bytes 393224 | tf_op jit(solution)/shard_map/ppermute | solution.py:265
  84.7 7.8 %collective-permute-start.19 = (bf16[16,32,128]{2,1,0:T(8,128)(2,1)S(1)}, bf16[16,32,128]{2,1,0:T(8,128)(2,1)S(1)}, u32[]{:S(2)}, u32[]{:S(2)}) collective-permute-start(bf16[16,32,128]{2,1,0:T(8,128)(2,1)S(1)} %get-tuple-element.37), channel_id=1, source_target_pairs={{0,16},{8,24},{16,0},{24,8},{1,17},{9,25},{17,1},{25,9},{2,18},{10... | collective-permute-start | bytes 393224 | tf_op jit(solution)/shard_map/ppermute | solution.py:265
  86.2 8.1 %collective-permute-start.20 = (bf16[16,32,128]{2,1,0:T(8,128)(2,1)S(1)}, bf16[16,32,128]{2,1,0:T(8,128)(2,1)S(1)}, u32[]{:S(2)}, u32[]{:S(2)}) collective-permute-start(bf16[16,32,128]{2,1,0:T(8,128)(2,1)S(1)} %get-tuple-element.38), channel_id=1, source_target_pairs={{0,24},{8,16},{16,8},{24,0},{1,25},{9,17},{17,9},{25,1},{2,26},{10... | collective-permute-start | bytes 393224 | tf_op jit(solution)/shard_map/ppermute | solution.py:265
  92.4 5.7 %collective-permute-start.13 = (bf16[128,1024]{1,0:T(8,128)(2,1)S(1)}, bf16[128,1024]{1,0:T(8,128)(2,1)S(1)}, u32[]{:S(2)}, u32[]{:S(2)}) collective-permute-start(bf16[128,1024]{1,0:T(8,128)(2,1)S(1)} %get-tuple-element.44), channel_id=1, source_target_pairs={{0,2},{1,3},{6,4},{7,5},{8,10},{9,11},{14,12},{15,13},{16,18},{17,... | collective-permute-start | bytes 786440 | tf_op jit(solution)/shard_map/ppermute | solution.py:261
  94.3 6.1 %collective-permute-start.11 = (bf16[128,1024]{1,0:T(8,128)(2,1)S(1)}, bf16[128,1024]{1,0:T(8,128)(2,1)S(1)}, u32[]{:S(2)}, u32[]{:S(2)}) collective-permute-start(bf16[128,1024]{1,0:T(8,128)(2,1)S(1)} %add_convert_fusion.2), channel_id=1, source_target_pairs={{2,4},{3,5},{4,2},{5,3},{10,12},{11,13},{12,10},{13,11},{18,20},{1... | collective-permute-start | bytes 786440 | tf_op jit(solution)/shard_map/ppermute | solution.py:261
  95.0 17.7 %collective-permute-start.26 = (bf16[128,2560]{1,0:T(8,128)(2,1)S(1)}, bf16[128,2560]{1,0:T(8,128)(2,1)S(1)}, u32[]{:S(2)}, u32[]{:S(2)}) collective-permute-start(bf16[128,2560]{1,0:T(8,128)(2,1)S(1)} %get-tuple-element.28.refs_1_.refs_7_), channel_id=1, source_target_pairs={{0,16},{8,24},{16,0},{24,8},{1,17},{9,25},{17,1},{25,9},{2,18},{10... | collective-permute-start | bytes 1966088 | tf_op jit(solution)/shard_map/ppermute | solution.py:265
  96.7 3.9 %collective-permute-start.22 = (bf16[16,32,512]{2,1,0:T(8,128)(2,1)S(1)}, bf16[16,32,512]{2,1,0:T(8,128)(2,1)S(1)}, u32[]{:S(2)}, u32[]{:S(2)}) collective-permute-start(bf16[16,32,512]{2,1,0:T(8,128)(2,1)S(1)} %shard_map.101.refs_1_), channel_id=1, source_target_pairs={{0,1},{1,0},{2,3},{3,2},{4,5},{5,4},{6,7},{7,6},{8,9},{9,8},{10,11... | collective-permute-start | bytes 1572872 | tf_op jit(solution)/shard_map/ppermute | solution.py:261
  96.7 17.9 %collective-permute-start.23 = (bf16[128,2560]{1,0:T(8,128)(2,1)S(1)}, bf16[128,2560]{1,0:T(8,128)(2,1)S(1)}, u32[]{:S(2)}, u32[]{:S(2)}) collective-permute-start(bf16[128,2560]{1,0:T(8,128)(2,1)S(1)} %get-tuple-element.27.refs_0_.refs_4_), channel_id=1, source_target_pairs={{0,8},{8,0},{16,24},{24,16},{1,9},{9,1},{17,25},{25,17},{2,10},{10... | collective-permute-start | bytes 1966088 | tf_op jit(solution)/shard_map/ppermute | solution.py:265
  98.1 26.0 %collective-permute-start.28 = (bf16[128,2560]{1,0:T(8,128)(2,1)S(1)}, bf16[128,2560]{1,0:T(8,128)(2,1)S(1)}, u32[]{:S(2)}, u32[]{:S(2)}) collective-permute-start(bf16[128,2560]{1,0:T(8,128)(2,1)S(1)} %collective-permute-done.25.refs_8_), channel_id=1, source_target_pairs={{0,16},{8,24},{16,0},{24,8},{1,17},{9,25},{17,1},{25,9},{2,18},{10... | collective-permute-start | bytes 1966088 | tf_op jit(solution)/shard_map/ppermute | solution.py:265
  100.4 27.5 %collective-permute-start.27 = (bf16[128,2560]{1,0:T(8,128)(2,1)S(1)}, bf16[128,2560]{1,0:T(8,128)(2,1)S(1)}, u32[]{:S(2)}, u32[]{:S(2)}) collective-permute-start(bf16[128,2560]{1,0:T(8,128)(2,1)S(1)} %collective-permute-done.24.refs_6_), channel_id=1, source_target_pairs={{0,8},{8,0},{16,24},{24,16},{1,9},{9,1},{17,25},{25,17},{2,10},{10... | collective-permute-start | bytes 1966088 | tf_op jit(solution)/shard_map/ppermute | solution.py:265
  100.6 31.7 %collective-permute-start.12 = (bf16[128,1024]{1,0:T(8,128)(2,1)S(1)}, bf16[128,1024]{1,0:T(8,128)(2,1)S(1)}, u32[]{:S(2)}, u32[]{:S(2)}) collective-permute-start(bf16[128,1024]{1,0:T(8,128)(2,1)S(1)} %get-tuple-element.41), channel_id=1, source_target_pairs={{0,2},{1,3},{2,0},{3,1},{4,6},{5,7},{6,4},{7,5},{8,10},{9,11},{10,... | collective-permute-start | bytes 786440 | tf_op jit(solution)/shard_map/ppermute | solution.py:261
  112.7 19.6 %collective-permute-start.14 = (bf16[128,1024]{1,0:T(8,128)(2,1)S(1)}, bf16[128,1024]{1,0:T(8,128)(2,1)S(1)}, u32[]{:S(2)}, u32[]{:S(2)}) collective-permute-start(bf16[128,1024]{1,0:T(8,128)(2,1)S(1)} %get-tuple-element.42), channel_id=1, source_target_pairs={{2,4},{3,5},{4,2},{5,3},{10,12},{11,13},{12,10},{13,11},{18,20},{1... | collective-permute-start | bytes 786440 | tf_op jit(solution)/shard_map/ppermute | solution.py:261
